TPU v7x, 32 devices: a whole 2x2x4 slice. The times are simulated.
32 devices in a mesh: seq: 8 (over z, y), head: 4 (over x, core).
Axes of the slice: x: 2, y: 2, z: 4, core: 2. Of those that a mesh axis runs over, the one named last changes fastest.
Arguments:
- inputs: bfloat16 [2, 4096, 1024], P(None, ('seq', 'head')), may hold values from -6 to 6
- attn_gain: float32 [1024], replicated, may hold values from 0.5 to 1.5
- mixer_weights: bfloat16 [4, 1024, 1024], P(None, None, 'head'), may hold values from -0.1875 to 0.1875
- beta_weight: bfloat16 [1024, 8], P(None, 'head'), may hold values from -0.1875 to 0.1875
- filter_weights: bfloat16 [3, 4, 1024], P(None, None, 'head'), may hold values from -3 to 3
- out_gain: float32 [128], replicated, may hold values from 0.5 to 1.5
- dense_gain: float32 [1024], replicated, may hold values from 0.5 to 1.5
- dense_weights: bfloat16 [3, 1024, 2816], P(None, 'seq', 'head'), may hold values from -0.1875 to 0.1875
- seq_offsets: int32 [2, 3], replicated, may hold values from 0 to 3072, as said below
- seq_lengths: int32 [2, 3], replicated, may hold values from 961 to 2048, as said below
- out_grad: bfloat16 [2, 4096, 1024], P(None, ('seq', 'head')), may hold values from -6 to 6
Outputs:
- output: bfloat16 [2, 4096, 1024], P(None, ('seq', 'head'))
- input_grad: float32 [2, 4096, 1024], P(None, ('seq', 'head'))
- attn_gain_grad: float32 [1024], replicated
- mixer_weights_grad: float32 [4, 1024, 1024], P(None, None, 'head')
- beta_weight_grad: float32 [1024, 8], P(None, 'head')
- filter_weights_grad: float32 [3, 4, 1024], P(None, None, 'head')
- out_gain_grad: float32 [128], replicated
- dense_gain_grad: float32 [1024], replicated
- dense_weights_grad: float32 [3, 1024, 2816], P(None, 'seq', 'head')
Inputs may be any that keep to these rules, and one draw needn't show every extreme that they name: seq_offsets[m] starts at 0, rises by 1024 or more from one slot to the next, holds multiples of 64, and the last slot ends at token 4096. `seq_lengths`: each sequence fills its slot from the slot's first token and leaves fewer than 64 padding tokens at the slot's end.
All inputs are finite; a program needn't handle non-finite values.
Results may differ from a plain program's by a relative error of at most 0.02.
Values may be sent and summed in bfloat16 or wider, within the bound.
A program may use at most 192 MiB of HBM per device.

v0:
```python
import jax
import jax.numpy as jnp
from jax import lax
from jax.sharding import PartitionSpec as P

HEAD_DIM = 128
CONV = 4
STRETCH = 64


norm_eps = 1e-06
highest_precision = lax.Precision.HIGHEST


def passed_along(block, axis, distance):
    devices = range(lax.axis_size(axis))
    route = [(i - distance, i) for i in devices if i - distance in devices]
    return lax.ppermute(block, axis, route)


def prefix(x, axis, join, neutral):
    place = lax.axis_index(axis)
    gathered = jax.tree.map(
        lambda a, kind: lax.all_gather(a.astype(kind), axis), x, (jnp.bfloat16, jnp.bfloat16)
    )
    state = jax.tree.map(lambda a, e: jnp.zeros_like(a) + jnp.asarray(e, a.dtype), x, neutral)

    def one(lap, state):
        return join(
            state,
            jax.tree.map(
                lambda a, own: lax.dynamic_index_in_dim(a, lap, 0, False).astype(own.dtype),
                gathered,
                x,
            ),
        )

    return lax.fori_loop(0, place, one, state)


def prefix_2(x, axis, join, neutral):
    count = lax.axis_size(axis)
    place = lax.axis_index(axis)
    ahead = count - 1 - place
    gathered = jax.tree.map(
        lambda a, kind: lax.all_gather(a.astype(kind), axis),
        x,
        jax.tree.map(lambda a: jnp.bfloat16 if a.dtype == jnp.float32 else a.dtype, x),
    )
    state = jax.tree.map(lambda a, e: jnp.zeros_like(a) + jnp.asarray(e, a.dtype), x, neutral)

    def one(lap, state):
        source = count - 1 - lap
        return join(
            state,
            jax.tree.map(
                lambda a, own: lax.dynamic_index_in_dim(a, source, 0, False).astype(own.dtype),
                gathered,
                x,
            ),
        )

    return lax.fori_loop(0, ahead, one, state)


def rms_scale(values, gain_vec):
    return (
        values * lax.rsqrt(jnp.mean(values * values, axis=-1, keepdims=True) + norm_eps) * gain_vec
    )


def rms_back(grad_out, values, gain_vec):
    inv_rms = lax.rsqrt(jnp.mean(values * values, axis=-1, keepdims=True) + norm_eps)
    weighted = grad_out * gain_vec
    grad_in = inv_rms * weighted - values * inv_rms**3 * jnp.mean(
        weighted * values, axis=-1, keepdims=True
    )
    grad_gain = jnp.sum(grad_out * values * inv_rms, axis=0)
    return (grad_in, grad_gain)


def unit_rows(values):
    return values * lax.rsqrt(jnp.sum(values * values, axis=-1, keepdims=True) + norm_eps)


def solve_one(system_one, right_one):
    return jax.scipy.linalg.solve_triangular(system_one, right_one, lower=True, unit_diagonal=True)


def stretch_solve(key_row_matrix, values, rate_rows):
    inner_prod = jnp.einsum(
        "...ck,...dk->...cd", key_row_matrix, key_row_matrix, precision=highest_precision
    )
    lower_part = jnp.tril(rate_rows[..., :, None] * inner_prod, -1)
    system = lower_part + jnp.eye(key_row_matrix.shape[-2], dtype=key_row_matrix.dtype)
    right_side = rate_rows[..., :, None] * jnp.concatenate([key_row_matrix, values], axis=-1)
    flat_system = system.reshape((-1,) + system.shape[-2:])
    flat_right = right_side.reshape((-1,) + right_side.shape[-2:])
    solved = jax.vmap(solve_one)(flat_system, flat_right).reshape(right_side.shape)
    key_width = key_row_matrix.shape[-1]
    return (solved[..., :key_width], solved[..., key_width:])


def mixer_inputs(extended, rates_raw, filter_taps, offset_rel, valid_rows):
    row_count = rates_raw.shape[0]
    local_heads = rates_raw.shape[1]
    summed = jnp.zeros((3, row_count, filter_taps.shape[2]), jnp.float32)
    for lag_step in range(CONV):
        first_row = CONV - 1 - lag_step
        lag_mask = (offset_rel >= lag_step).astype(jnp.float32)[None, :, None]
        summed = (
            summed
            + filter_taps[:, lag_step, None, :]
            * extended[:, first_row : first_row + row_count, :]
            * lag_mask
        )
    active = jax.nn.silu(summed).reshape(3, row_count, local_heads, HEAD_DIM)
    query_rows = unit_rows(active[0])
    key_row_matrix = unit_rows(active[1])
    values = active[2]
    rate_rows = jax.nn.sigmoid(rates_raw) * valid_rows[:, None]
    return (query_rows, key_row_matrix, values, rate_rows)


def heads_first(array_in):
    return array_in.reshape(-1, STRETCH, array_in.shape[1], array_in.shape[2]).transpose(0, 2, 1, 3)


def stretch_prep(query_rows, key_row_matrix, values, rate_rows):
    query_block_list = heads_first(query_rows)
    key_block_list = heads_first(key_row_matrix)
    value_blocks = heads_first(values)
    rate_blocks = rate_rows.reshape(-1, STRETCH, rate_rows.shape[1]).transpose(0, 2, 1)
    write_rows, update_rows = stretch_solve(key_block_list, value_blocks, rate_blocks)
    score_matrix = jnp.tril(
        jnp.einsum("nhck,nhdk->nhcd", query_block_list, key_block_list, precision=highest_precision)
    )
    return (query_block_list, key_block_list, write_rows, update_rows, score_matrix)


def stretch_carry(carry_pair, inputs):
    trans_mat, state_matrix = carry_pair
    key_block_list, write_rows, update_rows, keep_flag = inputs
    trans_mat = trans_mat * keep_flag
    state_matrix = state_matrix * keep_flag
    trans_mat = trans_mat - jnp.einsum(
        "hck,hcj->hkj",
        key_block_list,
        jnp.einsum("hck,hkj->hcj", write_rows, trans_mat, precision=highest_precision),
        precision=highest_precision,
    )
    fresh_value_rows = update_rows - jnp.einsum(
        "bdw,bws->bds", write_rows, state_matrix, precision=highest_precision
    )
    state_matrix = state_matrix + jnp.einsum(
        "bua,buq->baq", key_block_list, fresh_value_rows, precision=highest_precision
    )
    return ((trans_mat, state_matrix), None)


def stretch_run(state_matrix, inputs):
    query_block_list, key_block_list, write_rows, update_rows, score_matrix, keep_flag = inputs
    state_matrix = state_matrix * keep_flag
    fresh_value_rows = update_rows - jnp.einsum(
        "bdw,bws->bds", write_rows, state_matrix, precision=highest_precision
    )
    output_rows = jnp.einsum(
        "bdw,bws->bds", query_block_list, state_matrix, precision=highest_precision
    ) + jnp.einsum("tbg,tgx->tbx", score_matrix, fresh_value_rows, precision=highest_precision)
    state_matrix = state_matrix + jnp.einsum(
        "bua,buq->baq", key_block_list, fresh_value_rows, precision=highest_precision
    )
    return (state_matrix, output_rows)


def chain_combine(earlier, later_pair):
    trans_early, state_early = earlier
    trans_late, state_late = later_pair
    joined_trans = jnp.einsum("hij,hjk->hik", trans_late, trans_early, precision=highest_precision)
    joined_state = (
        jnp.einsum("hij,hjk->hik", trans_late, state_early, precision=highest_precision)
        + state_late
    )
    return (joined_trans, joined_state)


def head_norm_of(mixed, gain_vec):
    row_count = mixed.shape[0] * mixed.shape[2]
    token_major = mixed.transpose(0, 2, 1, 3).reshape(row_count, mixed.shape[1], mixed.shape[3])
    return rms_scale(token_major, gain_vec).reshape(row_count, -1)


def mixer_local(
    extended, rates_raw, filter_taps, gain_vec, state_start, offset_rel, valid_rows, keep_flags
):
    query_rows, key_row_matrix, values, rate_rows = mixer_inputs(
        extended, rates_raw, filter_taps, offset_rel, valid_rows
    )
    blocks = stretch_prep(query_rows, key_row_matrix, values, rate_rows)
    state_out, mixed = lax.scan(stretch_run, state_start, blocks + (keep_flags,))
    return (head_norm_of(mixed, gain_vec), state_out)


def per_device(
    inputs,
    attn_gain,
    mixer_weights,
    beta_weight,
    filter_weights,
    out_gain,
    dense_gain,
    dense_weights,
    seq_offsets,
    seq_lengths,
    out_grad,
):
    micro_count = inputs.shape[0]
    local_rows = inputs.shape[1]
    model_width = inputs.shape[2]
    row_count = local_rows * lax.axis_size("head")
    head_width = mixer_weights.shape[2]
    local_heads = beta_weight.shape[1]
    hidden_width = dense_weights.shape[2]
    rim_rows = CONV - 1
    positions = lax.axis_index("seq") * row_count + jnp.arange(row_count, dtype=jnp.int32)
    eye_block = jnp.broadcast_to(
        jnp.eye(HEAD_DIM, dtype=jnp.float32), (local_heads, HEAD_DIM, HEAD_DIM)
    )
    zero_block = jnp.zeros((local_heads, HEAD_DIM, HEAD_DIM), jnp.float32)
    filter_f32 = filter_weights.astype(jnp.float32)
    beta_f32 = beta_weight.astype(jnp.float32)
    out_weight = mixer_weights[3]
    mixer_acc = jnp.zeros((4, model_width, head_width), jnp.float32)
    beta_acc = jnp.zeros((model_width, local_heads), jnp.float32)
    filter_acc = jnp.zeros(filter_weights.shape, jnp.float32)
    out_gain_acc = jnp.zeros((HEAD_DIM,), jnp.float32)
    attn_gain_acc = jnp.zeros((model_width,), jnp.float32)
    dense_gain_acc = jnp.zeros((model_width,), jnp.float32)
    dense_acc = jnp.zeros((3, model_width, hidden_width), jnp.float32)
    results = []
    input_grads = []
    for micro_batch in range(micro_count):
        offsets_now = seq_offsets[micro_batch]
        lengths_now = seq_lengths[micro_batch]
        inside = offsets_now[None, :] <= positions[:, None]
        seq_index = jnp.sum(inside.astype(jnp.int32), axis=1) - 1
        one_hot = (
            jnp.arange(offsets_now.shape[0], dtype=jnp.int32)[None, :] == seq_index[:, None]
        ).astype(jnp.int32)
        starts_now = jnp.sum(one_hot * offsets_now[None, :], axis=1)
        offset_rel = positions - starts_now
        valid_rows = (offset_rel < jnp.sum(one_hot * lengths_now[None, :], axis=1)).astype(
            jnp.float32
        )
        keep_flags = (offset_rel[::STRETCH] != 0).astype(jnp.float32)
        resid_in = inputs[micro_batch].astype(jnp.float32)
        normed_local = rms_scale(resid_in, attn_gain).astype(jnp.bfloat16)
        gathered_norm = lax.all_gather(normed_local, "head", axis=0, tiled=True)
        projected = jnp.einsum(
            "td,ndc->ntc", gathered_norm, mixer_weights[:3], preferred_element_type=jnp.float32
        ).astype(jnp.bfloat16)
        rates_raw = jnp.dot(gathered_norm, beta_weight, preferred_element_type=jnp.float32)
        rim_prev = passed_along(projected[:, row_count - rim_rows :, :], "seq", 1)
        extended = jnp.concatenate([rim_prev, projected], axis=1).astype(jnp.float32)
        query_rows, key_row_matrix, values, rate_rows = mixer_inputs(
            extended, rates_raw, filter_f32, offset_rel, valid_rows
        )
        blocks = stretch_prep(query_rows, key_row_matrix, values, rate_rows)
        carry_end = lax.scan(
            stretch_carry, (eye_block, zero_block), (blocks[1], blocks[2], blocks[3], keep_flags)
        )[0]
        trans_mat, state_end = carry_end
        state_in = prefix((trans_mat, state_end), "seq", chain_combine, (eye_block, zero_block))[1]
        mixed = lax.scan(stretch_run, state_in, blocks + (keep_flags,))[1]
        head_out = head_norm_of(mixed, out_gain).astype(jnp.bfloat16)
        attn_out = lax.psum_scatter(
            lax.dot_general(
                head_out, out_weight, (((1,), (1,)), ((), ())), preferred_element_type=jnp.float32
            ).astype(jnp.bfloat16),
            "head",
            scatter_dimension=0,
            tiled=True,
        ).astype(jnp.float32)
        resid_mid = resid_in + attn_out
        dense_in_local = rms_scale(resid_mid, dense_gain).astype(jnp.bfloat16)
        dense_in, grad_top = (
            lax.all_gather(dense_in_local, "head", axis=0, tiled=True),
            lax.all_gather(out_grad[micro_batch], "head", axis=0, tiled=True),
        )
        dense_full = lax.all_gather(dense_weights, "seq", axis=1, tiled=True)
        gate_up = jnp.einsum(
            "rd,ndf->nrf", dense_in, dense_full[:2], preferred_element_type=jnp.float32
        )
        gate_vals = gate_up[0]
        up_vals = gate_up[1]
        sig_gate = jax.nn.sigmoid(gate_vals)
        silu_gate = gate_vals * sig_gate
        hidden = (silu_gate * up_vals).astype(jnp.bfloat16)
        dense_out = lax.psum_scatter(
            lax.dot_general(
                hidden, dense_full[2], (((1,), (1,)), ((), ())), preferred_element_type=jnp.float32
            ).astype(jnp.bfloat16),
            "head",
            scatter_dimension=0,
            tiled=True,
        ).astype(jnp.float32)
        results.append((resid_mid + dense_out).astype(jnp.bfloat16))
        grad_hidden = jnp.dot(grad_top, dense_full[2], preferred_element_type=jnp.float32)
        deriv_gate = sig_gate * (1.0 + gate_vals * (1.0 - sig_gate))
        grad_pair = jnp.stack([grad_hidden * up_vals * deriv_gate, grad_hidden * silu_gate]).astype(
            jnp.bfloat16
        )
        grad_pair_w = jnp.einsum(
            "rd,nrf->ndf", dense_in, grad_pair, preferred_element_type=jnp.float32
        )
        grad_down = lax.dot_general(
            grad_top, hidden, (((0,), (0,)), ((), ())), preferred_element_type=jnp.float32
        )
        dense_acc = dense_acc + jnp.concatenate([grad_pair_w, grad_down[None]], axis=0)
        grad_dense_part = jnp.einsum(
            "nrf,ndf->rd", grad_pair, dense_full[:2], preferred_element_type=jnp.float32
        )
        grad_dense_in = lax.psum_scatter(
            grad_dense_part.astype(jnp.bfloat16), "head", scatter_dimension=0, tiled=True
        ).astype(jnp.float32)
        grad_mid_norm, dense_gain_part = rms_back(grad_dense_in, resid_mid, dense_gain)
        dense_gain_acc = dense_gain_acc + dense_gain_part
        grad_mid = out_grad[micro_batch].astype(jnp.float32) + grad_mid_norm
        grad_attn = lax.all_gather(grad_mid.astype(jnp.bfloat16), "head", axis=0, tiled=True)
        out_weight_grad = lax.dot_general(
            grad_attn, head_out, (((0,), (0,)), ((), ())), preferred_element_type=jnp.float32
        )
        grad_head = jnp.dot(grad_attn, out_weight, preferred_element_type=jnp.float32)

        def local_piece(ext_in, raw_in, taps_in, gain_in, state_start):
            return mixer_local(
                ext_in, raw_in, taps_in, gain_in, state_start, offset_rel, valid_rows, keep_flags
            )

        pullback = jax.vjp(local_piece, extended, rates_raw, filter_f32, out_gain, state_in)[1]
        state_grad_here = pullback((grad_head, zero_block))[4]
        trans_back = jnp.swapaxes(trans_mat, 1, 2)
        state_out_grad = prefix_2(
            (trans_back, state_grad_here), "seq", chain_combine, (eye_block, zero_block)
        )[1]
        grads_full = pullback((grad_head, state_out_grad))
        grad_ext = grads_full[0]
        grad_rates_raw = grads_full[1]
        filter_acc = filter_acc + grads_full[2]
        out_gain_acc = out_gain_acc + grads_full[3]
        rim_back = passed_along(grad_ext[:, :rim_rows, :], "seq", -1)
        grad_proj = grad_ext[:, rim_rows:, :]
        grad_proj = grad_proj.at[:, row_count - rim_rows :, :].add(rim_back).astype(jnp.bfloat16)
        proj_weight_grad = jnp.einsum(
            "td,ntc->ndc", gathered_norm, grad_proj, preferred_element_type=jnp.float32
        )
        mixer_acc = mixer_acc + jnp.concatenate([proj_weight_grad, out_weight_grad[None]], axis=0)
        beta_acc = beta_acc + jnp.einsum(
            "td,th->dh",
            gathered_norm.astype(jnp.float32),
            grad_rates_raw,
            precision=highest_precision,
        )
        grad_normed = jnp.einsum(
            "ntc,ndc->td", grad_proj, mixer_weights[:3], preferred_element_type=jnp.float32
        )
        grad_normed = grad_normed + jnp.dot(grad_rates_raw, beta_f32.T, precision=highest_precision)
        grad_norm_rows = lax.psum_scatter(
            grad_normed.astype(jnp.bfloat16), "head", scatter_dimension=0, tiled=True
        ).astype(jnp.float32)
        grad_in_norm, attn_gain_part = rms_back(grad_norm_rows, resid_in, attn_gain)
        attn_gain_acc = attn_gain_acc + attn_gain_part
        input_grads.append(grad_mid + grad_in_norm)
    mixer_total, beta_total, filter_total = lax.psum((mixer_acc, beta_acc, filter_acc), "seq")
    attn_gain_total, out_gain_total, dense_gain_total = lax.psum(
        (attn_gain_acc, out_gain_acc, dense_gain_acc), ("seq", "head")
    )
    dense_total = lax.psum_scatter(dense_acc, "seq", scatter_dimension=1, tiled=True)
    return (
        jnp.stack(results),
        jnp.stack(input_grads),
        attn_gain_total,
        mixer_total,
        beta_total,
        filter_total,
        out_gain_total,
        dense_gain_total,
        dense_total,
    )


def solution(mesh):
    placed = (
        P(None, ("seq", "head"), None),
        P(),
        P(None, None, "head"),
        P(None, "head"),
        P(None, None, "head"),
        P(),
        P(),
        P(None, "seq", "head"),
        P(),
        P(),
        P(None, ("seq", "head"), None),
    )
    return jax.shard_map(
        per_device,
        mesh=mesh,
        in_specs=placed,
        out_specs=(
            P(None, ("seq", "head"), None),
            P(None, ("seq", "head"), None),
            P(),
            P(None, None, "head"),
            P(None, "head"),
            P(None, None, "head"),
            P(),
            P(),
            P(None, "seq", "head"),
        ),
        check_vma=False,
    )
```

profile of v0, /device:TPU:0, one launch (start us, length us, event | category | flops | bytes accessed | tf_op | source)
XLA Modules:
  0.0 2086.9 jit_solution(1284363658794357828)
XLA Ops:
  107.6 80.0 %custom-call.14 = f32[16,1,64,64]{2,3,1,0:T(8,128)} custom-call(f32[16,1,64,64]{3,2,1,0:T(8,128)} %bitcast.1203), custom_call_target="InvertDiagBlocksLowerTriangular" | custom-call | tf_op jit(solution)/shard_map/vmap(jit(_solve_triangular))/triangular_solve/custom-call.1 | solution.py:87
  192.3 68.0 %while.224 = (s32[]{:T(128)}, f32[2,128,128]{2,1,0:T(8,128)S(1)}, f32[2,128,128]{2,1,0:T(8,128)S(1)}, f32[8]{0:T(128)}, f32[8,2,64,128]{3,2,1,0:T(8,128)}, /*ind...) while((s32[]{:T(128)}, f32[2,128,128]{2,1,0:T(8,128)S(1)}, ...), condition=%wide.region_6.8_spmd.clone, body=%wide.region_5.0_spmd.clone.sunk | while | flops 100941824 | bytes 1379975 | solution.py:269
  260.4 33.4 %all-gather = bf16[16,128,128]{2,1,0:T(8,128)(2,1)} all-gather(bf16[2,128,128]{2,1,0:T(8,128)(2,1)S(1)} %convert_element_type.347), channel_id=2, replica_groups=mesh['seq'=8,'head'=4] {'seq'}, dimensions={0}, use_global_device_ids=true | all-gather | bytes 589824 | tf_op jit(solution)/shard_map/all_gather | solution.py:24
  293.8 33.8 %all-gather.1 = bf16[16,128,128]{2,1,0:T(8,128)(2,1)} all-gather(bf16[2,128,128]{2,1,0:T(8,128)(2,1)S(1)} %convert_element_type.348), channel_id=3, replica_groups=mesh['seq'=8,'head'=4] {'seq'}, dimensions={0}, use_global_device_ids=true | all-gather | bytes 589824 | tf_op jit(solution)/shard_map/all_gather | solution.py:24
  342.8 66.1 %while.215 = (s32[]{:T(128)}, f32[2,128,128]{2,1,0:T(8,128)S(1)}, f32[8,2,64,128]{3,2,1,0:T(8,128)}, f32[8]{0:T(128)}, f32[8,2,64,128]{3,2,1,0:T(8,128)}, /*inde...) while((s32[]{:T(128)}, f32[2,128,128]{2,1,0:T(8,128)S(1)}, ...), condition=%wide.region_11.13_spmd, body=%wide.region_10.12_spmd.sunk | while | flops 88244224 | bytes 1248897 | solution.py:274
  414.7 80.0 %custom-call.15 = f32[16,1,64,64]{2,3,1,0:T(8,128)} custom-call(f32[16,1,64,64]{3,2,1,0:T(8,128)} %bitcast.1202), custom_call_target="InvertDiagBlocksLowerTriangular" | custom-call | tf_op jit(solution)/shard_map/vmap(jit(_solve_triangular))/triangular_solve/custom-call.1 | solution.py:87
  499.5 74.7 %while.225 = (s32[]{:T(128)}, f32[2,128,128]{2,1,0:T(8,128)S(1)}, f32[2,128,128]{2,1,0:T(8,128)}, f32[8]{0:T(128)}, f32[8,2,64,128]{3,2,1,0:T(8,128)}, /*index=5...) while((s32[]{:T(128)}, f32[2,128,128]{2,1,0:T(8,128)S(1)}, ...), condition=%wide.region_22.24_spmd.clone, body=%wide.region_21.23_spmd.clone.sunk | while | flops 100941824 | bytes 1379975 | solution.py:269
  574.2 38.2 %all-gather.2 = bf16[16,128,128]{2,1,0:T(8,128)(2,1)} all-gather(bf16[2,128,128]{2,1,0:T(8,128)(2,1)S(1)} %convert_element_type.372), channel_id=4, replica_groups=mesh['seq'=8,'head'=4] {'seq'}, dimensions={0}, use_global_device_ids=true | all-gather | bytes 589824 | tf_op jit(solution)/shard_map/all_gather | solution.py:24
  658.5 68.4 %while.217 = (s32[]{:T(128)}, f32[2,128,128]{2,1,0:T(8,128)}, f32[8,2,64,128]{3,2,1,0:T(8,128)}, f32[8]{0:T(128)S(1)}, f32[8,2,64,128]{3,2,1,0:T(8,128)}, /*inde...) while((s32[]{:T(128)}, f32[2,128,128]{2,1,0:T(8,128)}, ...), condition=%wide.region_27.29_spmd, body=%wide.region_26.28_spmd.sunk | while | flops 88244224 | bytes 1248897 | solution.py:274
  737.3 34.3 %reduce-scatter.10.cloned.1.call-done = bf16[128,1024]{1,0:T(8,128)(2,1)} async-done(((bf16[512,1024]{1,0:T(8,128)(2,1)}), bf16[128,1024]{1,0:T(8,128)(2,1)}) %reduce-scatter.10.cloned.1.call-update) | async-done | bytes 262160 | tf_op jit(solution)/shard_map/reduce_scatter | solution.py:276
  820.4 78.4 %all-gather.24.cloned.1.call-done = bf16[3,1024,704]{1,2,0:T(8,128)(2,1)} async-done(((bf16[3,128,704]{1,2,0:T(8,128)(2,1)}), bf16[3,1024,704]{1,2,0:T(8,128)(2,1)}) %all-gather.24.cloned.1.call-update) | async-done | bytes 4325392 | tf_op jit(solution)/shard_map/all_gather | solution.py:290
  973.8 75.6 %while.218 = (s32[]{:T(128)}, f32[2,128,128]{2,1,0:T(8,128)S(1)}, f32[8,2,64,128]{3,2,1,0:T(8,128)}, f32[8,2,128,128]{3,2,1,0:T(8,128)}, f32[8,2,64,128]{3,2,1,0...) while((s32[]{:T(128)}, f32[2,128,128]{2,1,0:T(8,128)S(1)}, ...), condition=%wide.region_35.37_spmd, body=%wide.region_34.36_spmd.sunk | while | flops 88276992 | bytes 1577109 | solution.py:200
  1057.7 76.8 %while.221 = (s32[]{:T(128)}, f32[2,128,128]{2,1,0:T(8,128)S(1)}, f32[8,2,64,128]{3,2,1,0:T(8,128)}, f32[8,2,128,128]{3,2,1,0:T(8,128)}, f32[8,2,64,128]{3,2,1,0...) while((s32[]{:T(128)}, f32[2,128,128]{2,1,0:T(8,128)S(1)}, ...), condition=%wide.region_53.56_spmd, body=%wide.region_52.55_spmd.sunk | while | flops 88276992 | bytes 1577109 | solution.py:200
  1141.4 33.3 %all-gather.5 = bf16[16,128,128]{2,1,0:T(8,128)(2,1)} all-gather(bf16[2,128,128]{2,1,0:T(8,128)(2,1)S(1)} %copy.502), channel_id=7, replica_groups=mesh['seq'=8,'head'=4] {'seq'}, dimensions={0}, use_global_device_ids=true | all-gather | bytes 589824 | tf_op jit(solution)/shard_map/all_gather | solution.py:46
  1174.6 33.2 %all-gather.8 = bf16[16,128,128]{2,1,0:T(8,128)(2,1)} all-gather(bf16[2,128,128]{2,1,0:T(8,128)(2,1)S(1)} %copy.527), channel_id=10, replica_groups=mesh['seq'=8,'head'=4] {'seq'}, dimensions={0}, use_global_device_ids=true | all-gather | bytes 589824 | tf_op jit(solution)/shard_map/all_gather | solution.py:46
  1216.2 47.3 %while.226 = (s32[]{:T(128)}, f32[2,128,128]{2,1,0:T(8,128)S(1)}, f32[8,2,64,128]{3,2,1,0:T(8,128)}, f32[8,2,64,128]{3,2,1,0:T(8,128)}, f32[8,2,64,128]{3,2,1,0:...) while((s32[]{:T(128)}, f32[2,128,128]{2,1,0:T(8,128)S(1)}, ...), condition=%wide.region_39.41_spmd.clone, body=%wide.region_38.40_spmd.clone.sunk | while | flops 88276992 | bytes 1313951 | solution.py:200
  1263.5 33.4 %all-gather.6 = bf16[16,128,128]{2,1,0:T(8,128)(2,1)} all-gather(bf16[2,128,128]{2,1,0:T(8,128)(2,1)S(1)} %convert_element_type.389), channel_id=8, replica_groups=mesh['seq'=8,'head'=4] {'seq'}, dimensions={0}, use_global_device_ids=true | all-gather | bytes 589824 | tf_op jit(solution)/shard_map/all_gather | solution.py:46
  1309.2 110.9 %while.220 = (s32[]{:T(128)}, f32[2,128,128]{2,1,0:T(8,128)S(1)}, f32[8,2,64,128]{3,2,1,0:T(8,128)}, f32[8,2,64,128]{3,2,1,0:T(8,128)}, f32[8,2,64,128]{3,2,1,0:...) while((s32[]{:T(128)}, f32[2,128,128]{2,1,0:T(8,128)S(1)}, ...), condition=%wide.region_43.45_spmd, body=%wide.region_42.44_spmd.sunk | while | flops 176308224 | bytes 2367685 | solution.py:200
  1426.6 47.5 %while.227 = (s32[]{:T(128)}, f32[2,128,128]{2,1,0:T(8,128)S(1)}, f32[8,2,64,128]{3,2,1,0:T(8,128)}, f32[8,2,64,128]{3,2,1,0:T(8,128)}, f32[8,2,64,128]{3,2,1,0:...) while((s32[]{:T(128)}, f32[2,128,128]{2,1,0:T(8,128)S(1)}, ...), condition=%wide.region_57.60_spmd.clone, body=%wide.region_56.59_spmd.clone.sunk | while | flops 88276992 | bytes 1313951 | solution.py:200
  1519.6 111.2 %while.223 = (s32[]{:T(128)}, f32[2,128,128]{2,1,0:T(8,128)S(1)}, f32[8,2,64,128]{3,2,1,0:T(8,128)}, f32[8,2,64,128]{3,2,1,0:T(8,128)}, f32[8,2,64,128]{3,2,1,0:...) while((s32[]{:T(128)}, f32[2,128,128]{2,1,0:T(8,128)S(1)}, ...), condition=%wide.region_61.64_spmd, body=%wide.region_60.63_spmd.sunk | while | flops 176308224 | bytes 2367685 | solution.py:200
  1727.1 36.3 %all-reduce.27 = (f32[1024,2]{0,1:T(2,128)}, f32[3,4,256]{2,0,1:T(4,128)S(1)}) all-reduce(f32[1024,2]{0,1:T(2,128)S(1)} %convolution_add_fusion.34, f32[3,4,256]{2,0,1:T(4,128)S(1)} %add_add_fusion.6), channel_id=1, replica_groups=mesh['seq'=8,'head'=4] {'seq'}, use_global_device_ids=true, to_apply=%region_72.75 | all-reduce | flops 5120 | bytes 40960 | tf_op jit(solution)/shard_map/psum | solution.py:374
  1765.5 40.4 %all-reduce.26 = (f32[1024]{0:T(1024)}, f32[128]{0:T(128)}, f32[1024]{0:T(1024)}) all-reduce(f32[1024]{0:T(1024)S(1)} %add.708, f32[128]{0:T(128)S(1)} %add.712, f32[1024]{0:T(1024)S(1)} %add.713), channel_id=1, replica_groups=mesh['seq'=8,'head'=4] {'seq','head'}, use_global_device_ids=true, to_apply=%region_70.73 | all-reduce | flops 2176 | bytes 17408 | tf_op jit(solution)/shard_map/psum | solution.py:375
  1810.0 113.0 %all-reduce.30.cloned.1.call-done = f32[4,1024,256]{1,2,0:T(8,128)} async-done(((f32[4,1024,256]{1,2,0:T(8,128)}), f32[4,1024,256]{1,2,0:T(8,128)}) %all-reduce.30.cloned.1.call-update) | async-done | bytes 4194320 | tf_op jit(solution)/shard_map/psum | solution.py:374
  1928.4 151.8 %reduce-scatter.26.cloned.1.call-done = f32[3,128,704]{1,2,0:T(8,128)} async-done(((f32[3,1024,704]{1,2,0:T(8,128)}), f32[3,128,704]{1,2,0:T(8,128)}) %reduce-scatter.26.cloned.1.call-update) | async-done | bytes 1081360 | tf_op jit(solution)/shard_map/reduce_scatter | solution.py:378
  (1182 shorter events, 1263.5 us)
Async XLA Ops:
  7.2 23.5 %all-gather.20.cloned.1.call-start = ((), (), s32[]{:S(2)}) async-start(), calls=%async_computation.9 | async-start | bytes 1310720 | tf_op jit(solution)/shard_map/all_gather | solution.py:258
  11.1 38.5 %all-gather.26.cloned.1.call-start = ((), (), s32[]{:S(2)}) async-start(), calls=%async_computation.14 | async-start | bytes 1310720 | tf_op jit(solution)/shard_map/all_gather | solution.py:258
  11.9 759.8 %reduce-scatter.10.cloned.1.call-start = ((), (), s32[]{:S(2)}) async-start(), calls=%async_computation.10 | async-start | bytes 1310720 | tf_op jit(solution)/shard_map/reduce_scatter | solution.py:276
  33.5 24.0 %collective-permute-start = (bf16[3,3,256]{2,1,0:T(4,128)(2,1)S(1)}, bf16[3,3,256]{2,1,0:T(4,128)(2,1)S(1)}, u32[]{:S(2)}, u32[]{:S(2)}) collective-permute-start(bf16[3,3,256]{2,1,0:T(4,128)(2,1)S(1)} %slice.294), channel_id=1, source_target_pairs={{0,4},{4,8},{8,12},{12,16},{16,20},{20,24},{24,28},{1,5},{5,9},{9,... | collective-permute-start | bytes 13832 | tf_op jit(solution)/shard_map/ppermute | solution.py:18
  52.4 14.0 collective-permute-start.1
  733.3 66.4 %reduce-scatter.14.cloned.1.call-start = ((), (), s32[]{:S(2)}) async-start(), calls=%async_computation.15 | async-start | bytes 1310720 | tf_op jit(solution)/shard_map/reduce_scatter | solution.py:276
  737.1 83.3 %all-gather.22.cloned.1.call-start = ((), (), s32[]{:S(2)}) async-start(), calls=%async_computation.11 | async-start | bytes 1310720 | tf_op jit(solution)/shard_map/all_gather | solution.py:287
  801.2 250.7 %copy-start.133 = (f32[128]{0:T(128)}, f32[128]{0:T(128)S(1)}, u32[]{:S(2)}) copy-start(f32[128]{0:T(128)S(1)} %get-tuple-element.2529) | copy-start | bytes 1540
  803.4 95.4 %all-gather.24.cloned.1.call-start = ((), (), s32[]{:S(2)}) async-start(), calls=%async_computation.12 | async-start | bytes 4866048 | tf_op jit(solution)/shard_map/all_gather | solution.py:290
  804.0 111.3 %all-gather.34.cloned.1.call-start = ((), (), s32[]{:S(2)}) async-start(), calls=%async_computation.26 | async-start | bytes 1310720 | tf_op jit(solution)/shard_map/all_gather | solution.py:288
  806.0 128.2 %all-gather.28.cloned.1.call-start = ((), (), s32[]{:S(2)}) async-start(), calls=%async_computation.16 | async-start | bytes 1310720 | tf_op jit(solution)/shard_map/all_gather | solution.py:287
  806.7 145.8 %all-gather.36.cloned.1.call-start = ((), (), s32[]{:S(2)}) async-start(), calls=%async_computation.27 | async-start | bytes 1310720 | tf_op jit(solution)/shard_map/all_gather | solution.py:288
  807.4 242.0 %reduce-scatter.18.cloned.1.call-start = ((), (), s32[]{:S(2)}) async-start(), calls=%async_computation.18 | async-start | bytes 1310720 | tf_op jit(solution)/shard_map/reduce_scatter | solution.py:323
  923.4 126.1 %reduce-scatter.22.cloned.1.call-start = ((), (), s32[]{:S(2)}) async-start(), calls=%async_computation.21 | async-start | bytes 1310720 | tf_op jit(solution)/shard_map/reduce_scatter | solution.py:323
  962.2 89.6 %reduce-scatter.16.cloned.1.call-start = ((), (), s32[]{:S(2)}) async-start(), calls=%async_computation.17 | async-start | bytes 1310720 | tf_op jit(solution)/shard_map/reduce_scatter | solution.py:299
  970.6 237.3 %all-gather.32.cloned.1.call-start = ((), (), s32[]{:S(2)}) async-start(), calls=%async_computation.22 | async-start | bytes 1310720 | tf_op jit(solution)/shard_map/all_gather | solution.py:329
  1054.8 155.7 %all-gather.30.cloned.1.call-start = ((), (), s32[]{:S(2)}) async-start(), calls=%async_computation.19 | async-start | bytes 1310720 | tf_op jit(solution)/shard_map/all_gather | solution.py:329
  1134.5 629.6 %reduce-scatter.20.cloned.1.call-start = ((), (), s32[]{:S(2)}) async-start(), calls=%async_computation.20 | async-start | bytes 1310720 | tf_op jit(solution)/shard_map/reduce_scatter | solution.py:368
  1671.9 5.6 collective-permute-start.2
  1683.2 80.9 %reduce-scatter.24.cloned.1.call-start = ((), (), s32[]{:S(2)}) async-start(), calls=%async_computation.23 | async-start | bytes 1310720 | tf_op jit(solution)/shard_map/reduce_scatter | solution.py:368
  1684.2 6.1 collective-permute-start.3
  1696.0 110.0 %reduce-scatter.12.cloned.1.call-start = ((), (), s32[]{:S(2)}) async-start(), calls=%async_computation.13 | async-start | bytes 1310720 | tf_op jit(solution)/shard_map/reduce_scatter | solution.py:299
  1700.4 222.7 %all-reduce.30.cloned.1.call-start = ((), (), s32[]{:S(2)}) async-start(), calls=%async_computation.24 | async-start | bytes 8388608 | tf_op jit(solution)/shard_map/psum | solution.py:374
  1711.0 369.2 %reduce-scatter.26.cloned.1.call-start = ((), (), s32[]{:S(2)}) async-start(), calls=%async_computation.25 | async-start | bytes 9732096 | tf_op jit(solution)/shard_map/reduce_scatter | solution.py:378
  (164 other events, 3082.0 us)
Sparse Core Ops, SparseCore 0:
  11.3 19.4 all-gather.19
  32.8 16.7 all-gather.25
  733.4 38.2 reduce-scatter.9
  774.8 24.8 reduce-scatter.13
  803.6 16.7 all-gather.21
  822.2 76.5 all-gather.23
  900.4 14.8 all-gather.33
  917.4 16.7 all-gather.27
  935.8 16.7 all-gather.35
  955.5 24.8 reduce-scatter.17
  983.7 24.8 reduce-scatter.21
  1011.0 24.9 reduce-scatter.15
  1054.9 16.7 all-gather.31
  1134.6 16.6 all-gather.29
  1683.3 23.5 reduce-scatter.19
  1709.2 24.8 reduce-scatter.23
  1736.7 24.8 reduce-scatter.11
  1765.7 157.2 all-reduce.29
  1927.2 152.8 reduce-scatter.25
where the time goes:
time: 2110 us; the launch traced here: 2090 us
  matrix products  790 us (37%)
  waiting for transfers between devices  485 us (23%)
  blocking collectives  348 us (16%)
  other arithmetic  259 us (12%)
  local copies, waits for them, and re-layouts  173 us (8%)
    another operation x5, other arithmetic, solve_one(): jax.scipy.linalg.solve_triangular(system_one, right_one, lower=True, unit...  162 us
    dot_general x80, matrix products, stretch_run(): jnp.einsum('bdw,bws->bds', write_rows, state_matrix, precision=highest_pr...  156 us
    reduce_scatter x1, waiting for transfers between devices, per_device(): lax.psum_scatter(dense_acc, 'seq', scatter_dimension=1, tiled=True)  152 us
    all_gather x4, blocking collectives, prefix(): lax.all_gather(a.astype(kind), axis)  139 us
    all_gather x4, blocking collectives, prefix_2(): lax.all_gather(a.astype(kind), axis)  133 us
    dot_general x80, matrix products, stretch_run(): jnp.einsum('bua,buq->baq', key_block_list, fresh_value_rows, precision=hi...  130 us
    dot_general x80, matrix products, stretch_run(): jnp.einsum('bdw,bws->bds', query_block_list, state_matrix, precision=high...  127 us
    dot_general x80, matrix products, stretch_run(): jnp.einsum('tbg,tgx->tbx', score_matrix, fresh_value_rows, precision=high...  125 us
  transfers between devices with their start and end apart: 23, of which 13 were waited for; matrix products, arithmetic and copies ran while one was open for 13% of the time, Pallas kernels for 0%

commit v1 on v0

v1 whole, which is shorter than its diff:
```python
import functools

import jax
import jax.numpy as jnp
from jax import lax
from jax.experimental import pallas as pl
from jax.experimental.pallas import tpu as pltpu
from jax.sharding import PartitionSpec as P

HEAD_DIM = 128
CONV = 4
CHUNK = 128
HALO = 16
RIM = 8
EPS = 1e-06
F32 = jnp.float32
BF16 = jnp.bfloat16
VMEM_LIMIT = 56 * 1024 * 1024


def mm(a, b, ca=1, cb=0):
    return lax.dot_general(
        a.astype(BF16), b.astype(BF16), (((ca,), (cb,)), ((), ())), preferred_element_type=F32
    )


def split(a):
    high = a.astype(BF16)
    return high, (a - high.astype(F32)).astype(BF16)


def mm3(a, b, ca=1, cb=0):
    ah, al = split(a)
    bh, bl = split(b)
    return mm(ah, bh, ca, cb) + (mm(ah, bl, ca, cb) + mm(al, bh, ca, cb))


def sigmoid(v):
    return 1.0 / (1.0 + jnp.exp(-v))


def row_info(off_ref, len_ref, m, base, rows):
    t = base + lax.broadcasted_iota(jnp.int32, (rows, 1), 0)
    start = jnp.zeros_like(t)
    length = jnp.zeros_like(t)
    for i in range(off_ref.shape[1]):
        inside = t >= off_ref[m, i]
        start = jnp.where(inside, off_ref[m, i], start)
        length = jnp.where(inside, len_ref[m, i], length)
    rel = t - start
    return rel, (rel < length).astype(F32)


def chunk_masks(rel):
    n = rel.shape[0]
    i = lax.broadcasted_iota(jnp.int32, (n, n), 0)
    j = lax.broadcasted_iota(jnp.int32, (n, n), 1)
    same = rel >= i - j
    strict = jnp.logical_and(same, i > j)
    incl = jnp.logical_and(same, i >= j)
    col = lax.broadcasted_iota(jnp.int32, (n, 1), 0)
    sees = (rel > col).astype(F32)
    last = rel[n - 1 : n, :]
    stays = ((n - 1 - col) <= last).astype(F32)
    keep = (last > n - 1).astype(F32)
    return strict, incl, sees, stays, keep


def unit_lower_inverse(a_list):
    n = a_list[0].shape[0]
    i = lax.broadcasted_iota(jnp.int32, (n, n), 0)
    j = lax.broadcasted_iota(jnp.int32, (n, n), 1)
    eye = (i == j).astype(F32)
    size = 1
    inv_list = [eye for _ in a_list]
    while size < n:
        pair = jnp.logical_and(i // size == j // size + 1, (i // size) % 2 == 1)
        below = [jnp.where(pair, a, 0.0) for a in a_list]
        if size == 1:
            inv_list = [eye - b for b in below]
        else:
            half = [mm3(b, inv) for b, inv in zip(below, inv_list)]
            inv_list = [inv - mm3(inv, h) for inv, h in zip(inv_list, half)]
        size *= 2
    return inv_list


def lagged(ext, lag, rows):
    moved = pltpu.roll(ext, lag, 0) if lag else ext
    return moved[HALO : HALO + rows]


def lag_masks(rel):
    return [None] + [(rel >= lag).astype(F32) for lag in range(1, CONV)]


def filtered(ext, taps, masks, rows):
    total = None
    for lag in range(CONV):
        term = taps[lag : lag + 1, :] * lagged(ext, lag, rows)
        if masks[lag] is not None:
            term = term * masks[lag]
        total = term if total is None else total + term
    return total


def mix_fwd_body(
    off_ref, len_ref, base_ref, x_ref, w_ref, beta_ref, taps_ref,
    pq_ref, pk_ref, pv_ref, rate_ref, ps_ref, oloc_ref, phi_ref, psi_ref, m_ref, inv_ref, wr_ref, up_ref, ts_ref,
):
    mb = pl.program_id(0)
    head = pl.program_id(1)
    rows = x_ref.shape[1] - HALO
    rel, valid = row_info(off_ref, len_ref, mb, base_ref[0], rows)
    x = x_ref[0]
    masks = lag_masks(rel)
    acts = []
    for member, out in enumerate((pq_ref, pk_ref, pv_ref)):
        proj = mm(x, w_ref[member]).astype(BF16)
        out[0] = proj
        filt = filtered(proj.astype(F32), taps_ref[member], masks, rows)
        acts.append(filt * sigmoid(filt))
    query, key, value = acts
    query = query * lax.rsqrt(jnp.sum(query * query, axis=-1, keepdims=True) + EPS)
    key = key * lax.rsqrt(jnp.sum(key * key, axis=-1, keepdims=True) + EPS)
    raw_all = mm(x, beta_ref[...])[HALO:]
    lane = lax.broadcasted_iota(jnp.int32, raw_all.shape, 1)
    raw = jnp.sum(jnp.where(lane == head, raw_all, 0.0), axis=-1, keepdims=True)
    rate_ref[0, 0] = raw
    rate = sigmoid(raw) * valid
    spans = [slice(c * CHUNK, (c + 1) * CHUNK) for c in range(rows // CHUNK)]
    all_masks = [chunk_masks(rel[s]) for s in spans]
    systems, scores = [], []
    for s, (strict, incl, _, _, _) in zip(spans, all_masks):
        both = mm(jnp.concatenate([query[s], key[s]], axis=0), key[s], 1, 1)
        scores.append(jnp.where(incl, both[:CHUNK], 0.0))
        systems.append(jnp.where(strict, rate[s] * both[CHUNK:], 0.0))
    inverses = unit_lower_inverse(systems)
    i = lax.broadcasted_iota(jnp.int32, (HEAD_DIM, HEAD_DIM), 0)
    j = lax.broadcasted_iota(jnp.int32, (HEAD_DIM, HEAD_DIM), 1)
    eye = (i == j).astype(F32)
    phis, psis, ps, olocs = [], [], [], []
    for s, masks_c, inv, score in zip(spans, all_masks, inverses, scores):
        _, _, sees, stays, keep = masks_c
        right = rate[s] * jnp.concatenate([sees * key[s], value[s]], axis=1)
        solved = mm(inv, right)
        write, update = solved[:, :HEAD_DIM], solved[:, HEAD_DIM:]
        moved = mm(stays * key[s], solved, 0, 0)
        phi = keep * eye - moved[:, :HEAD_DIM]
        psi = moved[:, HEAD_DIM:]
        scored = mm(score, solved)
        p = sees * query[s] - scored[:, :HEAD_DIM]
        m_ref[0, 0, s] = score.astype(BF16)
        inv_ref[0, 0, s] = inv.astype(BF16)
        wr_ref[0, 0, s] = write.astype(BF16)
        up_ref[0, 0, s] = update
        ps_ref[0, 0, s] = p.astype(BF16)
        oloc_ref[0, 0, s] = scored[:, HEAD_DIM:]
        phi_ref[0, 0, s] = phi
        psi_ref[0, 0, s] = psi
        phis.append(phi)
        psis.append(psi)
    trans, state = phis[0], psis[0]
    for phi, psi in zip(phis[1:], psis[1:]):
        both = mm3(phi, jnp.concatenate([trans, state], axis=1))
        trans = both[:, :HEAD_DIM]
        state = both[:, HEAD_DIM:] + psi
    ts_ref[0, 0, 0] = trans.astype(BF16)
    ts_ref[1, 0, 0] = state.astype(BF16)


def smem_spec():
    return pl.BlockSpec(memory_space=pltpu.SMEM)


def params(count):
    return pltpu.CompilerParams(
        dimension_semantics=("arbitrary",) * count, vmem_limit_bytes=VMEM_LIMIT
    )


def mix_fwd(offsets, lengths, base, x_ext, mixer_weights, beta_weight, taps):
    count, ext_rows, width = x_ext.shape
    rows = ext_rows - HALO
    heads = beta_weight.shape[1]
    per_head = pl.BlockSpec((1, 1, rows, HEAD_DIM), lambda m, h: (m, h, 0, 0))
    proj_spec = pl.BlockSpec((1, ext_rows, HEAD_DIM), lambda m, h: (m, 0, h))
    proj_shape = jax.ShapeDtypeStruct((count, ext_rows, heads * HEAD_DIM), BF16)

    def big(kind):
        return jax.ShapeDtypeStruct((count, heads, rows, HEAD_DIM), kind)

    return pl.pallas_call(
        mix_fwd_body,
        grid=(count, heads),
        in_specs=[
            smem_spec(), smem_spec(), smem_spec(),
            pl.BlockSpec((1, ext_rows, width), lambda m, h: (m, 0, 0)),
            pl.BlockSpec((3, width, HEAD_DIM), lambda m, h: (0, 0, h)),
            pl.BlockSpec(beta_weight.shape, lambda m, h: (0, 0)),
            pl.BlockSpec((3, CONV, HEAD_DIM), lambda m, h: (0, 0, h)),
        ],
        out_specs=[proj_spec] * 3
        + [pl.BlockSpec((1, 1, rows, 1), lambda m, h: (m, h, 0, 0))]
        + [per_head] * 8
        + [pl.BlockSpec((2, 1, 1, HEAD_DIM, HEAD_DIM), lambda m, h: (0, m, h, 0, 0))],
        out_shape=[proj_shape] * 3
        + [jax.ShapeDtypeStruct((count, heads, rows, 1), F32)]
        + [big(BF16), big(F32), big(F32), big(F32), big(BF16), big(BF16), big(BF16), big(F32)]
        + [jax.ShapeDtypeStruct((2, count, heads, HEAD_DIM, HEAD_DIM), BF16)],
        compiler_params=params(2),
        name="mix_fwd",
    )(offsets, lengths, base, x_ext, mixer_weights, beta_weight, taps)


def mix_out_body(state_ref, ps_ref, oloc_ref, phi_ref, psi_ref, gain_ref, w_ref, start_ref, mixed_ref, head_ref, part_ref):
    heads = ps_ref.shape[1]
    rows = ps_ref.shape[2]
    gain = gain_ref[...]
    states = [state_ref[0, h] for h in range(heads)]
    for c in range(rows // CHUNK):
        s = slice(c * CHUNK, (c + 1) * CHUNK)
        for h in range(heads):
            state = states[h]
            start_ref[0, h, s] = state.astype(BF16)
            mixed = oloc_ref[0, h, s] + mm(ps_ref[0, h, s], state)
            mixed_ref[0, h, s] = mixed
            normed = mixed * lax.rsqrt(jnp.mean(mixed * mixed, axis=-1, keepdims=True) + EPS) * gain
            head_ref[0, s, h * HEAD_DIM : (h + 1) * HEAD_DIM] = normed.astype(BF16)
            states[h] = mm3(phi_ref[0, h, s], state) + psi_ref[0, h, s]
    part_ref[0] = mm(head_ref[0], w_ref[0], 1, 1).astype(BF16)


def mix_out(state_in, ps, oloc, phi, psi, out_gain, mixer_weights):
    count, heads, rows, _ = ps.shape
    width = mixer_weights.shape[1]
    head_width = mixer_weights.shape[2]
    per_mb = pl.BlockSpec((1, heads, rows, HEAD_DIM), lambda m: (m, 0, 0, 0))
    return pl.pallas_call(
        mix_out_body,
        grid=(count,),
        in_specs=[
            pl.BlockSpec((1, heads, HEAD_DIM, HEAD_DIM), lambda m: (m, 0, 0, 0)),
            per_mb, per_mb, per_mb, per_mb,
            pl.BlockSpec((1, HEAD_DIM), lambda m: (0, 0)),
            pl.BlockSpec((1, width, head_width), lambda m: (3, 0, 0)),
        ],
        out_specs=[
            per_mb, per_mb,
            pl.BlockSpec((1, rows, head_width), lambda m: (m, 0, 0)),
            pl.BlockSpec((1, rows, width), lambda m: (m, 0, 0)),
        ],
        out_shape=[
            jax.ShapeDtypeStruct(ps.shape, BF16),
            jax.ShapeDtypeStruct(ps.shape, F32),
            jax.ShapeDtypeStruct((count, rows, head_width), BF16),
            jax.ShapeDtypeStruct((count, rows, width), BF16),
        ],
        compiler_params=params(1),
        name="mix_out",
    )(state_in, ps, oloc, phi, psi, out_gain, mixer_weights)


def dense_body(x_ref, g_ref, w_ref, down_ref, gin_ref, grad_ref, acc_ref):
    step = pl.program_id(0)
    x = x_ref[...]
    g = g_ref[...]
    gate = mm(x, w_ref[0])
    up = mm(x, w_ref[1])
    grad_hidden = mm(g, w_ref[2])
    sg = sigmoid(gate)
    silu = gate * sg
    hidden = (silu * up).astype(BF16)
    grad_gate = (grad_hidden * up * (sg * (1.0 + gate * (1.0 - sg)))).astype(BF16)
    grad_up = (grad_hidden * silu).astype(BF16)
    down_ref[...] = mm(hidden, w_ref[2], 1, 1).astype(BF16)
    gin_ref[...] = (mm(grad_gate, w_ref[0], 1, 1) + mm(grad_up, w_ref[1], 1, 1)).astype(BF16)

    @pl.when(step == 0)
    def _():
        acc_ref[0] = mm(x, grad_gate, 0, 0)
        acc_ref[1] = mm(x, grad_up, 0, 0)
        acc_ref[2] = mm(g, hidden, 0, 0)

    @pl.when(step > 0)
    def _():
        acc_ref[0] += mm(x, grad_gate, 0, 0)
        acc_ref[1] += mm(x, grad_up, 0, 0)
        acc_ref[2] += mm(g, hidden, 0, 0)

    @pl.when(step == pl.num_programs(0) - 1)
    def _():
        grad_ref[...] = acc_ref[...].astype(BF16)


def dense(dense_in, grad_top, weights):
    rows, width = dense_in.shape
    hidden = weights.shape[2]
    tile = 256
    row_spec = pl.BlockSpec((tile, width), lambda i: (i, 0))
    whole = pl.BlockSpec((3, width, hidden), lambda i: (0, 0, 0), pipeline_mode=pl.Buffered(1))
    return pl.pallas_call(
        dense_body,
        grid=(rows // tile,),
        in_specs=[row_spec, row_spec, whole],
        out_specs=[row_spec, row_spec, whole],
        out_shape=[
            jax.ShapeDtypeStruct((rows, width), BF16),
            jax.ShapeDtypeStruct((rows, width), BF16),
            jax.ShapeDtypeStruct((3, width, hidden), BF16),
        ],
        scratch_shapes=[pltpu.VMEM((3, width, hidden), F32)],
        compiler_params=params(1),
        name="dense",
    )(dense_in, grad_top, weights)


def mix_back_body(grad_ref, w_ref, mixed_ref, gain_ref, ps_ref, phi_ref, dout_ref, gain_grad_ref, dstate_ref):
    heads = ps_ref.shape[1]
    rows = ps_ref.shape[2]
    gain = gain_ref[...]
    grad_head = mm(grad_ref[0], w_ref[0])
    gain_grad = jnp.zeros((1, HEAD_DIM), F32)
    douts = []
    for h in range(heads):
        e = grad_head[:, h * HEAD_DIM : (h + 1) * HEAD_DIM]
        v = mixed_ref[0, h]
        r = lax.rsqrt(jnp.mean(v * v, axis=-1, keepdims=True) + EPS)
        weighted = e * gain
        dout = r * weighted - v * (r * r * r * jnp.mean(weighted * v, axis=-1, keepdims=True))
        gain_grad += jnp.sum(e * v * r, axis=0, keepdims=True)
        dout = dout.astype(BF16)
        dout_ref[0, h] = dout
        douts.append(dout)
    states = [None] * heads
    for c in reversed(range(rows // CHUNK)):
        s = slice(c * CHUNK, (c + 1) * CHUNK)
        for h in range(heads):
            new = mm(ps_ref[0, h, s], douts[h][s], 0, 0)
            if states[h] is not None:
                new += mm3(phi_ref[0, h, s], states[h], 0, 0)
            states[h] = new
    for h in range(heads):
        dstate_ref[0, h] = states[h].astype(BF16)

    @pl.when(pl.program_id(0) == 0)
    def _():
        gain_grad_ref[...] = gain_grad

    @pl.when(pl.program_id(0) > 0)
    def _():
        gain_grad_ref[...] += gain_grad


def mix_back(grad_attn, mixer_weights, mixed, out_gain, ps, phi):
    count, heads, rows, _ = ps.shape
    width = mixer_weights.shape[1]
    head_width = mixer_weights.shape[2]
    per_mb = pl.BlockSpec((1, heads, rows, HEAD_DIM), lambda m: (m, 0, 0, 0))
    return pl.pallas_call(
        mix_back_body,
        grid=(count,),
        in_specs=[
            pl.BlockSpec((1, rows, width), lambda m: (m, 0, 0)),
            pl.BlockSpec((1, width, head_width), lambda m: (3, 0, 0)),
            per_mb,
            pl.BlockSpec((1, HEAD_DIM), lambda m: (0, 0)),
            per_mb, per_mb,
        ],
        out_specs=[
            per_mb,
            pl.BlockSpec((1, HEAD_DIM), lambda m: (0, 0)),
            pl.BlockSpec((1, heads, HEAD_DIM, HEAD_DIM), lambda m: (m, 0, 0, 0)),
        ],
        out_shape=[
            jax.ShapeDtypeStruct(ps.shape, BF16),
            jax.ShapeDtypeStruct((1, HEAD_DIM), F32),
            jax.ShapeDtypeStruct((count, heads, HEAD_DIM, HEAD_DIM), BF16),
        ],
        compiler_params=params(1),
        name="mix_back",
    )(grad_attn, mixer_weights, mixed, out_gain, ps, phi)


def mix_grad_body(
    off_ref, len_ref, base_ref, pq_ref, pk_ref, pv_ref, rate_ref, taps_ref, dend_ref, dout_ref, start_ref, ps_ref, phi_ref,
    m_ref, inv_ref, wr_ref, up_ref,
    gq_ref, gk_ref, gv_ref, tail_ref, rim_ref, grate_ref, gtaps_ref,
):
    mb = pl.program_id(1)
    rows = rate_ref.shape[2]
    rel, valid = row_info(off_ref, len_ref, mb, base_ref[0], rows)
    masks = lag_masks(rel)
    projs, filts, sigs, acts = [], [], [], []
    for member, ref in enumerate((pq_ref, pk_ref, pv_ref)):
        proj = ref[0].astype(F32)
        filt = filtered(proj, taps_ref[member], masks, rows)
        sg = sigmoid(filt)
        projs.append(proj)
        filts.append(filt)
        sigs.append(sg)
        acts.append(filt * sg)
    rq = lax.rsqrt(jnp.sum(acts[0] * acts[0], axis=-1, keepdims=True) + EPS)
    rk = lax.rsqrt(jnp.sum(acts[1] * acts[1], axis=-1, keepdims=True) + EPS)
    query = acts[0] * rq
    key = acts[1] * rk
    value = acts[2]
    sig_rate = sigmoid(rate_ref[0, 0])
    rate = sig_rate * valid
    dstate = dend_ref[0, 0]
    spans = [slice(c * CHUNK, (c + 1) * CHUNK) for c in range(rows // CHUNK)]
    dstates = [None] * len(spans)
    for c in reversed(range(len(spans))):
        s = spans[c]
        dstates[c] = dstate
        if c:
            dstate = mm3(phi_ref[0, 0, s], dstate, 0, 0) + mm(ps_ref[0, 0, s], dout_ref[0, 0, s], 0, 0)
    dqs, dks, dvs, drates = [], [], [], []
    for c, s in enumerate(spans):
        strict, incl, sees, stays, _ = chunk_masks(rel[s])
        q, k, v, b = query[s], key[s], value[s], rate[s]
        dout = dout_ref[0, 0, s]
        start = start_ref[0, 0, s]
        fresh = up_ref[0, 0, s] - mm(wr_ref[0, 0, s], start)
        dfresh = mm(m_ref[0, 0, s], dout, 0, 0) + mm(stays * k, dstates[c])
        e = mm(inv_ref[0, 0, s], dfresh, 0, 0)
        left = jnp.concatenate([dout, e.astype(BF16)], axis=0)
        right = jnp.concatenate([fresh.astype(BF16), start], axis=0)
        outer = mm(left, right, 1, 1)
        dscore = jnp.where(incl, outer[:CHUNK, :CHUNK], 0.0)
        dsystem = jnp.where(strict, -outer[CHUNK:, :CHUNK], 0.0)
        grads = jnp.concatenate([dscore, dsystem], axis=0).astype(BF16)
        byk = mm(grads, k)
        z = byk[CHUNK:] - sees * outer[CHUNK:, CHUNK:]
        dqs.append(sees * outer[:CHUNK, CHUNK:] + byk[:CHUNK])
        dk = mm(grads, jnp.concatenate([q, b * k], axis=0), 0, 0)
        dks.append(dk + stays * mm(fresh, dstates[c], 1, 1) + b * z)
        dvs.append(b * e)
        drates.append(jnp.sum(e * v + k * z, axis=-1, keepdims=True))
    dq = jnp.concatenate(dqs, axis=0)
    dk = jnp.concatenate(dks, axis=0)
    dv = jnp.concatenate(dvs, axis=0)
    drate = jnp.concatenate(drates, axis=0)
    grate_ref[0, 0] = drate * valid * sig_rate * (1.0 - sig_rate)
    dacts = [
        rq * dq - acts[0] * (rq * rq * rq * jnp.sum(dq * acts[0], axis=-1, keepdims=True)),
        rk * dk - acts[1] * (rk * rk * rk * jnp.sum(dk * acts[1], axis=-1, keepdims=True)),
        dv,
    ]
    for member, out in enumerate((gq_ref, gk_ref, gv_ref)):
        sg = sigs[member]
        dfilt = dacts[member] * (sg * (1.0 + filts[member] * (1.0 - sg)))
        taps = taps_ref[member]
        total = None
        pieces = []
        for lag in range(CONV):
            masked = dfilt if lag == 0 else dfilt * masks[lag]
            pieces.append(jnp.sum(masked * lagged(projs[member], lag, rows), axis=0, keepdims=True))
            scaled = masked * taps[lag : lag + 1, :]
            ext = jnp.concatenate([jnp.zeros((RIM, HEAD_DIM), F32), scaled], axis=0)
            if lag:
                ext = pltpu.roll(ext, rows + RIM - lag, 0)
            total = ext if total is None else total + ext
        here = total[RIM:]
        out[0] = here.astype(BF16)
        tail_ref[0, member] = here[rows - RIM :]
        rim_ref[0, member] = total[:RIM]
        gt = jnp.concatenate(pieces, axis=0)

        @pl.when(mb == 0)
        def _(gt=gt, member=member):
            gtaps_ref[member] = gt

        @pl.when(mb > 0)
        def _(gt=gt, member=member):
            gtaps_ref[member] += gt


def mix_grad(offsets, lengths, base, proj3, rates, taps, dend, dout, start, ps, phi, m, inv, wr, up):
    count, heads, rows, _ = ps.shape
    ext_rows = rows + HALO
    per_head = pl.BlockSpec((1, 1, rows, HEAD_DIM), lambda h, m: (m, h, 0, 0))
    proj_spec = pl.BlockSpec((1, ext_rows, HEAD_DIM), lambda h, m: (m, 0, h))
    out_spec = pl.BlockSpec((1, rows, HEAD_DIM), lambda h, m: (m, 0, h))
    rate_spec = pl.BlockSpec((1, 1, rows, 1), lambda h, m: (m, h, 0, 0))
    taps_spec = pl.BlockSpec((3, CONV, HEAD_DIM), lambda h, m: (0, 0, h))
    small = pl.BlockSpec((1, 3, RIM, HEAD_DIM), lambda h, m: (m, 0, 0, h))
    small_shape = jax.ShapeDtypeStruct((count, 3, RIM, heads * HEAD_DIM), F32)
    return pl.pallas_call(
        mix_grad_body,
        grid=(heads, count),
        in_specs=[
            smem_spec(), smem_spec(), smem_spec(),
            proj_spec, proj_spec, proj_spec, rate_spec, taps_spec,
            pl.BlockSpec((1, 1, HEAD_DIM, HEAD_DIM), lambda h, m: (m, h, 0, 0)),
        ]
        + [per_head] * 8,
        out_specs=[out_spec] * 3 + [small, small, rate_spec, taps_spec],
        out_shape=[jax.ShapeDtypeStruct((count, rows, heads * HEAD_DIM), BF16)] * 3
        + [
            small_shape, small_shape,
            jax.ShapeDtypeStruct(rates.shape, F32),
            jax.ShapeDtypeStruct(taps.shape, F32),
        ],
        compiler_params=params(2),
        name="mix_grad",
    )(offsets, lengths, base, *proj3, rates, taps, dend, dout, start, ps, phi, m, inv, wr, up)


def proj_back_body(
    gq_ref, gk_ref, gv_ref, tail_ref, rim_ref, grate_ref, x_ref, w_ref, beta_ref, gattn_ref, head_ref,
    gx_ref, gw_ref, gbeta_ref, acc_ref,
):
    step = pl.program_id(0)
    rows = gq_ref.shape[1]
    heads = grate_ref.shape[1]
    lane = lax.broadcasted_iota(jnp.int32, (rows, heads), 1)
    grate = jnp.zeros((rows, heads), F32)
    for h in range(heads):
        grate = jnp.where(lane == h, grate_ref[0, h], grate)
    x = x_ref[0, HALO:, :]
    total = mm(grate, beta_ref[...], 1, 1)
    adds = []
    for member, ref in enumerate((gq_ref, gk_ref, gv_ref)):
        last = (tail_ref[0, member] + rim_ref[0, member]).astype(BF16)
        g = jnp.concatenate([ref[0, : rows - RIM], last], axis=0)
        total += mm(g, w_ref[member], 1, 1)
        adds.append(mm(x, g, 0, 0))
    adds.append(mm(gattn_ref[0], head_ref[0], 0, 0))
    gx_ref[0] = total.astype(BF16)
    gb = mm(x, grate, 0, 0)

    @pl.when(step == 0)
    def _():
        for member in range(4):
            acc_ref[member] = adds[member]
        gbeta_ref[...] = gb

    @pl.when(step > 0)
    def _():
        for member in range(4):
            acc_ref[member] += adds[member]
        gbeta_ref[...] += gb

    @pl.when(step == pl.num_programs(0) - 1)
    def _():
        gw_ref[...] = acc_ref[...].astype(BF16)


def proj_back(g3, tail, rim, grate, x_ext, mixer_weights, beta_weight, grad_attn, head_out):
    count, rows, head_width = g3[0].shape
    ext_rows, width = x_ext.shape[1:]
    heads = beta_weight.shape[1]
    g_spec = pl.BlockSpec((1, rows, head_width), lambda m: (m, 0, 0))
    small = pl.BlockSpec((1, 3, RIM, head_width), lambda m: (m, 0, 0, 0))
    row_spec = pl.BlockSpec((1, rows, width), lambda m: (m, 0, 0))
    return pl.pallas_call(
        proj_back_body,
        grid=(count,),
        in_specs=[
            g_spec, g_spec, g_spec, small, small,
            pl.BlockSpec((1, heads, rows, 1), lambda m: (m, 0, 0, 0)),
            pl.BlockSpec((1, ext_rows, width), lambda m: (m, 0, 0)),
            pl.BlockSpec((3, width, head_width), lambda m: (0, 0, 0)),
            pl.BlockSpec((width, heads), lambda m: (0, 0)),
            row_spec, g_spec,
        ],
        out_specs=[
            row_spec,
            pl.BlockSpec((4, width, head_width), lambda m: (0, 0, 0)),
            pl.BlockSpec((width, heads), lambda m: (0, 0)),
        ],
        out_shape=[
            jax.ShapeDtypeStruct((count, rows, width), BF16),
            jax.ShapeDtypeStruct((4, width, head_width), BF16),
            jax.ShapeDtypeStruct((width, heads), F32),
        ],
        scratch_shapes=[pltpu.VMEM((4, width, head_width), F32)],
        compiler_params=params(1),
        name="proj_back",
    )(*g3, tail, rim, grate, x_ext, mixer_weights, beta_weight, grad_attn, head_out)


def shifted(block, axis, distance):
    count = lax.axis_size(axis)
    return lax.ppermute(block, axis, [(i, (i + distance) % count) for i in range(count)])


def compose(pair, axis, backward):
    count = lax.axis_size(axis)
    place = lax.axis_index(axis)
    gathered = lax.all_gather(pair, axis)
    laps = count - 1 - place if backward else place

    def one(lap, state):
        source = count - 1 - lap if backward else lap
        block = lax.dynamic_index_in_dim(gathered, source, 0, False)
        return (
            jnp.einsum("mhij,mhjk->mhik", block[0], state.astype(BF16), preferred_element_type=F32)
            + block[1]
        )

    return lax.fori_loop(0, laps, one, jnp.zeros(pair.shape[1:], F32))


def rms(values, gain):
    return values * lax.rsqrt(jnp.mean(values * values, axis=-1, keepdims=True) + EPS) * gain


def rms_back(grad, values, gain):
    inv = lax.rsqrt(jnp.mean(values * values, axis=-1, keepdims=True) + EPS)
    weighted = grad * gain
    grad_in = inv * weighted - values * inv**3 * jnp.mean(weighted * values, axis=-1, keepdims=True)
    return grad_in, jnp.sum(grad * values * inv, axis=(0, 1))


def per_device(
    inputs, attn_gain, mixer_weights, beta_weight, filter_weights, out_gain, dense_gain, dense_weights,
    seq_offsets, seq_lengths, out_grad,
):
    count, local_rows, width = inputs.shape
    rows = local_rows * lax.axis_size("head")
    base = (lax.axis_index("seq") * rows).astype(jnp.int32).reshape(1)
    taps = filter_weights.astype(F32)
    gain_row = out_gain.reshape(1, HEAD_DIM)
    dense_full = lax.all_gather(dense_weights, "seq", axis=1, tiled=True)
    grad_top = lax.all_gather(out_grad, "head", axis=1, tiled=True)

    resid_in = inputs.astype(F32)
    normed_local = rms(resid_in, attn_gain).astype(BF16)
    gathered = lax.all_gather(normed_local, "head", axis=1, tiled=True)
    halo = shifted(gathered[:, rows - HALO :, :], "seq", 1)
    x_ext = jnp.concatenate([halo, gathered], axis=1)
    pq, pk, pv, rates, ps, oloc, phi, psi, score, inv, wr, up, pair = mix_fwd(
        seq_offsets, seq_lengths, base, x_ext, mixer_weights, beta_weight, taps
    )
    state_in = compose(pair, "seq", False)
    start, mixed, head_out, attn_part = mix_out(state_in, ps, oloc, phi, psi, gain_row, mixer_weights)
    attn = lax.psum_scatter(attn_part, "head", scatter_dimension=1, tiled=True).astype(F32)
    resid_mid = resid_in + attn
    dense_in = lax.all_gather(rms(resid_mid, dense_gain).astype(BF16), "head", axis=1, tiled=True)
    down_part, gin_part, dense_part = dense(
        dense_in.reshape(-1, width), grad_top.reshape(-1, width), dense_full
    )
    gin = lax.psum_scatter(
        gin_part.reshape(count, rows, width), "head", scatter_dimension=1, tiled=True
    ).astype(F32)
    down = lax.psum_scatter(
        down_part.reshape(count, rows, width), "head", scatter_dimension=1, tiled=True
    ).astype(F32)
    dense_total = lax.psum_scatter(dense_part, "seq", scatter_dimension=1, tiled=True).astype(F32)
    output = (resid_mid + down).astype(BF16)
    grad_norm, dense_gain_part = rms_back(gin, resid_mid, dense_gain)
    grad_mid = out_grad.astype(F32) + grad_norm
    grad_attn = lax.all_gather(grad_mid.astype(BF16), "head", axis=1, tiled=True)
    dout, out_gain_part, dstate = mix_back(grad_attn, mixer_weights, mixed, gain_row, ps, phi)
    dpair = jnp.stack([jnp.swapaxes(pair[0], 2, 3), dstate])
    dend = compose(dpair, "seq", True)
    gq, gk, gv, tail, rim, grate, filter_part = mix_grad(
        seq_offsets, seq_lengths, base, (pq, pk, pv), rates, taps, dend, dout, start, ps, phi, score, inv, wr, up
    )
    rim_next = shifted(rim, "seq", -1)
    last_shard = lax.axis_index("seq") == lax.axis_size("seq") - 1
    rim_next = jnp.where(last_shard, 0.0, rim_next)
    gx_part, mixer_part, beta_part = proj_back(
        (gq, gk, gv), tail, rim_next, grate, x_ext, mixer_weights, beta_weight, grad_attn, head_out
    )
    gx = lax.psum_scatter(gx_part, "head", scatter_dimension=1, tiled=True).astype(F32)
    grad_in_norm, attn_gain_part = rms_back(gx, resid_in, attn_gain)
    input_grad = grad_mid + grad_in_norm
    mixer_total = lax.psum(mixer_part.astype(F32), "seq")
    beta_total, filter_total = lax.psum((beta_part, filter_part), "seq")
    attn_gain_total, out_gain_total, dense_gain_total = lax.psum(
        (attn_gain_part, out_gain_part.reshape(HEAD_DIM), dense_gain_part), ("seq", "head")
    )
    return (
        output, input_grad, attn_gain_total, mixer_total, beta_total, filter_total, out_gain_total,
        dense_gain_total, dense_total,
    )


def solution(mesh):
    rows = P(None, ("seq", "head"), None)
    return jax.shard_map(
        per_device,
        mesh=mesh,
        in_specs=(
            rows, P(), P(None, None, "head"), P(None, "head"), P(None, None, "head"), P(), P(),
            P(None, "seq", "head"), P(), P(), rows,
        ),
        out_specs=(
            rows, rows, P(), P(None, None, "head"), P(None, "head"), P(None, None, "head"), P(), P(),
            P(None, "seq", "head"),
        ),
        check_vma=False,
    )
```

time: 2110 us -> 768 us (0.36); the launches traced: 2090 us -> 767 us
  matrix products: 790 us -> 8.04 us
  other arithmetic: 259 us -> 17.6 us
  local copies, waits for them, and re-layouts: 173 us -> 9.75 us
  blocking collectives: 348 us -> 228 us
  Pallas kernels: 0 us -> 85.3 us
  waiting for transfers between devices: 485 us -> 401 us
    dot_general x442 -> x7, matrix products: 776 us -> 8.04 us  [one(): jnp.einsum('mhij,mhjk->mhik', block[0], state.astype(BF16), preferred_ele...]
    all_gather x8 -> x0, blocking collectives: 272 us -> none  [the longest x4 139 us: prefix(): lax.all_gather(a.astype(kind), axis)]
    another operation x9 -> x1, other arithmetic: 166 us -> 1.63 us  [per_device(): dpair = jnp.stack([jnp.swapaxes(pair[0], 2, 3), dstate])]
    psum x2, blocking collectives: 76.7 us -> 228 us  [the longest x1 190 us: per_device(): mixer_total = lax.psum(mixer_part.astype(F32), 'seq')]
    psum x1 -> x0, waiting for transfers between devices: 113 us -> none  [per_device(): lax.psum((mixer_acc, beta_acc, filter_acc), 'seq')]
    all_gather x8 -> x6, waiting for transfers between devices: 75.4 us -> 186 us  [the longest x2 95.5 us: compose(): gathered = lax.all_gather(pair, axis)]
    reduce_scatter x9 -> x5, waiting for transfers between devices: 214 us -> 121 us  [the longest x1 53.2 us: per_device(): lax.psum_scatter(dense_part, 'seq', scatter_dimension=1, tiled=True)]
    pallas_call x0 -> x6, Pallas kernels: none -> 85.3 us  [the longest x1 23.3 us: mix_fwd(): pl.pallas_call(mix_fwd_body, grid=(count, heads), in_specs=[smem_spec(),...]
  transfers between devices with their start and end apart: 23 -> 14, of which waited for: 13 -> 12; matrix products, arithmetic and copies ran while one was open for 13% -> 3% of each run, Pallas kernels for 0% -> 4%
where the time goes in v1:
time: 768 us; the launch traced here: 767 us
  waiting for transfers between devices  401 us (52%)
  blocking collectives  228 us (30%)
  Pallas kernels  85.3 us (11%)
  other arithmetic  17.6 us (2%)
  between operations  14.4 us (2%)
  local copies, waits for them, and re-layouts  9.75 us (1%)
  matrix products  8.04 us (1%)
    psum x1, blocking collectives, per_device(): mixer_total = lax.psum(mixer_part.astype(F32), 'seq')  190 us
    all_gather x2, waiting for transfers between devices, compose(): gathered = lax.all_gather(pair, axis)  95.5 us
    all_gather x1, waiting for transfers between devices, per_device(): dense_full = lax.all_gather(dense_weights, 'seq', axis=1, tiled=True)  82.8 us
    reduce_scatter x1, waiting for transfers between devices, per_device(): lax.psum_scatter(dense_part, 'seq', scatter_dimension=1, tiled=True)  53.2 us
    psum x1, blocking collectives, per_device(): lax.psum((attn_gain_part, out_gain_part.reshape(HEAD_DIM), dense_gain_par...  38.6 us
    reduce_scatter x1, waiting for transfers between devices, per_device(): lax.psum_scatter(attn_part, 'head', scatter_dimension=1, tiled=True)  36.4 us
    reduce_scatter x1, waiting for transfers between devices, per_device(): lax.psum_scatter(gin_part.reshape(count, rows, width), 'head', scatter_di...  31.5 us
    all_gather x1, waiting for transfers between devices, per_device(): gathered = lax.all_gather(normed_local, 'head', axis=1, tiled=True)  25.4 us
  transfers between devices with their start and end apart: 14, of which 12 were waited for; matrix products, arithmetic and copies ran while one was open for 3% of the time, Pallas kernels for 4%

profile of v1, /device:TPU:0, one launch (start us, length us, event | category | flops | bytes accessed | tf_op | source)
XLA Modules:
  0.0 767.2 jit_solution(10026897146058561820)
XLA Ops:
  10.6 25.4 %all-gather.10.cloned.1.call-done = bf16[2,512,1024]{2,1,0:T(8,128)(2,1)} async-done(((bf16[2,128,1024]{2,1,0:T(8,128)(2,1)}), bf16[2,512,1024]{2,1,0:T(8,128)(2,1)}) %all-gather.10.cloned.1.call-update) | async-done | bytes 2097168 | tf_op jit(solution)/shard_map/all_gather | solution.py:631
  39.8 4.0 collective-permute-done
  46.9 23.3 %mix_fwd.1 = (bf16[2,528,256]{2,1,0:T(8,128)(2,1)}, bf16[2,528,256]{2,1,0:T(8,128)(2,1)}, bf16[2,528,256]{2,1,0:T(8,128)(2,1)}, f32[2,2,512,1]{3,2,1,0:T(8,128)}...) custom-call(s32[2,3]{1,0:T(2,128)} %off_ref.3, ...), custom_call_target="tpu_custom_call" | custom-call | tf_op jit(solution)/shard_map/mix_fwd/pallas_call | solution.py:193
  70.3 46.7 %all-gather.20.cloned.1.call-done = bf16[16,2,2,128,128]{4,3,2,1,0:T(8,128)(2,1)} async-done(((bf16[2,2,2,128,128]{4,3,2,1,0:T(8,128)(2,1)}), bf16[16,2,2,128,128]{4,3,2,1,0:T(8,128)(2,1)}) %all-gather.20.cloned.1.call-update) | async-done | bytes 2097168 | tf_op jit(solution)/shard_map/all_gather | solution.py:592
  117.0 5.2 mix_out.1
  124.3 36.4 %reduce-scatter.6.cloned.1.call-done = bf16[2,128,1024]{2,1,0:T(8,128)(2,1)} async-done(((bf16[2,512,1024]{2,1,0:T(8,128)(2,1)}), bf16[2,128,1024]{2,1,0:T(8,128)(2,1)}) %reduce-scatter.6.cloned.1.call-update) | async-done | bytes 524304 | tf_op jit(solution)/shard_map/reduce_scatter | solution.py:639
  164.3 20.5 %all-gather.14.cloned.1.call-done = bf16[2,512,1024]{2,1,0:T(8,128)(2,1)} async-done(((bf16[2,128,1024]{2,1,0:T(8,128)(2,1)}), bf16[2,512,1024]{2,1,0:T(8,128)(2,1)}) %all-gather.14.cloned.1.call-update) | async-done | bytes 2097168 | tf_op jit(solution)/shard_map/all_gather | solution.py:627
  184.8 82.8 %all-gather.16.cloned.1.call-done.w_ref = bf16[3,1024,704]{2,1,0:T(8,128)(2,1)} async-done(((bf16[3,128,704]{2,1,0:T(8,128)(2,1)}), bf16[3,1024,704]{2,1,0:T(8,128)(2,1)}) %all-gather.16.cloned.1.call-update) | async-done | bytes 4325392 | tf_op jit(solution)/shard_map/all_gather | solution.py:626
  267.6 22.2 %all-gather.12.cloned.1.call-done = bf16[2,512,1024]{2,1,0:T(8,128)(2,1)} async-done(((bf16[2,128,1024]{2,1,0:T(8,128)(2,1)}), bf16[2,512,1024]{2,1,0:T(8,128)(2,1)}) %all-gather.12.cloned.1.call-update) | async-done | bytes 2097168 | tf_op jit(solution)/shard_map/all_gather | solution.py:641
  289.9 22.0 %dense.1 = (bf16[1024,1024]{1,0:T(8,128)(2,1)}, bf16[1024,1024]{1,0:T(8,128)(2,1)}, bf16[3,1024,704]{2,1,0:T(8,128)(2,1)}) custom-call(bf16[1024,1024]{1,0:T(8,128)(2,1)} %bitcast.41, bf16[1024,1024]{1,0:T(8,128)(2,1)} %bitcast.40, bf16[3,1024,704]{2,1,0:T(8,128)(2,1)} %all-gather.16.cloned.1.call-done.w_ref), custom_call_target="tpu_custom_call" | custom-call | tf_op jit(solution)/shard_map/dense/pallas_call | solution.py:302
  311.9 31.5 %reduce-scatter.10.cloned.1.call-done = bf16[2,128,1024]{2,1,0:T(8,128)(2,1)} async-done(((bf16[2,512,1024]{2,1,0:T(8,128)(2,1)}), bf16[2,128,1024]{2,1,0:T(8,128)(2,1)}) %reduce-scatter.10.cloned.1.call-update) | async-done | bytes 524304 | tf_op jit(solution)/shard_map/reduce_scatter | solution.py:645
  344.9 2.3 fusion.21
  347.5 22.5 %all-gather.18.cloned.1.call-done.grad_ref.gattn_ref = bf16[2,512,1024]{2,1,0:T(8,128)(2,1)} async-done(((bf16[2,128,1024]{2,1,0:T(8,128)(2,1)}), bf16[2,512,1024]{2,1,0:T(8,128)(2,1)}) %all-gather.18.cloned.1.call-update) | async-done | bytes 2097168 | tf_op jit(solution)/shard_map/all_gather | solution.py:655
  370.0 5.7 mix_back.1
  377.9 48.8 %all-gather.22.cloned.1.call-done = bf16[16,2,2,128,128]{4,3,2,1,0:T(8,128)(2,1)} async-done(((bf16[2,2,2,128,128]{4,3,2,1,0:T(8,128)(2,1)}), bf16[16,2,2,128,128]{4,3,2,1,0:T(8,128)(2,1)}) %all-gather.22.cloned.1.call-update) | async-done | bytes 2097168 | tf_op jit(solution)/shard_map/all_gather | solution.py:592
  426.8 8.5 %while.23 = (s32[]{:T(128)}, f32[2,2,128,128]{3,2,1,0:T(8,128)S(1)}, s32[]{:T(128)}, bf16[8,2,2,2,128,128]{5,4,3,2,1,0:T(8,128)(2,1)}, s32[]{:T(128)}, /*index=5*/s32[]{:T(128)}, s32[]{:T(128)}, s32[]{:T(128)}, s32[]{}) while((s32[]{:T(128)}, f32[2,2,128,128]{3,2,1,0:T(8,128)S(1)}, s32[]{:T(128)}, bf16[8,2,2,2,128,128]{5,4,3,2,1,0:T(8,128)(2,1)}, ...), condition=%wide.region_9.10_spmd, body=%wide.region_8.9_spmd.sunk | while | flops 16973832 | bytes 1312407 | solution.py:603
  435.2 17.7 %mix_grad.1 = (bf16[2,512,256]{2,1,0:T(8,128)(2,1)}, bf16[2,512,256]{2,1,0:T(8,128)(2,1)}, bf16[2,512,256]{2,1,0:T(8,128)(2,1)}, f32[2,3,8,256]{3,2,1,0:T(8,128)...) custom-call(s32[2,3]{1,0:T(2,128)} %off_ref.3, s32[2,3]{1,0:T(2,128)} %len_ref.3, ...), custom_call_target="tpu_custom_call" | custom-call | tf_op jit(solution)/shard_map/mix_grad/pallas_call | solution.py:489
  453.2 5.2 collective-permute-done.1
  459.0 11.5 %proj_back.1 = (bf16[2,512,1024]{2,1,0:T(8,128)(2,1)}, bf16[4,1024,256]{2,1,0:T(8,128)(2,1)}, f32[1024,2]{1,0:T(8,128)}) custom-call(bf16[2,512,256]{2,1,0:T(8,128)(2,1)} %get-tuple-element.143.gq_ref, bf16[2,512,256]{2,1,0:T(8,128)(2,1)} %get-tuple-element.144.gk_ref, bf16[2,512,256]{2,1,0:T(8,128)(2,1)} %get-tuple-element.145.gv_ref, ...), custom_call_target="tpu_custom_call" | custom-call | tf_op jit(solution)/shard_map/proj_back/pallas_call | solution.py:557
  471.2 53.2 %reduce-scatter.14.cloned.1.call-done = bf16[3,128,704]{2,1,0:T(8,128)(2,1)} async-done(((bf16[3,1024,704]{2,1,0:T(8,128)(2,1)}), bf16[3,128,704]{2,1,0:T(8,128)(2,1)}) %reduce-scatter.14.cloned.1.call-update) | async-done | bytes 540688 | tf_op jit(solution)/shard_map/reduce_scatter | solution.py:651
  524.4 2.3 copy.31
  526.7 189.8 %all-reduce.3 = (f32[4,1024,256]{2,1,0:T(8,128)}, f32[1024,2]{1,0:T(8,128)S(1)}, f32[3,4,256]{2,1,0:T(4,128)}) all-reduce(bf16[4,1024,256]{2,1,0:T(8,128)(2,1)} %get-tuple-element.151, f32[1024,2]{1,0:T(8,128)S(1)} %copy-done.7, f32[3,4,256]{2,1,0:T(4,128)S(1)} %copy-done.10), channel_id=1, replica_groups=mesh['seq'=8,'head'=4] {'seq'}, use_global_device_ids=true, to_apply=%region_14.15 | all-reduce | flops 1053696 | bytes 6332416 | tf_op jit(solution)/shard_map/psum | solution.py:671
  718.7 38.6 %all-reduce = (f32[1024]{0:T(1024)}, f32[128]{0:T(128)}, f32[1024]{0:T(1024)}) all-reduce(f32[1024]{0:T(1024)S(1)} %get-tuple-element.176, f32[128]{0:T(128)S(1)} %bitcast.49, f32[1024]{0:T(1024)S(1)} %get-tuple-element.174), channel_id=1, replica_groups=mesh['seq'=8,'head'=4] {'seq','head'}, use_global_device_ids=true, to_apply=%region_13.14 | all-reduce | flops 2176 | bytes 17408 | tf_op jit(solution)/shard_map/psum | solution.py:673
  757.3 3.0 fusion.8
  (94 shorter events, 32.0 us)
Async XLA Ops:
  7.2 32.0 %copy-start.11 = (bf16[3,4,256]{2,1,0:T(4,128)(2,1)S(1)}, bf16[3,4,256]{2,1,0:T(4,128)(2,1)}, u32[]{:S(2)}) copy-start(bf16[3,4,256]{2,1,0:T(4,128)(2,1)} %param.19) | copy-start | bytes 18436
  7.2 28.8 %all-gather.10.cloned.1.call-start = ((), (), s32[]{:S(2)}) async-start(), calls=%async_computation.5 | async-start | bytes 2621440 | tf_op jit(solution)/shard_map/all_gather | solution.py:631
  10.5 106.4 %all-gather.20.cloned.1.call-start = ((), (), s32[]{:S(2)}) async-start(), calls=%async_computation.15 | async-start | bytes 2359296 | tf_op jit(solution)/shard_map/all_gather | solution.py:592
  36.8 7.0 collective-permute-start
  70.2 90.5 %reduce-scatter.6.cloned.1.call-start = ((), (), s32[]{:S(2)}) async-start(), calls=%async_computation.6 | async-start | bytes 2621440 | tf_op jit(solution)/shard_map/reduce_scatter | solution.py:639
  122.2 38.6 %copy-start = (bf16[2,128,1024]{2,1,0:T(8,128)(2,1)S(1)}, bf16[2,128,1024]{2,1,0:T(8,128)(2,1)}, u32[]{:S(2)}) copy-start(bf16[2,128,1024]{2,1,0:T(8,128)(2,1)} %param.15) | copy-start | bytes 1572868
  122.2 39.8 %copy-start.8 = (f32[1024]{0:T(1024)S(1)}, f32[1024]{0:T(1024)}, u32[]{:S(2)}) copy-start(f32[1024]{0:T(1024)} %param.21) | copy-start | bytes 12292
  122.2 62.6 %all-gather.14.cloned.1.call-start = ((), (), s32[]{:S(2)}) async-start(), calls=%async_computation.8 | async-start | bytes 2621440 | tf_op jit(solution)/shard_map/all_gather | solution.py:627
  122.8 144.8 %all-gather.16.cloned.1.call-start = ((), (), s32[]{:S(2)}) async-start(), calls=%async_computation.9 | async-start | bytes 5308416 | tf_op jit(solution)/shard_map/all_gather | solution.py:626
  124.3 165.6 %all-gather.12.cloned.1.call-start = ((), (), s32[]{:S(2)}) async-start(), calls=%async_computation.7 | async-start | bytes 2621440 | tf_op jit(solution)/shard_map/all_gather | solution.py:641
  164.1 179.4 %reduce-scatter.10.cloned.1.call-start = ((), (), s32[]{:S(2)}) async-start(), calls=%async_computation.11 | async-start | bytes 2621440 | tf_op jit(solution)/shard_map/reduce_scatter | solution.py:645
  311.8 33.1 %copy-start.3 = (bf16[2,128,1024]{2,1,0:T(8,128)(2,1)S(1)}, bf16[2,128,1024]{2,1,0:T(8,128)(2,1)}, u32[]{:S(2)}) copy-start(bf16[2,128,1024]{2,1,0:T(8,128)(2,1)} %param.25) | copy-start | bytes 1572868
  311.9 35.4 %copy-start.5 = (bf16[2,2,2,128,128]{4,3,2,1,0:T(8,128)(2,1)S(1)}, bf16[2,2,2,128,128]{4,3,2,1,0:T(8,128)(2,1)}, u32[]{:S(2)}) copy-start(bf16[2,2,2,128,128]{4,3,2,1,0:T(8,128)(2,1)} %get-tuple-element.121) | copy-start | bytes 786436
  311.9 58.1 %all-gather.18.cloned.1.call-start = ((), (), s32[]{:S(2)}) async-start(), calls=%async_computation.12 | async-start | bytes 2621440 | tf_op jit(solution)/shard_map/all_gather | solution.py:655
  347.2 79.6 %all-gather.22.cloned.1.call-start = ((), (), s32[]{:S(2)}) async-start(), calls=%async_computation.16 | async-start | bytes 2359296 | tf_op jit(solution)/shard_map/all_gather | solution.py:592
  377.3 147.1 %reduce-scatter.14.cloned.1.call-start = ((), (), s32[]{:S(2)}) async-start(), calls=%async_computation.14 | async-start | bytes 5308416 | tf_op jit(solution)/shard_map/reduce_scatter | solution.py:651
  377.9 339.4 %reduce-scatter.12.cloned.1.call-start = ((), (), s32[]{:S(2)}) async-start(), calls=%async_computation.13 | async-start | bytes 2621440 | tf_op jit(solution)/shard_map/reduce_scatter | solution.py:668
  452.9 5.5 collective-permute-start.1
  470.6 56.1 %copy-start.7 = (f32[1024,2]{1,0:T(8,128)S(1)}, f32[1024,2]{1,0:T(8,128)}, u32[]{:S(2)}) copy-start(f32[1024,2]{1,0:T(8,128)} %get-tuple-element.152) | copy-start | bytes 24580
  470.6 56.1 %copy-start.10 = (f32[3,4,256]{2,1,0:T(4,128)S(1)}, f32[3,4,256]{2,1,0:T(4,128)}, u32[]{:S(2)}) copy-start(f32[3,4,256]{2,1,0:T(4,128)} %get-tuple-element.153) | copy-start | bytes 36868
  470.6 286.7 %reduce-scatter.8.cloned.1.call-start = ((), (), s32[]{:S(2)}) async-start(), calls=%async_computation.10 | async-start | bytes 2621440 | tf_op jit(solution)/shard_map/reduce_scatter | solution.py:648
  471.2 246.1 %copy-start.9 = (f32[1024]{0:T(1024)S(1)}, f32[1024]{0:T(1024)}, u32[]{:S(2)}) copy-start(f32[1024]{0:T(1024)} %param.16) | copy-start | bytes 12292
  526.7 192.0 %copy-start.13 = (f32[1,128]{1,0:T(1,128)S(1)}, f32[1,128]{1,0:T(1,128)}, u32[]{:S(2)}) copy-start(f32[1,128]{1,0:T(1,128)} %get-tuple-element.154) | copy-start | bytes 1540
  526.7 230.6 %copy-start.4 = (bf16[2,128,1024]{2,1,0:T(8,128)(2,1)S(1)}, bf16[2,128,1024]{2,1,0:T(8,128)(2,1)}, u32[]{:S(2)}) copy-start(bf16[2,128,1024]{2,1,0:T(8,128)(2,1)} %reduce-scatter.10.cloned.1.call-done) | copy-start | bytes 1572868
  (4 other events, 65.1 us)
Sparse Core Ops, SparseCore 0:
  10.7 25.2 all-gather.9
  70.3 46.5 all-gather.19
  122.3 38.3 reduce-scatter.5
  162.2 22.5 all-gather.13
  187.7 79.8 all-gather.15
  269.1 20.7 all-gather.11
  312.0 31.4 reduce-scatter.9
  347.3 22.5 all-gather.17
  377.4 49.2 all-gather.21
  430.2 94.1 reduce-scatter.13
  526.9 31.1 reduce-scatter.11
  560.7 31.4 reduce-scatter.7

commit v2 on v1

--- a/solution.py
+++ b/solution.py
@@ -106,7 +106,7 @@
 
 def mix_fwd_body(
     off_ref, len_ref, base_ref, x_ref, w_ref, beta_ref, taps_ref,
-    pq_ref, pk_ref, pv_ref, rate_ref, ps_ref, oloc_ref, phi_ref, psi_ref, m_ref, inv_ref, wr_ref, up_ref, ts_ref,
+    pq_ref, pk_ref, pv_ref, rate_ref, ps_ref, oloc_ref, phi_ref, psi_ref, m_ref, inv_ref, wr_ref, up_ref, trans_ref, state_ref,
 ):
     mb = pl.program_id(0)
     head = pl.program_id(1)
@@ -165,8 +165,8 @@
         both = mm3(phi, jnp.concatenate([trans, state], axis=1))
         trans = both[:, :HEAD_DIM]
         state = both[:, HEAD_DIM:] + psi
-    ts_ref[0, 0, 0] = trans.astype(BF16)
-    ts_ref[1, 0, 0] = state.astype(BF16)
+    trans_ref[0, 0] = trans.astype(BF16)
+    state_ref[0, 0] = state.astype(BF16)
 
 
 def smem_spec():
@@ -203,11 +203,11 @@
         out_specs=[proj_spec] * 3
         + [pl.BlockSpec((1, 1, rows, 1), lambda m, h: (m, h, 0, 0))]
         + [per_head] * 8
-        + [pl.BlockSpec((2, 1, 1, HEAD_DIM, HEAD_DIM), lambda m, h: (0, m, h, 0, 0))],
+        + [pl.BlockSpec((1, 1, HEAD_DIM, HEAD_DIM), lambda m, h: (m, h, 0, 0))] * 2,
         out_shape=[proj_shape] * 3
         + [jax.ShapeDtypeStruct((count, heads, rows, 1), F32)]
         + [big(BF16), big(F32), big(F32), big(F32), big(BF16), big(BF16), big(BF16), big(F32)]
-        + [jax.ShapeDtypeStruct((2, count, heads, HEAD_DIM, HEAD_DIM), BF16)],
+        + [jax.ShapeDtypeStruct((count, heads, HEAD_DIM, HEAD_DIM), BF16)] * 2,
         compiler_params=params(2),
         name="mix_fwd",
     )(offsets, lengths, base, x_ext, mixer_weights, beta_weight, taps)
@@ -586,23 +586,6 @@
     return lax.ppermute(block, axis, [(i, (i + distance) % count) for i in range(count)])
 
 
-def compose(pair, axis, backward):
-    count = lax.axis_size(axis)
-    place = lax.axis_index(axis)
-    gathered = lax.all_gather(pair, axis)
-    laps = count - 1 - place if backward else place
-
-    def one(lap, state):
-        source = count - 1 - lap if backward else lap
-        block = lax.dynamic_index_in_dim(gathered, source, 0, False)
-        return (
-            jnp.einsum("mhij,mhjk->mhik", block[0], state.astype(BF16), preferred_element_type=F32)
-            + block[1]
-        )
-
-    return lax.fori_loop(0, laps, one, jnp.zeros(pair.shape[1:], F32))
-
-
 def rms(values, gain):
     return values * lax.rsqrt(jnp.mean(values * values, axis=-1, keepdims=True) + EPS) * gain
 
@@ -611,7 +594,390 @@
     inv = lax.rsqrt(jnp.mean(values * values, axis=-1, keepdims=True) + EPS)
     weighted = grad * gain
     grad_in = inv * weighted - values * inv**3 * jnp.mean(weighted * values, axis=-1, keepdims=True)
-    return grad_in, jnp.sum(grad * values * inv, axis=(0, 1))
+    return grad_in, jnp.sum(grad * values * inv, axis=0, keepdims=True)
+
+MESH = pl.DeviceIdType.MESH
+
+
+def flip(index, bit):
+    return index + bit * (1 - 2 * (index // bit % 2))
+
+
+def remote(src, dst, send, recv, seq, head):
+    return pltpu.make_async_remote_copy(
+        src_ref=src, dst_ref=dst, send_sem=send, recv_sem=recv, device_id=(seq, head), device_id_type=MESH
+    )
+
+
+def greet(devices, expected):
+    barrier = pltpu.get_barrier_semaphore()
+    for seq, head in devices:
+        pl.semaphore_signal(barrier, inc=1, device_id=(seq, head), device_id_type=MESH)
+    pl.semaphore_wait(barrier, expected)
+
+
+def pieces_of(count, rows, piece):
+    return [(m, r) for m in range(count) for r in range(0, rows, piece)]
+
+
+class HeadGather:
+    def __init__(self, out_ref, local, first_row, send, recv, piece):
+        self.out, self.local, self.first, self.piece = out_ref, local, first_row, piece
+        self.send, self.recv = send, recv
+        self.seq, self.head = lax.axis_index("seq"), lax.axis_index("head")
+        self.far, self.near = flip(self.head, 2), flip(self.head, 1)
+        self.copies = {}
+
+    def rows(self, block, r):
+        start = self.first + block * self.local + r
+        return pl.ds(pl.multiple_of(start, 16), self.piece)
+
+    def copy(self, kind, at, block, target):
+        m, r = at
+        n = self.local // self.piece
+        ref = self.out.at[m, self.rows(block, r), :]
+        c = remote(ref, ref, self.send.at[kind, m * n + r // self.piece], self.recv.at[kind, m * n + r // self.piece], self.seq, target)
+        c.start()
+        self.copies[kind, at] = c
+
+    def own(self, at):
+        self.copy(0, at, self.head, self.far)
+        self.copy(1, at, self.head, self.near)
+
+    def forward(self, at):
+        self.copies[0, at].wait_recv()
+        self.copy(2, at, self.far, self.near)
+
+    def finish(self):
+        for (kind, at), c in self.copies.items():
+            c.wait_send()
+            if kind:
+                c.wait_recv()
+
+
+class HeadScatter:
+    def __init__(self, part_ref, local, near_ref, stage_ref, far_ref, send, recv, piece):
+        self.part, self.local, self.piece = part_ref, local, piece
+        self.nearby, self.stage, self.faraway = near_ref, stage_ref, far_ref
+        self.send, self.recv = send, recv
+        self.seq, self.head = lax.axis_index("seq"), lax.axis_index("head")
+        self.far, self.near = flip(self.head, 2), flip(self.head, 1)
+        self.copies = {}
+
+    def index(self, at):
+        return at[0] * (self.local // self.piece) + at[1] // self.piece
+
+    def block(self, block, at):
+        m, r = at
+        return self.part.at[m, pl.ds(pl.multiple_of(block * self.local + r, 16), self.piece), :]
+
+    def start(self, at):
+        i = self.index(at)
+        for kind, block in ((0, flip(self.near, 2)), (1, self.near)):
+            c = remote(
+                self.block(block, at), self.nearby.at[kind, i], self.send.at[kind, i], self.recv.at[kind, i], self.seq, self.near
+            )
+            c.start()
+            self.copies[kind, at] = c
+
+    def forward(self, at):
+        i = self.index(at)
+        self.copies[0, at].wait_recv()
+        total = self.block(self.far, at)[...].astype(F32) + self.nearby[0, i].astype(F32)
+        self.stage[i] = total.astype(BF16)
+        c = remote(self.stage.at[i], self.faraway.at[i], self.send.at[2, i], self.recv.at[2, i], self.seq, self.far)
+        c.start()
+        self.copies[2, at] = c
+
+    def total(self, at):
+        i = self.index(at)
+        self.copies[1, at].wait_recv()
+        self.copies[2, at].wait_recv()
+        near = self.block(self.head, at)[...].astype(F32) + self.nearby[1, i].astype(F32)
+        return near + self.faraway[i].astype(F32)
+
+    def finish(self):
+        for c in self.copies.values():
+            c.wait_send()
+
+
+def scatter_scratch(count, local, width, piece):
+    n = count * local // piece
+    return [
+        pltpu.VMEM((2, n, piece, width), BF16),
+        pltpu.VMEM((n, piece, width), BF16),
+        pltpu.VMEM((n, piece, width), BF16),
+        pltpu.SemaphoreType.DMA((3, n)),
+        pltpu.SemaphoreType.DMA((3, n)),
+    ]
+
+
+def gather_scratch(count, local, piece):
+    n = count * local // piece
+    return [pltpu.SemaphoreType.DMA((3, n)), pltpu.SemaphoreType.DMA((3, n))]
+
+
+def vmem_specs(count):
+    return [pl.BlockSpec(memory_space=pltpu.VMEM)] * count
+
+
+def comm_params(collective):
+    return pltpu.CompilerParams(
+        collective_id=collective, has_side_effects=True, vmem_limit_bytes=VMEM_LIMIT
+    )
+
+
+PIECE = 64
+
+
+def norm_gather_body(heads, shards, x_ref, gain_ref, out_ref, send, recv, halo_send, halo_recv):
+    count, local, _ = x_ref.shape
+    seq, head = lax.axis_index("seq"), lax.axis_index("head")
+    after = lax.rem(seq + 1, shards)
+    before = lax.rem(seq + shards - 1, shards)
+    last = head == heads - 1
+    gather = HeadGather(out_ref, local, HALO, send, recv, PIECE)
+    for m, r in pieces_of(count, local, PIECE):
+        x = x_ref[m, pl.ds(r, PIECE), :].astype(F32)
+        out_ref[m, gather.rows(head, r), :] = rms(x, gain_ref[...]).astype(BF16)
+    greet(
+        [(seq, gather.far), (seq, gather.near), (before, heads - 1)],
+        2 + heads * last.astype(jnp.int32),
+    )
+    for at in pieces_of(count, local, PIECE):
+        gather.own(at)
+
+    def halo(target):
+        src = out_ref.at[:, pl.ds(heads * local, HALO), :]
+        return remote(src, out_ref.at[:, pl.ds(0, HALO), :], halo_send.at[target], halo_recv, after, target)
+
+    @pl.when(last)
+    def _():
+        for target in range(heads):
+            halo(target).start()
+
+    for at in pieces_of(count, local, PIECE):
+        gather.forward(at)
+    gather.finish()
+    halo(0).wait_recv()
+
+    @pl.when(last)
+    def _():
+        for target in range(heads):
+            halo(target).wait_send()
+
+
+def norm_gather(inputs, gain, heads, shards):
+    count, local, width = inputs.shape
+    return pl.pallas_call(
+        functools.partial(norm_gather_body, heads, shards),
+        in_specs=vmem_specs(2),
+        out_specs=vmem_specs(1)[0],
+        out_shape=jax.ShapeDtypeStruct((count, HALO + heads * local, width), BF16),
+        scratch_shapes=gather_scratch(count, local, PIECE)
+        + [pltpu.SemaphoreType.DMA((heads,)), pltpu.SemaphoreType.DMA],
+        compiler_params=comm_params(0),
+        name="norm_gather",
+    )(inputs, gain)
+
+
+def resid_gather_body(part_ref, x_ref, gain_ref, resid_ref, out_ref, near_ref, stage_ref, far_ref, ss, sr, gs, gr):
+    count, local, _ = x_ref.shape
+    scatter = HeadScatter(part_ref, local, near_ref, stage_ref, far_ref, ss, sr, PIECE)
+    gather = HeadGather(out_ref, local, 0, gs, gr, PIECE)
+    greet([(gather.seq, gather.far), (gather.seq, gather.near)], 2)
+    order = pieces_of(count, local, PIECE)
+    for at in order:
+        scatter.start(at)
+    for at in order:
+        scatter.forward(at)
+    for at in order:
+        m, r = at
+        resid = x_ref[m, pl.ds(r, PIECE), :].astype(F32) + scatter.total(at)
+        resid_ref[m, pl.ds(r, PIECE), :] = resid
+        out_ref[m, gather.rows(gather.head, r), :] = rms(resid, gain_ref[...]).astype(BF16)
+        gather.own(at)
+    for at in order:
+        gather.forward(at)
+    gather.finish()
+    scatter.finish()
+
+
+def resid_gather(part, inputs, gain):
+    count, local, width = inputs.shape
+    return pl.pallas_call(
+        resid_gather_body,
+        in_specs=vmem_specs(3),
+        out_specs=vmem_specs(2),
+        out_shape=[jax.ShapeDtypeStruct(inputs.shape, F32), jax.ShapeDtypeStruct(part.shape, BF16)],
+        scratch_shapes=scatter_scratch(count, local, width, PIECE) + gather_scratch(count, local, PIECE),
+        compiler_params=comm_params(1),
+        name="resid_gather",
+    )(part, inputs, gain)
+
+
+def grad_gather_body(
+    part_ref, resid_ref, top_ref, gain_ref, mid_ref, out_ref, gain_grad_ref, near_ref, stage_ref, far_ref, ss, sr, gs, gr
+):
+    count, local, width = resid_ref.shape
+    scatter = HeadScatter(part_ref, local, near_ref, stage_ref, far_ref, ss, sr, PIECE)
+    gather = HeadGather(out_ref, local, 0, gs, gr, PIECE)
+    greet([(gather.seq, gather.far), (gather.seq, gather.near)], 2)
+    order = pieces_of(count, local, PIECE)
+    for at in order:
+        scatter.start(at)
+    for at in order:
+        scatter.forward(at)
+    gain_grad = jnp.zeros((1, width), F32)
+    for at in order:
+        m, r = at
+        grad, gain_part = rms_back(scatter.total(at), resid_ref[m, pl.ds(r, PIECE), :], gain_ref[...])
+        mid = top_ref[m, pl.ds(r, PIECE), :].astype(F32) + grad
+        gain_grad += gain_part
+        mid_ref[m, pl.ds(r, PIECE), :] = mid
+        out_ref[m, gather.rows(gather.head, r), :] = mid.astype(BF16)
+        gather.own(at)
+    gain_grad_ref[...] = gain_grad
+    for at in order:
+        gather.forward(at)
+    gather.finish()
+    scatter.finish()
+
+
+def grad_gather(part, resid, grad_top, gain):
+    count, local, width = resid.shape
+    return pl.pallas_call(
+        grad_gather_body,
+        in_specs=vmem_specs(4),
+        out_specs=vmem_specs(3),
+        out_shape=[
+            jax.ShapeDtypeStruct(resid.shape, F32),
+            jax.ShapeDtypeStruct(part.shape, BF16),
+            jax.ShapeDtypeStruct((1, width), F32),
+        ],
+        scratch_shapes=scatter_scratch(count, local, width, PIECE) + gather_scratch(count, local, PIECE),
+        compiler_params=comm_params(2),
+        name="grad_gather",
+    )(part, resid, grad_top, gain)
+
+
+def last_scatter_body(part_ref, x_ref, mid_ref, gain_ref, out_ref, gain_grad_ref, near_ref, stage_ref, far_ref, ss, sr):
+    count, local, width = x_ref.shape
+    scatter = HeadScatter(part_ref, local, near_ref, stage_ref, far_ref, ss, sr, PIECE)
+    greet([(scatter.seq, scatter.far), (scatter.seq, scatter.near)], 2)
+    order = pieces_of(count, local, PIECE)
+    for at in order:
+        scatter.start(at)
+    for at in order:
+        scatter.forward(at)
+    gain_grad = jnp.zeros((1, width), F32)
+    for at in order:
+        m, r = at
+        here = pl.ds(r, PIECE)
+        grad, gain_part = rms_back(scatter.total(at), x_ref[m, here, :].astype(F32), gain_ref[...])
+        gain_grad += gain_part
+        out_ref[m, here, :] = mid_ref[m, here, :] + grad
+    gain_grad_ref[...] = gain_grad
+    scatter.finish()
+
+
+def last_scatter(part, inputs, mid, gain):
+    count, local, width = inputs.shape
+    return pl.pallas_call(
+        last_scatter_body,
+        in_specs=vmem_specs(4),
+        out_specs=vmem_specs(2),
+        out_shape=[jax.ShapeDtypeStruct(inputs.shape, F32), jax.ShapeDtypeStruct((1, width), F32)],
+        scratch_shapes=scatter_scratch(count, local, width, PIECE),
+        compiler_params=comm_params(3),
+        name="last_scatter",
+    )(part, inputs, mid, gain)
+
+
+def compose_body(shards, backward, trans_ref, state_ref, out_ref, stage_ref, got_ref, tx_ref, t_ref, s_ref, send, recv):
+    groups = trans_ref.shape[0]
+    seq, head = lax.axis_index("seq"), lax.axis_index("head")
+    place = shards - 1 - seq if backward else seq
+    steps = [1 << k for k in range((shards - 1).bit_length())]
+
+    def peer(distance):
+        return lax.rem(seq + shards + distance, shards)
+
+    sign = -1 if backward else 1
+    greet([(peer(-sign * d), head) for d in steps], len(steps))
+
+    def apply(trans, state):
+        return mm(trans, state, 0, 0) if backward else mm(trans, state)
+
+    def join(late, early):
+        return mm(early, late) if backward else mm(late, early)
+
+    for k, d in enumerate(steps):
+        final = k == len(steps) - 1
+        copies = []
+        for part in range(1 if final else 2):
+            if k == 0:
+                src = state_ref if part == 0 else trans_ref
+            else:
+                src = stage_ref.at[k - 1, part]
+            copies.append(
+                remote(src, got_ref.at[k, part], send.at[k, part], recv.at[k, part], peer(sign * d), head)
+            )
+        for c in copies:
+            c.start()
+        for c in copies:
+            c.wait_recv()
+        here = (place >= d).astype(F32)
+
+        @pl.loop(0, groups)
+        def _(g, k=k, final=final, here=here):
+            state = got_ref[k, 0, g].astype(F32) * here
+            if k == 0:
+                out_ref[g] = state
+            else:
+                out_ref[g] += apply(tx_ref[g], state)
+            if not final:
+                trans = got_ref[k, 1, g].astype(F32) * here
+                if k == 0:
+                    old_t, old_s = trans_ref[g].astype(F32), state_ref[g].astype(F32)
+                    tx_ref[g] = trans.astype(BF16)
+                else:
+                    old_t, old_s = t_ref[g], s_ref[g]
+                    tx_ref[g] = join(tx_ref[g], trans).astype(BF16)
+                new_s = old_s + apply(old_t, state)
+                new_t = join(old_t, trans)
+                s_ref[g] = new_s
+                t_ref[g] = new_t
+                stage_ref[k, 0, g] = new_s.astype(BF16)
+                stage_ref[k, 1, g] = new_t.astype(BF16)
+
+        for c in copies:
+            c.wait_send()
+
+
+def compose(trans, state, shards, backward):
+    count, heads = state.shape[:2]
+    groups = count * heads
+    flat = (groups, HEAD_DIM, HEAD_DIM)
+    rounds = (shards - 1).bit_length()
+    out = pl.pallas_call(
+        functools.partial(compose_body, shards, backward),
+        in_specs=vmem_specs(2),
+        out_specs=vmem_specs(1)[0],
+        out_shape=jax.ShapeDtypeStruct(flat, F32),
+        scratch_shapes=[
+            pltpu.VMEM((max(rounds - 1, 1), 2) + flat, BF16),
+            pltpu.VMEM((rounds, 2) + flat, BF16),
+            pltpu.VMEM(flat, BF16),
+            pltpu.VMEM(flat, F32),
+            pltpu.VMEM(flat, F32),
+            pltpu.SemaphoreType.DMA((rounds, 2)),
+            pltpu.SemaphoreType.DMA((rounds, 2)),
+        ],
+        compiler_params=comm_params(5 if backward else 4),
+        name="compose_back" if backward else "compose",
+    )(trans.reshape(flat), state.reshape(flat))
+    return out.reshape(state.shape)
 
 
 def per_device(
@@ -619,59 +985,48 @@
     seq_offsets, seq_lengths, out_grad,
 ):
     count, local_rows, width = inputs.shape
-    rows = local_rows * lax.axis_size("head")
+    heads, shards = lax.axis_size("head"), lax.axis_size("seq")
+    rows = local_rows * heads
     base = (lax.axis_index("seq") * rows).astype(jnp.int32).reshape(1)
     taps = filter_weights.astype(F32)
     gain_row = out_gain.reshape(1, HEAD_DIM)
+    attn_row = attn_gain.reshape(1, width)
+    dense_row = dense_gain.reshape(1, width)
     dense_full = lax.all_gather(dense_weights, "seq", axis=1, tiled=True)
     grad_top = lax.all_gather(out_grad, "head", axis=1, tiled=True)
 
-    resid_in = inputs.astype(F32)
-    normed_local = rms(resid_in, attn_gain).astype(BF16)
-    gathered = lax.all_gather(normed_local, "head", axis=1, tiled=True)
-    halo = shifted(gathered[:, rows - HALO :, :], "seq", 1)
-    x_ext = jnp.concatenate([halo, gathered], axis=1)
-    pq, pk, pv, rates, ps, oloc, phi, psi, score, inv, wr, up, pair = mix_fwd(
+    x_ext = norm_gather(inputs, attn_row, heads, shards)
+    pq, pk, pv, rates, ps, oloc, phi, psi, score, inv, wr, up, trans, state = mix_fwd(
         seq_offsets, seq_lengths, base, x_ext, mixer_weights, beta_weight, taps
     )
-    state_in = compose(pair, "seq", False)
+    state_in = compose(trans, state, shards, False)
     start, mixed, head_out, attn_part = mix_out(state_in, ps, oloc, phi, psi, gain_row, mixer_weights)
-    attn = lax.psum_scatter(attn_part, "head", scatter_dimension=1, tiled=True).astype(F32)
-    resid_mid = resid_in + attn
-    dense_in = lax.all_gather(rms(resid_mid, dense_gain).astype(BF16), "head", axis=1, tiled=True)
+    resid_mid, dense_in = resid_gather(attn_part, inputs, dense_row)
     down_part, gin_part, dense_part = dense(
         dense_in.reshape(-1, width), grad_top.reshape(-1, width), dense_full
     )
-    gin = lax.psum_scatter(
-        gin_part.reshape(count, rows, width), "head", scatter_dimension=1, tiled=True
-    ).astype(F32)
     down = lax.psum_scatter(
         down_part.reshape(count, rows, width), "head", scatter_dimension=1, tiled=True
     ).astype(F32)
     dense_total = lax.psum_scatter(dense_part, "seq", scatter_dimension=1, tiled=True).astype(F32)
     output = (resid_mid + down).astype(BF16)
-    grad_norm, dense_gain_part = rms_back(gin, resid_mid, dense_gain)
-    grad_mid = out_grad.astype(F32) + grad_norm
-    grad_attn = lax.all_gather(grad_mid.astype(BF16), "head", axis=1, tiled=True)
+    grad_mid, grad_attn, dense_gain_part = grad_gather(
+        gin_part.reshape(count, rows, width), resid_mid, out_grad, dense_row
+    )
     dout, out_gain_part, dstate = mix_back(grad_attn, mixer_weights, mixed, gain_row, ps, phi)
-    dpair = jnp.stack([jnp.swapaxes(pair[0], 2, 3), dstate])
-    dend = compose(dpair, "seq", True)
+    dend = compose(trans, dstate, shards, True)
     gq, gk, gv, tail, rim, grate, filter_part = mix_grad(
         seq_offsets, seq_lengths, base, (pq, pk, pv), rates, taps, dend, dout, start, ps, phi, score, inv, wr, up
     )
     rim_next = shifted(rim, "seq", -1)
-    last_shard = lax.axis_index("seq") == lax.axis_size("seq") - 1
-    rim_next = jnp.where(last_shard, 0.0, rim_next)
     gx_part, mixer_part, beta_part = proj_back(
         (gq, gk, gv), tail, rim_next, grate, x_ext, mixer_weights, beta_weight, grad_attn, head_out
     )
-    gx = lax.psum_scatter(gx_part, "head", scatter_dimension=1, tiled=True).astype(F32)
-    grad_in_norm, attn_gain_part = rms_back(gx, resid_in, attn_gain)
-    input_grad = grad_mid + grad_in_norm
-    mixer_total = lax.psum(mixer_part.astype(F32), "seq")
+    input_grad, attn_gain_part = last_scatter(gx_part, inputs, grad_mid, attn_row)
+    mixer_total = lax.psum(mixer_part, "seq").astype(F32)
     beta_total, filter_total = lax.psum((beta_part, filter_part), "seq")
     attn_gain_total, out_gain_total, dense_gain_total = lax.psum(
-        (attn_gain_part, out_gain_part.reshape(HEAD_DIM), dense_gain_part), ("seq", "head")
+        (attn_gain_part.reshape(width), out_gain_part.reshape(HEAD_DIM), dense_gain_part.reshape(width)), ("seq", "head")
     )
     return (
         output, input_grad, attn_gain_total, mixer_total, beta_total, filter_total, out_gain_total,

time: 768 us -> 520 us (0.68)
  waiting for transfers between devices: 401 us -> 134 us
  Pallas kernels: 85.3 us -> 268 us
  blocking collectives: 228 us -> 86.8 us
  other arithmetic: 17.6 us -> 6.56 us
  matrix products: 8.04 us -> 0 us
    pallas_call x0 -> x6, Pallas kernels: none -> 183 us  [the longest x2 75.2 us: compose(): pl.pallas_call(functools.partial(compose_body, shards, backward), in_spec...]
    all_gather x5 -> x0, waiting for transfers between devices: 166 us -> none  [the longest x2 95.5 us: compose(): gathered = lax.all_gather(pair, axis)]
    psum x2, blocking collectives: 228 us -> 86.8 us  [the longest x1 47.7 us: per_device(): beta_total, filter_total = lax.psum((beta_part, filter_part), 'seq')]
    all_gather x1, waiting for transfers between devices: 82.8 us -> 0.02 us  [per_device(): dense_full = lax.all_gather(dense_weights, 'seq', axis=1, tiled=True)]
    reduce_scatter x3 -> x0, waiting for transfers between devices: 67.9 us -> none  [the longest x1 36.4 us: per_device(): lax.psum_scatter(attn_part, 'head', scatter_dimension=1, tiled=True)]
    reduce_scatter x1, waiting for transfers between devices: 53.2 us -> 97.2 us  [per_device(): lax.psum_scatter(dense_part, 'seq', scatter_dimension=1, tiled=True)]
    reduce_scatter x1, waiting for transfers between devices: 0.01 us -> 29.6 us  [per_device(): lax.psum_scatter(down_part.reshape(count, rows, width), 'head', scatter_d...]
    all_gather x1, waiting for transfers between devices: 20.5 us -> 0.02 us  [per_device(): grad_top = lax.all_gather(out_grad, 'head', axis=1, tiled=True)]
  transfers between devices with their start and end apart: 14 -> 6, of which waited for: 12 -> 4; matrix products, arithmetic and copies ran while one was open for 3% -> 2% of each run, Pallas kernels for 4% -> 29%
where the time goes in v2:
time: 520 us
  Pallas kernels  268 us (52%)
  waiting for transfers between devices  134 us (26%)
  blocking collectives  86.8 us (17%)
  between operations  14 us (3%)
  local copies, waits for them, and re-layouts  7.76 us (1%)
  other arithmetic  6.56 us (1%)
    reduce_scatter x1, waiting for transfers between devices, per_device(): lax.psum_scatter(dense_part, 'seq', scatter_dimension=1, tiled=True)  97.2 us
    pallas_call x2, Pallas kernels, compose(): pl.pallas_call(functools.partial(compose_body, shards, backward), in_spec...  75.2 us
    psum x1, blocking collectives, per_device(): beta_total, filter_total = lax.psum((beta_part, filter_part), 'seq')  47.7 us
    psum x1, blocking collectives, per_device(): lax.psum((attn_gain_part.reshape(width), out_gain_part.reshape(HEAD_DIM),...  39.2 us
    pallas_call x1, Pallas kernels, grad_gather(): pl.pallas_call(grad_gather_body, in_specs=vmem_specs(4), out_specs=vmem_s...  31.8 us
    pallas_call x1, Pallas kernels, resid_gather(): pl.pallas_call(resid_gather_body, in_specs=vmem_specs(3), out_specs=vmem_...  30.8 us
    reduce_scatter x1, waiting for transfers between devices, per_device(): lax.psum_scatter(down_part.reshape(count, rows, width), 'head', scatter_d...  29.6 us
    pallas_call x1, Pallas kernels, norm_gather(): pl.pallas_call(functools.partial(norm_gather_body, heads, shards), in_spe...  27 us
  transfers between devices with their start and end apart: 6, of which 4 were waited for; matrix products, arithmetic and copies ran while one was open for 2% of the time, Pallas kernels for 29%

profile of v2, /device:TPU:0, one launch (start us, length us, event | category | flops | bytes accessed | tf_op | source)
XLA Modules:
  0.0 519.9 jit_solution(11393634111756794567)
XLA Ops:
  8.0 2.2 copy.21
  11.7 27.0 %norm_gather.1.x_ref = bf16[2,528,1024]{2,1,0:T(8,128)(2,1)} custom-call(bf16[2,128,1024]{2,1,0:T(8,128)(2,1)} %x_ref.5, f32[1,1024]{1,0:T(1,128)} %bitcast.28), custom_call_target="tpu_custom_call" | custom-call | tf_op jit(solution)/shard_map/norm_gather/pallas_call | solution.py:772
  38.7 23.4 %mix_fwd.1 = (bf16[2,528,256]{2,1,0:T(8,128)(2,1)}, bf16[2,528,256]{2,1,0:T(8,128)(2,1)}, bf16[2,528,256]{2,1,0:T(8,128)(2,1)}, f32[2,2,512,1]{3,2,1,0:T(8,128)}...) custom-call(s32[2,3]{1,0:T(2,128)} %off_ref.3, ...), custom_call_target="tpu_custom_call" | custom-call | tf_op jit(solution)/shard_map/mix_fwd/pallas_call | solution.py:193
  62.1 44.5 %compose.1 = f32[4,128,128]{2,1,0:T(8,128)} custom-call(bf16[4,128,128]{2,1,0:T(8,128)(2,1)} %bitcast.22, bf16[4,128,128]{2,1,0:T(8,128)(2,1)} %bitcast.24), custom_call_target="tpu_custom_call" | custom-call | tf_op jit(solution)/shard_map/compose/pallas_call | solution.py:963
  106.7 5.3 %mix_out.1 = (bf16[2,2,512,128]{3,2,1,0:T(8,128)(2,1)}, f32[2,2,512,128]{3,2,1,0:T(8,128)}, bf16[2,512,256]{2,1,0:T(8,128)(2,1)}, bf16[2,512,1024]{2,1,0:T(8,128)(2,1)}) custom-call(f32[2,2,128,128]{3,2,1,0:T(8,128)} %bitcast.21, bf16[2,2,512,128]{3,2,1,0:T(8,128)(2,1)} %get-tuple-element.52.ps_ref, f32[2,2,512,128]{3,2,1,0:T(8,128)} %get-tuple-element.53.oloc_ref, ...), custom_call_target="tpu_custom_call" | custom-call | tf_op jit(solution)/shard_map/mix_out/pallas_call | solution.py:239
  112.0 30.8 %resid_gather.1 = (f32[2,128,1024]{2,1,0:T(8,128)}, bf16[2,512,1024]{2,1,0:T(8,128)(2,1)}) custom-call(bf16[2,512,1024]{2,1,0:T(8,128)(2,1)} %get-tuple-element.56.part_ref, bf16[2,128,1024]{2,1,0:T(8,128)(2,1)} %x_ref.5, f32[1,1024]{1,0:T(1,128)} %bitcast.26), custom_call_target="tpu_custom_call" | custom-call | tf_op jit(solution)/shard_map/resid_gather/pallas_call | solution.py:808
  142.9 22.0 %dense.1 = (bf16[1024,1024]{1,0:T(8,128)(2,1)}, bf16[1024,1024]{1,0:T(8,128)(2,1)}, bf16[3,1024,704]{2,1,0:T(8,128)(2,1)}) custom-call(bf16[1024,1024]{1,0:T(8,128)(2,1)} %bitcast.17, bf16[1024,1024]{1,0:T(8,128)(2,1)} %bitcast.16, bf16[3,1024,704]{2,1,0:T(8,128)(2,1)} %all-gather.5.cloned.1.call-done.w_ref), custom_call_target="tpu_custom_call" | custom-call | tf_op jit(solution)/shard_map/dense/pallas_call | solution.py:302
  164.9 31.8 %grad_gather.1 = (f32[2,128,1024]{2,1,0:T(8,128)}, bf16[2,512,1024]{2,1,0:T(8,128)(2,1)}, f32[1,1024]{1,0:T(1,128)}) custom-call(bf16[2,512,1024]{2,1,0:T(8,128)(2,1)} %bitcast.19, f32[2,128,1024]{2,1,0:T(8,128)} %get-tuple-element.57.resid_ref, bf16[2,128,1024]{2,1,0:T(8,128)(2,1)} %top_ref.1, f32[1,1024]{1,0:T(1,128)} %bitcast.27), custom_call_target="tpu_custom_call" | custom-call | tf_op jit(solution)/shard_map/grad_gather/pallas_call | solution.py:849
  196.7 5.7 %mix_back.1 = (bf16[2,2,512,128]{3,2,1,0:T(8,128)(2,1)}, f32[1,128]{1,0:T(1,128)}, bf16[2,2,128,128]{3,2,1,0:T(8,128)(2,1)}) custom-call(bf16[2,512,1024]{2,1,0:T(8,128)(2,1)} %get-tuple-element.65.grad_ref.gattn_ref, bf16[4,1024,256]{2,1,0:T(8,128)(2,1)} %w_ref.7, f32[2,2,512,128]{3,2,1,0:T(8,128)} %get-tuple-element.66.mixed_ref, f32[1,128]{1,0:T(1,128)} %bitcast.33, ...), custom_call_target="tpu_custom_call" | custom-call | tf_op jit(solution)/shard_map/mix_back/pallas_call | solution.py:360
  202.4 30.7 %compose_back.1 = f32[4,128,128]{2,1,0:T(8,128)} custom-call(bf16[4,128,128]{2,1,0:T(8,128)(2,1)} %bitcast.23, bf16[4,128,128]{2,1,0:T(8,128)(2,1)} %bitcast.25), custom_call_target="tpu_custom_call" | custom-call | tf_op jit(solution)/shard_map/compose_back/pallas_call | solution.py:963
  233.1 17.4 %mix_grad.1 = (bf16[2,512,256]{2,1,0:T(8,128)(2,1)}, bf16[2,512,256]{2,1,0:T(8,128)(2,1)}, bf16[2,512,256]{2,1,0:T(8,128)(2,1)}, f32[2,3,8,256]{3,2,1,0:T(8,128)...) custom-call(s32[2,3]{1,0:T(2,128)} %off_ref.3, s32[2,3]{1,0:T(2,128)} %len_ref.3, ...), custom_call_target="tpu_custom_call" | custom-call | tf_op jit(solution)/shard_map/mix_grad/pallas_call | solution.py:489
  250.5 2.1 collective-permute-start
  252.7 3.5 collective-permute-done.rim_ref
  256.8 11.4 %proj_back.1 = (bf16[2,512,1024]{2,1,0:T(8,128)(2,1)}, bf16[4,1024,256]{2,1,0:T(8,128)(2,1)}, f32[1024,2]{1,0:T(8,128)}) custom-call(bf16[2,512,256]{2,1,0:T(8,128)(2,1)} %get-tuple-element.74.gq_ref, bf16[2,512,256]{2,1,0:T(8,128)(2,1)} %get-tuple-element.75.gk_ref, bf16[2,512,256]{2,1,0:T(8,128)(2,1)} %get-tuple-element.76.gv_ref, ...), custom_call_target="tpu_custom_call" | custom-call | tf_op jit(solution)/shard_map/proj_back/pallas_call | solution.py:557
  269.4 18.3 %last_scatter.1 = (f32[2,128,1024]{2,1,0:T(8,128)}, f32[1,1024]{1,0:T(1,128)}) custom-call(bf16[2,512,1024]{2,1,0:T(8,128)(2,1)} %get-tuple-element.81.part_ref, bf16[2,128,1024]{2,1,0:T(8,128)(2,1)} %x_ref.5, f32[2,128,1024]{2,1,0:T(8,128)} %get-tuple-element.82.mid_ref, f32[1,1024]{1,0:T(1,128)} %bitcast.29), custom_call_target="tpu_custom_call" | custom-call | tf_op jit(solution)/shard_map/last_scatter/pallas_call | solution.py:886
  287.7 47.7 %all-reduce.1 = (f32[1024,2]{1,0:T(8,128)S(1)}, f32[3,4,256]{2,1,0:T(4,128)}) all-reduce(f32[1024,2]{1,0:T(8,128)S(1)} %copy-done.2, f32[3,4,256]{2,1,0:T(4,128)S(1)} %copy-done.4), channel_id=1, replica_groups=mesh['seq'=8,'head'=4] {'seq'}, use_global_device_ids=true, to_apply=%region_3.0 | all-reduce | flops 5120 | bytes 40960 | tf_op jit(solution)/shard_map/psum | solution.py:1027
  336.2 39.2 %all-reduce = (f32[1024]{0:T(1024)}, f32[128]{0:T(128)}, f32[1024]{0:T(1024)}) all-reduce(f32[1024]{0:T(1024)} %bitcast.31, f32[128]{0:T(128)S(1)} %bitcast.34, f32[1024]{0:T(1024)S(1)} %bitcast.30), channel_id=1, replica_groups=mesh['seq'=8,'head'=4] {'seq','head'}, use_global_device_ids=true, to_apply=%region_1.0 | all-reduce | flops 2176 | bytes 17408 | tf_op jit(solution)/shard_map/psum | solution.py:1028
  375.3 2.1 all-reduce.4.cloned.1.call-done
  377.4 4.0 convert_element_type.18
  381.4 29.6 %reduce-scatter.3.cloned.1.call-done = bf16[2,128,1024]{2,1,0:T(8,128)(2,1)} async-done(((bf16[2,512,1024]{2,1,0:T(8,128)(2,1)}), bf16[2,128,1024]{2,1,0:T(8,128)(2,1)}) %reduce-scatter.3.cloned.1.call-update) | async-done | bytes 524304 | tf_op jit(solution)/shard_map/reduce_scatter | solution.py:1008
  410.9 2.0 add_convert_fusion
  412.9 97.2 %reduce-scatter.5.cloned.1.call-done = bf16[3,128,704]{2,1,0:T(8,128)(2,1)} async-done(((bf16[3,1024,704]{2,1,0:T(8,128)(2,1)}), bf16[3,128,704]{2,1,0:T(8,128)(2,1)}) %reduce-scatter.5.cloned.1.call-update) | async-done | bytes 540688 | tf_op jit(solution)/shard_map/reduce_scatter | solution.py:1011
  510.2 2.3 copy.24
  512.4 1.0 copy.27
  (33 shorter events, 5.0 us)
Async XLA Ops:
  7.2 3.0 copy-start.5
  7.2 3.6 copy-start.6
  7.2 135.6 %all-gather.3.cloned.1.call-start = ((), (), s32[]{:S(2)}) async-start(), calls=%async_computation.2 | async-start | bytes 2621440 | tf_op jit(solution)/shard_map/all_gather | solution.py:996
  7.9 134.9 %all-gather.5.cloned.1.call-start = ((), (), s32[]{:S(2)}) async-start(), calls=%async_computation.3 | async-start | bytes 5308416 | tf_op jit(solution)/shard_map/all_gather | solution.py:995
  10.2 367.3 %all-reduce.4.cloned.1.call-start = ((), (), s32[]{:S(2)}) async-start(), calls=%async_computation.5 | async-start | bytes 4194304 | tf_op jit(solution)/shard_map/psum | solution.py:1026
  250.5 5.6 %collective-permute-start = (f32[2,3,8,256]{3,2,1,0:T(8,128)}, f32[2,3,8,256]{3,2,1,0:T(8,128)S(1)}, u32[]{:S(2)}, u32[]{:S(2)}) collective-permute-start(f32[2,3,8,256]{3,2,1,0:T(8,128)} %get-tuple-element.78), channel_id=1, source_target_pairs={{0,28},{4,0},{8,4},{12,8},{16,12},{20,16},{24,20},{28,24},{1,29},{... | collective-permute-start | bytes 147464 | tf_op jit(solution)/shard_map/ppermute | solution.py:586
  256.1 0.6 copy-start.3
  268.2 142.8 %reduce-scatter.3.cloned.1.call-start = ((), (), s32[]{:S(2)}) async-start(), calls=%async_computation.4 | async-start | bytes 2621440 | tf_op jit(solution)/shard_map/reduce_scatter | solution.py:1008
  268.7 241.4 %reduce-scatter.5.cloned.1.call-start = ((), (), s32[]{:S(2)}) async-start(), calls=%async_computation.6 | async-start | bytes 5308416 | tf_op jit(solution)/shard_map/reduce_scatter | solution.py:1011
  269.3 18.3 %copy-start.2 = (f32[1024,2]{1,0:T(8,128)S(1)}, f32[1024,2]{1,0:T(8,128)}, u32[]{:S(2)}) copy-start(f32[1024,2]{1,0:T(8,128)} %get-tuple-element.86) | copy-start | bytes 24580
  269.3 18.3 %copy-start.4 = (f32[3,4,256]{2,1,0:T(4,128)S(1)}, f32[3,4,256]{2,1,0:T(4,128)}, u32[]{:S(2)}) copy-start(f32[3,4,256]{2,1,0:T(4,128)} %get-tuple-element.87) | copy-start | bytes 36868
  269.3 66.8 %copy-start.7 = (f32[1,1024]{1,0:T(1,128)S(1)}, f32[1,1024]{1,0:T(1,128)}, u32[]{:S(2)}) copy-start(f32[1,1024]{1,0:T(1,128)} %get-tuple-element.89) | copy-start | bytes 12292
  269.4 66.8 %copy-start.8 = (f32[1,128]{1,0:T(1,128)S(1)}, f32[1,128]{1,0:T(1,128)}, u32[]{:S(2)}) copy-start(f32[1,128]{1,0:T(1,128)} %get-tuple-element.88) | copy-start | bytes 1540
  375.3 35.6 %copy-start = (f32[2,128,1024]{2,1,0:T(8,128)S(1)}, f32[2,128,1024]{2,1,0:T(8,128)}, u32[]{:S(2)}) copy-start(f32[2,128,1024]{2,1,0:T(8,128)} %get-tuple-element.57.resid_ref) | copy-start | bytes 3145732
  381.4 131.1 %copy-start.1 = (f32[2,128,1024]{2,1,0:T(8,128)S(1)}, f32[2,128,1024]{2,1,0:T(8,128)}, u32[]{:S(2)}) copy-start(f32[2,128,1024]{2,1,0:T(8,128)} %get-tuple-element.115) | copy-start | bytes 3145732
Sparse Core Ops, SparseCore 0:
  9.6 33.2 all-gather.2
  45.1 90.9 all-gather.4
  268.3 109.0 all-reduce.3
  379.8 31.1 reduce-scatter.2
  414.9 95.2 reduce-scatter.4

commit v3 on v1

--- a/solution.py
+++ b/solution.py
@@ -106,7 +106,7 @@
 
 def mix_fwd_body(
     off_ref, len_ref, base_ref, x_ref, w_ref, beta_ref, taps_ref,
-    pq_ref, pk_ref, pv_ref, rate_ref, ps_ref, oloc_ref, phi_ref, psi_ref, m_ref, inv_ref, wr_ref, up_ref, ts_ref,
+    pq_ref, pk_ref, pv_ref, rate_ref, ps_ref, oloc_ref, phi_ref, psi_ref, m_ref, inv_ref, wr_ref, up_ref, trans_ref, state_ref,
 ):
     mb = pl.program_id(0)
     head = pl.program_id(1)
@@ -118,12 +118,12 @@
     for member, out in enumerate((pq_ref, pk_ref, pv_ref)):
         proj = mm(x, w_ref[member]).astype(BF16)
         out[0] = proj
-        filt = filtered(proj.astype(F32), taps_ref[member], masks, rows)
+        filt = filtered(proj.astype(F32), taps_ref[member].astype(F32), masks, rows)
         acts.append(filt * sigmoid(filt))
     query, key, value = acts
     query = query * lax.rsqrt(jnp.sum(query * query, axis=-1, keepdims=True) + EPS)
     key = key * lax.rsqrt(jnp.sum(key * key, axis=-1, keepdims=True) + EPS)
-    raw_all = mm(x, beta_ref[...])[HALO:]
+    raw_all = mm(x, beta_ref[...], 1, 1)[HALO:]
     lane = lax.broadcasted_iota(jnp.int32, raw_all.shape, 1)
     raw = jnp.sum(jnp.where(lane == head, raw_all, 0.0), axis=-1, keepdims=True)
     rate_ref[0, 0] = raw
@@ -165,8 +165,12 @@
         both = mm3(phi, jnp.concatenate([trans, state], axis=1))
         trans = both[:, :HEAD_DIM]
         state = both[:, HEAD_DIM:] + psi
-    ts_ref[0, 0, 0] = trans.astype(BF16)
-    ts_ref[1, 0, 0] = state.astype(BF16)
+    trans_ref[0, 0] = trans.astype(BF16)
+    state_ref[0, 0] = state.astype(BF16)
+
+
+def cost(us):
+    return pl.CostEstimate(flops=0, bytes_accessed=int(us * 3.0e6), transcendentals=0)
 
 
 def smem_spec():
@@ -182,7 +186,7 @@
 def mix_fwd(offsets, lengths, base, x_ext, mixer_weights, beta_weight, taps):
     count, ext_rows, width = x_ext.shape
     rows = ext_rows - HALO
-    heads = beta_weight.shape[1]
+    heads = beta_weight.shape[0]
     per_head = pl.BlockSpec((1, 1, rows, HEAD_DIM), lambda m, h: (m, h, 0, 0))
     proj_spec = pl.BlockSpec((1, ext_rows, HEAD_DIM), lambda m, h: (m, 0, h))
     proj_shape = jax.ShapeDtypeStruct((count, ext_rows, heads * HEAD_DIM), BF16)
@@ -203,12 +207,13 @@
         out_specs=[proj_spec] * 3
         + [pl.BlockSpec((1, 1, rows, 1), lambda m, h: (m, h, 0, 0))]
         + [per_head] * 8
-        + [pl.BlockSpec((2, 1, 1, HEAD_DIM, HEAD_DIM), lambda m, h: (0, m, h, 0, 0))],
+        + [pl.BlockSpec((1, 1, HEAD_DIM, HEAD_DIM), lambda m, h: (m, h, 0, 0))] * 2,
         out_shape=[proj_shape] * 3
         + [jax.ShapeDtypeStruct((count, heads, rows, 1), F32)]
         + [big(BF16), big(F32), big(F32), big(F32), big(BF16), big(BF16), big(BF16), big(F32)]
-        + [jax.ShapeDtypeStruct((2, count, heads, HEAD_DIM, HEAD_DIM), BF16)],
+        + [jax.ShapeDtypeStruct((count, heads, HEAD_DIM, HEAD_DIM), BF16)] * 2,
         compiler_params=params(2),
+        cost_estimate=cost(23),
         name="mix_fwd",
     )(offsets, lengths, base, x_ext, mixer_weights, beta_weight, taps)
 
@@ -257,62 +262,9 @@
             jax.ShapeDtypeStruct((count, rows, width), BF16),
         ],
         compiler_params=params(1),
+        cost_estimate=cost(5),
         name="mix_out",
     )(state_in, ps, oloc, phi, psi, out_gain, mixer_weights)
-
-
-def dense_body(x_ref, g_ref, w_ref, down_ref, gin_ref, grad_ref, acc_ref):
-    step = pl.program_id(0)
-    x = x_ref[...]
-    g = g_ref[...]
-    gate = mm(x, w_ref[0])
-    up = mm(x, w_ref[1])
-    grad_hidden = mm(g, w_ref[2])
-    sg = sigmoid(gate)
-    silu = gate * sg
-    hidden = (silu * up).astype(BF16)
-    grad_gate = (grad_hidden * up * (sg * (1.0 + gate * (1.0 - sg)))).astype(BF16)
-    grad_up = (grad_hidden * silu).astype(BF16)
-    down_ref[...] = mm(hidden, w_ref[2], 1, 1).astype(BF16)
-    gin_ref[...] = (mm(grad_gate, w_ref[0], 1, 1) + mm(grad_up, w_ref[1], 1, 1)).astype(BF16)
-
-    @pl.when(step == 0)
-    def _():
-        acc_ref[0] = mm(x, grad_gate, 0, 0)
-        acc_ref[1] = mm(x, grad_up, 0, 0)
-        acc_ref[2] = mm(g, hidden, 0, 0)
-
-    @pl.when(step > 0)
-    def _():
-        acc_ref[0] += mm(x, grad_gate, 0, 0)
-        acc_ref[1] += mm(x, grad_up, 0, 0)
-        acc_ref[2] += mm(g, hidden, 0, 0)
-
-    @pl.when(step == pl.num_programs(0) - 1)
-    def _():
-        grad_ref[...] = acc_ref[...].astype(BF16)
-
-
-def dense(dense_in, grad_top, weights):
-    rows, width = dense_in.shape
-    hidden = weights.shape[2]
-    tile = 256
-    row_spec = pl.BlockSpec((tile, width), lambda i: (i, 0))
-    whole = pl.BlockSpec((3, width, hidden), lambda i: (0, 0, 0), pipeline_mode=pl.Buffered(1))
-    return pl.pallas_call(
-        dense_body,
-        grid=(rows // tile,),
-        in_specs=[row_spec, row_spec, whole],
-        out_specs=[row_spec, row_spec, whole],
-        out_shape=[
-            jax.ShapeDtypeStruct((rows, width), BF16),
-            jax.ShapeDtypeStruct((rows, width), BF16),
-            jax.ShapeDtypeStruct((3, width, hidden), BF16),
-        ],
-        scratch_shapes=[pltpu.VMEM((3, width, hidden), F32)],
-        compiler_params=params(1),
-        name="dense",
-    )(dense_in, grad_top, weights)
 
 
 def mix_back_body(grad_ref, w_ref, mixed_ref, gain_ref, ps_ref, phi_ref, dout_ref, gain_grad_ref, dstate_ref):
@@ -378,6 +330,7 @@
             jax.ShapeDtypeStruct((count, heads, HEAD_DIM, HEAD_DIM), BF16),
         ],
         compiler_params=params(1),
+        cost_estimate=cost(6),
         name="mix_back",
     )(grad_attn, mixer_weights, mixed, out_gain, ps, phi)
 
@@ -394,7 +347,7 @@
     projs, filts, sigs, acts = [], [], [], []
     for member, ref in enumerate((pq_ref, pk_ref, pv_ref)):
         proj = ref[0].astype(F32)
-        filt = filtered(proj, taps_ref[member], masks, rows)
+        filt = filtered(proj, taps_ref[member].astype(F32), masks, rows)
         sg = sigmoid(filt)
         projs.append(proj)
         filts.append(filt)
@@ -450,7 +403,7 @@
     for member, out in enumerate((gq_ref, gk_ref, gv_ref)):
         sg = sigs[member]
         dfilt = dacts[member] * (sg * (1.0 + filts[member] * (1.0 - sg)))
-        taps = taps_ref[member]
+        taps = taps_ref[member].astype(F32)
         total = None
         pieces = []
         for lag in range(CONV):
@@ -503,6 +456,7 @@
             jax.ShapeDtypeStruct(taps.shape, F32),
         ],
         compiler_params=params(2),
+        cost_estimate=cost(17),
         name="mix_grad",
     )(offsets, lengths, base, *proj3, rates, taps, dend, dout, start, ps, phi, m, inv, wr, up)
 
@@ -519,7 +473,7 @@
     for h in range(heads):
         grate = jnp.where(lane == h, grate_ref[0, h], grate)
     x = x_ref[0, HALO:, :]
-    total = mm(grate, beta_ref[...], 1, 1)
+    total = mm(grate, beta_ref[...])
     adds = []
     for member, ref in enumerate((gq_ref, gk_ref, gv_ref)):
         last = (tail_ref[0, member] + rim_ref[0, member]).astype(BF16)
@@ -528,7 +482,7 @@
         adds.append(mm(x, g, 0, 0))
     adds.append(mm(gattn_ref[0], head_ref[0], 0, 0))
     gx_ref[0] = total.astype(BF16)
-    gb = mm(x, grate, 0, 0)
+    gb = mm(grate, x, 0, 0)
 
     @pl.when(step == 0)
     def _():
@@ -550,7 +504,7 @@
 def proj_back(g3, tail, rim, grate, x_ext, mixer_weights, beta_weight, grad_attn, head_out):
     count, rows, head_width = g3[0].shape
     ext_rows, width = x_ext.shape[1:]
-    heads = beta_weight.shape[1]
+    heads = beta_weight.shape[0]
     g_spec = pl.BlockSpec((1, rows, head_width), lambda m: (m, 0, 0))
     small = pl.BlockSpec((1, 3, RIM, head_width), lambda m: (m, 0, 0, 0))
     row_spec = pl.BlockSpec((1, rows, width), lambda m: (m, 0, 0))
@@ -562,21 +516,22 @@
             pl.BlockSpec((1, heads, rows, 1), lambda m: (m, 0, 0, 0)),
             pl.BlockSpec((1, ext_rows, width), lambda m: (m, 0, 0)),
             pl.BlockSpec((3, width, head_width), lambda m: (0, 0, 0)),
-            pl.BlockSpec((width, heads), lambda m: (0, 0)),
+            pl.BlockSpec((heads, width), lambda m: (0, 0)),
             row_spec, g_spec,
         ],
         out_specs=[
             row_spec,
             pl.BlockSpec((4, width, head_width), lambda m: (0, 0, 0)),
-            pl.BlockSpec((width, heads), lambda m: (0, 0)),
+            pl.BlockSpec((heads, width), lambda m: (0, 0)),
         ],
         out_shape=[
             jax.ShapeDtypeStruct((count, rows, width), BF16),
             jax.ShapeDtypeStruct((4, width, head_width), BF16),
-            jax.ShapeDtypeStruct((width, heads), F32),
+            jax.ShapeDtypeStruct((heads, width), F32),
         ],
         scratch_shapes=[pltpu.VMEM((4, width, head_width), F32)],
         compiler_params=params(1),
+        cost_estimate=cost(11),
         name="proj_back",
     )(*g3, tail, rim, grate, x_ext, mixer_weights, beta_weight, grad_attn, head_out)
 
@@ -584,23 +539,6 @@
 def shifted(block, axis, distance):
     count = lax.axis_size(axis)
     return lax.ppermute(block, axis, [(i, (i + distance) % count) for i in range(count)])
-
-
-def compose(pair, axis, backward):
-    count = lax.axis_size(axis)
-    place = lax.axis_index(axis)
-    gathered = lax.all_gather(pair, axis)
-    laps = count - 1 - place if backward else place
-
-    def one(lap, state):
-        source = count - 1 - lap if backward else lap
-        block = lax.dynamic_index_in_dim(gathered, source, 0, False)
-        return (
-            jnp.einsum("mhij,mhjk->mhik", block[0], state.astype(BF16), preferred_element_type=F32)
-            + block[1]
-        )
-
-    return lax.fori_loop(0, laps, one, jnp.zeros(pair.shape[1:], F32))
 
 
 def rms(values, gain):
@@ -611,7 +549,664 @@
     inv = lax.rsqrt(jnp.mean(values * values, axis=-1, keepdims=True) + EPS)
     weighted = grad * gain
     grad_in = inv * weighted - values * inv**3 * jnp.mean(weighted * values, axis=-1, keepdims=True)
-    return grad_in, jnp.sum(grad * values * inv, axis=(0, 1))
+    return grad_in, jnp.sum(grad * values * inv, axis=0, keepdims=True)
+
+MESH = pl.DeviceIdType.MESH
+
+
+def flip(index, bit):
+    return index + bit * (1 - 2 * (index // bit % 2))
+
+
+def remote(src, dst, send, recv, seq, head):
+    return pltpu.make_async_remote_copy(
+        src_ref=src, dst_ref=dst, send_sem=send, recv_sem=recv, device_id=(seq, head), device_id_type=MESH
+    )
+
+
+def greet(devices, expected):
+    barrier = pltpu.get_barrier_semaphore()
+    for seq, head in devices:
+        pl.semaphore_signal(barrier, inc=1, device_id=(seq, head), device_id_type=MESH)
+    pl.semaphore_wait(barrier, expected)
+
+
+class Pieces:
+    def __init__(self, count, local):
+        self.local = local
+        self.per = local // PIECE
+        self.total = count * self.per
+        self.seq, self.head = lax.axis_index("seq"), lax.axis_index("head")
+        self.far, self.near = flip(self.head, 2), flip(self.head, 1)
+
+    def mine(self, k):
+        return k // self.per, pl.ds(pl.multiple_of(k % self.per * PIECE, PIECE), PIECE)
+
+    def block(self, ref, k, owner, tiled, first=0):
+        if tiled:
+            return ref.at[k, pl.ds(pl.multiple_of(owner * PIECE, PIECE), PIECE), :]
+        start = first + owner * self.local + k % self.per * PIECE
+        return ref.at[k // self.per, pl.ds(pl.multiple_of(start, 16), PIECE), :]
+
+
+class HeadGather:
+    def __init__(self, pieces, out_ref, tiled, first, send, recv):
+        self.pieces, self.out, self.tiled, self.first = pieces, out_ref, tiled, first
+        self.send, self.recv = send, recv
+
+    def place(self, k, owner):
+        return self.pieces.block(self.out, k, owner, self.tiled, self.first)
+
+    def copy(self, kind, k):
+        p = self.pieces
+        owner = p.far if kind == 2 else p.head
+        target = p.near if kind else p.far
+        ref = self.place(k, owner)
+        return remote(ref, ref, self.send.at[kind, k], self.recv.at[kind, k], p.seq, target)
+
+    def own(self, k):
+        self.copy(0, k).start()
+        self.copy(1, k).start()
+
+    def forward(self, k):
+        self.copy(0, k).wait_recv()
+        self.copy(2, k).start()
+
+    def arrived(self, k):
+        self.copy(1, k).wait_recv()
+        self.copy(2, k).wait_recv()
+
+    def sent(self, k):
+        for kind in range(3):
+            self.copy(kind, k).wait_send()
+
+
+class HeadScatter:
+    def __init__(self, pieces, part_ref, tiled, near_ref, stage_ref, far_ref, send, recv):
+        self.pieces, self.part, self.tiled = pieces, part_ref, tiled
+        self.nearby, self.stage, self.faraway = near_ref, stage_ref, far_ref
+        self.send, self.recv = send, recv
+
+    def block(self, k, owner):
+        return self.pieces.block(self.part, k, owner, self.tiled)
+
+    def copy(self, kind, k):
+        p = self.pieces
+        if kind == 2:
+            return remote(
+                self.stage.at[k], self.faraway.at[k], self.send.at[2, k], self.recv.at[2, k], p.seq, p.far
+            )
+        owner = p.near if kind else flip(p.near, 2)
+        return remote(
+            self.block(k, owner), self.nearby.at[kind, k], self.send.at[kind, k], self.recv.at[kind, k], p.seq, p.near
+        )
+
+    def start(self, k):
+        self.copy(0, k).start()
+        self.copy(1, k).start()
+
+    def forward(self, k):
+        self.copy(0, k).wait_recv()
+        total = self.block(k, self.pieces.far)[...].astype(F32) + self.nearby[0, k].astype(F32)
+        self.stage[k] = total.astype(BF16)
+        self.copy(2, k).start()
+
+    def total(self, k):
+        self.copy(1, k).wait_recv()
+        self.copy(2, k).wait_recv()
+        near = self.block(k, self.pieces.head)[...].astype(F32) + self.nearby[1, k].astype(F32)
+        return near + self.faraway[k].astype(F32)
+
+    def sent(self, k):
+        for kind in range(3):
+            self.copy(kind, k).wait_send()
+
+
+def each(count, *steps):
+    for step in steps:
+        pl.loop(0, count)(step)
+
+
+def scatter_scratch(count, local, width):
+    n = count * local // PIECE
+    return [
+        pltpu.VMEM((2, n, PIECE, width), BF16),
+        pltpu.VMEM((n, PIECE, width), BF16),
+        pltpu.VMEM((n, PIECE, width), BF16),
+        pltpu.SemaphoreType.DMA((3, n)),
+        pltpu.SemaphoreType.DMA((3, n)),
+    ]
+
+
+def gather_scratch(count, local):
+    n = count * local // PIECE
+    return [pltpu.SemaphoreType.DMA((3, n)), pltpu.SemaphoreType.DMA((3, n))]
+
+
+def vmem_specs(count):
+    return [pl.BlockSpec(memory_space=pltpu.VMEM)] * count
+
+
+def comm_params(collective):
+    return pltpu.CompilerParams(
+        collective_id=collective, has_side_effects=True, vmem_limit_bytes=VMEM_LIMIT
+    )
+
+
+PIECE = 64
+
+
+def norm_gather_body(heads, shards, x_ref, gain_ref, out_ref, send, recv, halo_send, halo_recv):
+    count, local, _ = x_ref.shape
+    pieces = Pieces(count, local)
+    seq, head = pieces.seq, pieces.head
+    after = lax.rem(seq + 1, shards)
+    before = lax.rem(seq + shards - 1, shards)
+    last = head == heads - 1
+    gather = HeadGather(pieces, out_ref, False, HALO, send, recv)
+    for k in range(pieces.total):
+        m, here = pieces.mine(k)
+        x = x_ref[m, here, :].astype(F32)
+        gather.place(k, head)[...] = rms(x, gain_ref[...]).astype(BF16)
+    greet(
+        [(seq, pieces.far), (seq, pieces.near), (before, heads - 1)],
+        2 + heads * last.astype(jnp.int32),
+    )
+    each(pieces.total, gather.own)
+
+    def halo(target):
+        src = out_ref.at[:, pl.ds(heads * local, HALO), :]
+        return remote(src, out_ref.at[:, pl.ds(0, HALO), :], halo_send.at[target], halo_recv, after, target)
+
+    @pl.when(last)
+    def _():
+        for target in range(heads):
+            halo(target).start()
+
+    each(pieces.total, gather.forward, gather.arrived, gather.sent)
+    halo(0).wait_recv()
+
+    @pl.when(last)
+    def _():
+        for target in range(heads):
+            halo(target).wait_send()
+
+
+def norm_gather(inputs, gain, heads, shards):
+    count, local, width = inputs.shape
+    return pl.pallas_call(
+        functools.partial(norm_gather_body, heads, shards),
+        in_specs=vmem_specs(2),
+        out_specs=vmem_specs(1)[0],
+        out_shape=jax.ShapeDtypeStruct((count, HALO + heads * local, width), BF16),
+        scratch_shapes=gather_scratch(count, local)
+        + [pltpu.SemaphoreType.DMA((heads,)), pltpu.SemaphoreType.DMA],
+        compiler_params=comm_params(0),
+        cost_estimate=cost(15),
+        name="norm_gather",
+    )(inputs, gain)
+
+
+def dense_block_body(
+    part_ref, x_ref, top_ref, all_top_ref, gain_ref, w_ref,
+    resid_ref, down_ref, grad_ref, mid_ref, out_ref, gain_grad_ref,
+    wt_ref, wsem, acc_ref, gh_ref, in_ref, gin_ref, *scratch,
+):
+    count, local, width = x_ref.shape
+    shards = w_ref.shape[0]
+    cut = width // shards
+    pieces = Pieces(count, local)
+    first = HeadScatter(pieces, part_ref, False, *scratch[:5])
+    spread = HeadGather(pieces, in_ref, True, 0, *scratch[5:7])
+    second = HeadScatter(pieces, gin_ref, True, *scratch[7:12])
+    back = HeadGather(pieces, out_ref, False, 0, *scratch[12:14])
+
+    def weights(p):
+        return pltpu.make_async_copy(w_ref.at[p], wt_ref.at[:, :, pl.ds(p * cut, cut)], wsem.at[p])
+
+    for p in range(shards):
+        weights(p).start()
+    greet([(pieces.seq, pieces.far), (pieces.seq, pieces.near)], 2)
+    n = pieces.total
+    each(n, first.start, first.forward)
+    for p in range(shards):
+        weights(p).wait()
+    gain_grad_ref[...] = jnp.zeros_like(gain_grad_ref)
+
+    @pl.loop(0, n)
+    def _(k):
+        gh_ref[k] = mm(all_top_ref[k], wt_ref[2], 1, 1)
+        m, here = pieces.mine(k)
+        resid = x_ref[m, here, :].astype(F32) + first.total(k)
+        resid_ref[m, here, :] = resid
+        spread.place(k, pieces.head)[...] = rms(resid, gain_ref[...]).astype(BF16)
+        spread.own(k)
+
+    def turn_back(k):
+        m, here = pieces.mine(k)
+        grad, gain_part = rms_back(second.total(k), resid_ref[m, here, :], gain_ref[...])
+        mid = top_ref[m, here, :].astype(F32) + grad
+        gain_grad_ref[...] += gain_part
+        mid_ref[m, here, :] = mid
+        back.place(k, pieces.head)[...] = mid.astype(BF16)
+        back.own(k)
+
+    spread.forward(0)
+
+    @pl.loop(0, n)
+    def _(k):
+        spread.arrived(k)
+        x = in_ref[k]
+        gate = mm(x, wt_ref[0], 1, 1)
+        up = mm(x, wt_ref[1], 1, 1)
+        grad_hidden = gh_ref[k]
+        sg = sigmoid(gate)
+        silu = gate * sg
+        hidden = (silu * up).astype(BF16)
+        grad_gate = (grad_hidden * up * (sg * (1.0 + gate * (1.0 - sg)))).astype(BF16)
+        grad_up = (grad_hidden * silu).astype(BF16)
+        gin_ref[k] = (mm(grad_gate, wt_ref[0]) + mm(grad_up, wt_ref[1])).astype(BF16)
+        second.start(k)
+
+        @pl.when(k + 1 < n)
+        def _():
+            spread.forward(k + 1)
+
+        down_ref[k] = mm(hidden, wt_ref[2]).astype(BF16)
+        second.forward(k)
+        adds = (mm(grad_gate, x, 0, 0), mm(grad_up, x, 0, 0), mm(hidden, all_top_ref[k], 0, 0))
+
+        @pl.when(k == 0)
+        def _():
+            for i, add in enumerate(adds):
+                acc_ref[i] = add
+
+        @pl.when(jnp.logical_and(k > 0, k + 1 < n))
+        def _():
+            for i, add in enumerate(adds):
+                acc_ref[i] += add
+
+        @pl.when(k + 1 == n)
+        def _():
+            for i, add in enumerate(adds):
+                total = (acc_ref[i] + add).astype(BF16)
+                for p in range(shards):
+                    grad_ref[p, i] = total[:, p * cut : (p + 1) * cut]
+
+        @pl.when(k > 0)
+        def _():
+            turn_back(k - 1)
+
+        @pl.when(k > 1)
+        def _():
+            back.forward(k - 2)
+
+    turn_back(n - 1)
+    back.forward(n - 2)
+    back.forward(n - 1)
+    each(n, back.arrived, back.sent, second.sent, spread.sent, first.sent)
+
+
+def dense_block(part, inputs, top, all_top, gain, weights):
+    count, local, width = inputs.shape
+    shards, _, hidden, cut = weights.shape
+    n = count * local // PIECE
+    tile = all_top.shape[1]
+    rows = part.shape[1]
+    return pl.pallas_call(
+        dense_block_body,
+        in_specs=vmem_specs(5) + [pl.BlockSpec(memory_space=pl.ANY)],
+        out_specs=vmem_specs(6),
+        out_shape=[
+            jax.ShapeDtypeStruct(inputs.shape, F32),
+            jax.ShapeDtypeStruct((n, tile, width), BF16),
+            jax.ShapeDtypeStruct(weights.shape, BF16),
+            jax.ShapeDtypeStruct(inputs.shape, F32),
+            jax.ShapeDtypeStruct((count, rows, width), BF16),
+            jax.ShapeDtypeStruct((1, width), F32),
+        ],
+        scratch_shapes=[
+            pltpu.VMEM((3, hidden, width), BF16),
+            pltpu.SemaphoreType.DMA((shards,)),
+            pltpu.VMEM((3, hidden, width), F32),
+            pltpu.VMEM((n, tile, hidden), F32),
+            pltpu.VMEM((n, tile, width), BF16),
+            pltpu.VMEM((n, tile, width), BF16),
+        ]
+        + (scatter_scratch(count, local, width) + gather_scratch(count, local)) * 2,
+        compiler_params=comm_params(1),
+        cost_estimate=cost(55),
+        name="dense_block",
+    )(part, inputs, top, all_top, gain, weights)
+
+
+class SeqSum:
+    def __init__(self, shards, part_ref, work_ref, got_ref, full_ref, send, recv):
+        self.part, self.work, self.got, self.full = part_ref, work_ref, got_ref, full_ref
+        self.send, self.recv = send, recv
+        self.seq, self.head = lax.axis_index("seq"), lax.axis_index("head")
+        self.bits = [1 << k for k in range((shards - 1).bit_length())]
+        self.members, self.rows = part_ref.shape[0], part_ref.shape[1] // 2
+        self.half = 128
+        self.chunks = 2 * self.members * (part_ref.shape[2] // self.half)
+        self.steps = 2 * len(self.bits)
+        self.copies = {}
+        self.kept, self.gone = [0], []
+        size = self.rows
+        for bit in self.bits:
+            size //= 2
+            mine = self.seq // bit % 2
+            self.gone.append(self.kept[-1] + size * (1 - mine))
+            self.kept.append(self.kept[-1] + size * mine)
+
+    def view(self, ref, chunk, first, size):
+        per = self.chunks // self.members
+        first = pl.multiple_of(chunk % 2 * self.rows + first, 8)
+        return ref.at[chunk // per, pl.ds(first, size), pl.ds(chunk % per // 2 * self.half, self.half)]
+
+    def begin(self, chunk, step):
+        size = self.rows >> (step + 1)
+        src = self.view(self.part if step == 0 else self.work, chunk, self.gone[step], size)
+        offset = self.rows - 2 * size
+        dst = self.view(self.got, chunk, offset, size)
+        c = remote(src, dst, self.send.at[step, chunk], self.recv.at[step, chunk], flip(self.seq, self.bits[step]), self.head)
+        c.start()
+        self.copies[step, chunk] = c
+
+    def fold(self, chunk, step):
+        size = self.rows >> (step + 1)
+        self.copies[step, chunk].wait_recv()
+        got = self.view(self.got, chunk, self.rows - 2 * size, size)
+        kept = self.view(self.part if step == 0 else self.work, chunk, self.kept[step + 1], size)
+        total = (kept[...].astype(F32) + got[...].astype(F32)).astype(BF16)
+        last = step == len(self.bits) - 1
+        self.view(self.full if last else self.work, chunk, self.kept[step + 1], size)[...] = total
+
+    def spread(self, chunk, step):
+        back = len(self.bits) - 1 - step
+        size = self.rows >> (back + 1)
+        ref = self.view(self.full, chunk, self.kept[back + 1], size)
+        at = len(self.bits) + step
+        c = remote(ref, ref, self.send.at[at, chunk], self.recv.at[at, chunk], flip(self.seq, self.bits[back]), self.head)
+        c.start()
+        self.copies[at, chunk] = c
+
+    def stage(self, chunk, step):
+        n = len(self.bits)
+        if step > n:
+            self.copies[step - 1, chunk].wait_recv()
+        elif step > 0:
+            self.fold(chunk, step - 1)
+        if step < n:
+            self.begin(chunk, step)
+        elif step < 2 * n:
+            self.spread(chunk, step - n)
+
+    def tick(self, t):
+        done = []
+        for chunk in range(self.chunks):
+            step, odd = divmod(t - chunk, 2)
+            if not odd and 0 <= step <= self.steps:
+                self.stage(chunk, step)
+                if step == self.steps:
+                    done.append(chunk)
+        return done
+
+    def ticks(self):
+        return self.chunks + 2 * self.steps
+
+    def finish(self):
+        for c in self.copies.values():
+            c.wait_send()
+
+
+def finish_body(
+    shards, gx_ref, down_ref, mixer_ref, beta_ref, taps_ref, attn_part_ref, dense_part_ref, out_part_ref,
+    x_ref, mid_ref, resid_ref, gain_ref,
+    in_grad_ref, output_ref, total_ref, rows_ref, filter_ref, *scratch,
+):
+    gx_scratch, down_scratch = scratch[:5], scratch[5:10]
+    work_ref, got_ref, full_ref, ms, mr, row_got, row_now, tap_got, tap_now, rs, rr, gain_grad_ref = scratch[10:]
+    count, local, width = x_ref.shape
+    heads = beta_ref.shape[0]
+    members = taps_ref.shape[0]
+    pieces = Pieces(count, local)
+    gx = HeadScatter(pieces, gx_ref, False, *gx_scratch)
+    down = HeadScatter(pieces, down_ref, True, *down_scratch)
+    total = SeqSum(shards, mixer_ref, work_ref, got_ref, full_ref, ms, mr)
+    seq, head = pieces.seq, pieces.head
+
+    row_now[0] = jnp.zeros(row_now.shape[1:], F32)
+    tap_now[0] = jnp.zeros(tap_now.shape[1:], F32)
+    row_now[0, 0:heads, :] = beta_ref[...]
+    row_now[0, heads : heads + 1, :] = dense_part_ref[...]
+    row_now[0, heads + 1 : heads + 2, 0:HEAD_DIM] = out_part_ref[...]
+    for k in range(members):
+        tap_now[0, 8 * k : 8 * k + CONV, :] = taps_ref[k]
+    rounds = [(flip(seq, bit), head) for bit in total.bits] + [(seq, flip(head, 2)), (seq, flip(head, 1))]
+    greet(rounds, len(rounds))
+    small = {}
+
+    def small_start(k):
+        small[k] = [
+            remote(row_now.at[k], row_got.at[k], rs.at[0, k], rr.at[0, k], *rounds[k]),
+            remote(tap_now.at[k], tap_got.at[k], rs.at[1, k], rr.at[1, k], *rounds[k]),
+        ]
+        for c in small[k]:
+            c.start()
+
+    def small_end(k):
+        for c in small[k]:
+            c.wait_recv()
+        row_now[k + 1] = row_now[k] + row_got[k]
+        tap_now[k + 1] = tap_now[k] + tap_got[k]
+
+    n = pieces.total
+    gain_grad_ref[...] = attn_part_ref[...]
+
+    def gx_end(k):
+        m, here = pieces.mine(k)
+        grad, gain_part = rms_back(gx.total(k), x_ref[m, here, :].astype(F32), gain_ref[...])
+        gain_grad_ref[...] += gain_part
+        in_grad_ref[m, here, :] = mid_ref[m, here, :] + grad
+        down.forward(k)
+
+    def down_end(k):
+        m, here = pieces.mine(k)
+        output_ref[m, here, :] = (resid_ref[m, here, :] + down.total(k)).astype(BF16)
+
+    def small_turn(k):
+        if k == 0:
+            row_now[0, heads + 2 : heads + 3, :] = gain_grad_ref[...]
+        else:
+            small_end(k - 1)
+        if k < len(rounds):
+            small_start(k)
+
+    aside = [(1, lambda: each(n, gx.forward, down.start))]
+    aside += [(n + 2 * k, functools.partial(gx_end, k)) for k in range(n)]
+    for k in range(max(len(rounds) + 1, n)):
+        if k <= len(rounds):
+            aside.append((3 * n + 2 * k, functools.partial(small_turn, k)))
+        if k < n:
+            aside.append((3 * n + 2 * k + 1, functools.partial(down_end, k)))
+    each(n, gx.start)
+    for t in range(total.ticks()):
+        for chunk in total.tick(t):
+            whole = total.view(full_ref, chunk, 0, total.rows)
+            total.view(total_ref, chunk, 0, total.rows)[...] = whole[...].astype(F32)
+        while aside and aside[0][0] <= t:
+            aside.pop(0)[1]()
+    for _, act in aside:
+        act()
+    k = len(total.bits)
+    rows_ref[0] = row_now[k]
+    rows_ref[1] = row_now[len(rounds)]
+    for member in range(members):
+        filter_ref[member] = tap_now[k, 8 * member : 8 * member + CONV, :]
+    for group in small.values():
+        for c in group:
+            c.wait_send()
+    each(pieces.total, gx.sent, down.sent)
+    total.finish()
+
+
+def finish(gx_part, down_part, mixer_part, beta_part, taps_part, attn_part, dense_part, out_part, inputs, mid, resid, gain, shards):
+    count, local, width = inputs.shape
+    members, _, head_width = mixer_part.shape
+    bits = (shards - 1).bit_length()
+    rounds = bits + 2
+    chunks = 2 * members * head_width // 128
+    whole = pltpu.VMEM(mixer_part.shape, BF16)
+    return pl.pallas_call(
+        functools.partial(finish_body, shards),
+        in_specs=vmem_specs(12),
+        out_specs=vmem_specs(5),
+        out_shape=[
+            jax.ShapeDtypeStruct(inputs.shape, F32),
+            jax.ShapeDtypeStruct(inputs.shape, BF16),
+            jax.ShapeDtypeStruct(mixer_part.shape, F32),
+            jax.ShapeDtypeStruct((2, 8, width), F32),
+            jax.ShapeDtypeStruct(taps_part.shape, F32),
+        ],
+        scratch_shapes=scatter_scratch(count, local, width) * 2
+        + [
+            whole, whole, whole,
+            pltpu.SemaphoreType.DMA((2 * bits, chunks)),
+            pltpu.SemaphoreType.DMA((2 * bits, chunks)),
+            pltpu.VMEM((rounds, 8, width), F32),
+            pltpu.VMEM((rounds + 1, 8, width), F32),
+            pltpu.VMEM((rounds, 24, head_width), F32),
+            pltpu.VMEM((rounds + 1, 24, head_width), F32),
+            pltpu.SemaphoreType.DMA((2, rounds)),
+            pltpu.SemaphoreType.DMA((2, rounds)),
+            pltpu.VMEM((1, width), F32),
+        ],
+        compiler_params=comm_params(3),
+        cost_estimate=cost(70),
+        name="finish",
+    )(gx_part, down_part, mixer_part, beta_part, taps_part, attn_part, dense_part, out_part, inputs, mid, resid, gain)
+
+
+def compose_body(shards, backward, trans_ref, state_ref, *refs):
+    gather = None
+    if backward:
+        out_ref, stage_ref, got_ref, tx_ref, t_ref, s_ref, send, recv = refs
+    else:
+        top_ref, out_ref, all_ref, stage_ref, got_ref, tx_ref, t_ref, s_ref, send, recv, gs, gr = refs
+        pieces = Pieces(top_ref.shape[0], top_ref.shape[1])
+        gather = HeadGather(pieces, all_ref, True, 0, gs, gr)
+        for k in range(pieces.total):
+            m, here = pieces.mine(k)
+            gather.place(k, pieces.head)[...] = top_ref[m, here, :]
+    groups = trans_ref.shape[0]
+    seq, head = lax.axis_index("seq"), lax.axis_index("head")
+    place = shards - 1 - seq if backward else seq
+    steps = [1 << k for k in range((shards - 1).bit_length())]
+
+    def peer(distance):
+        return lax.rem(seq + shards + distance, shards)
+
+    sign = -1 if backward else 1
+    pair = [(seq, pieces.far), (seq, pieces.near)] if gather else []
+    greet([(peer(-sign * d), head) for d in steps] + pair, len(steps) + len(pair))
+
+    def apply(trans, state):
+        return mm(trans, state, 0, 0) if backward else mm(trans, state)
+
+    def join(late, early):
+        return mm(early, late) if backward else mm(late, early)
+
+    for k, d in enumerate(steps):
+        final = k == len(steps) - 1
+        copies = []
+        for part in range(1 if final else 2):
+            if k == 0:
+                src = state_ref if part == 0 else trans_ref
+            else:
+                src = stage_ref.at[k - 1, part]
+            copies.append(
+                remote(src, got_ref.at[k, part], send.at[k, part], recv.at[k, part], peer(sign * d), head)
+            )
+        for c in copies:
+            c.start()
+        if gather and k == 0:
+            each(pieces.total, gather.own)
+        if gather and k == min(1, len(steps) - 1):
+            each(pieces.total, gather.forward)
+        for c in copies:
+            c.wait_recv()
+        here = (place >= d).astype(F32)
+
+        @pl.loop(0, groups)
+        def _(g, k=k, final=final, here=here):
+            state = got_ref[k, 0, g].astype(F32) * here
+            if k == 0:
+                out_ref[g] = state
+            else:
+                out_ref[g] += apply(tx_ref[g], state)
+            if not final:
+                trans = got_ref[k, 1, g].astype(F32) * here
+                if k == 0:
+                    old_t, old_s = trans_ref[g].astype(F32), state_ref[g].astype(F32)
+                    tx_ref[g] = trans.astype(BF16)
+                else:
+                    old_t, old_s = t_ref[g], s_ref[g]
+                    tx_ref[g] = join(tx_ref[g], trans).astype(BF16)
+                new_s = old_s + apply(old_t, state)
+                new_t = join(old_t, trans)
+                s_ref[g] = new_s
+                t_ref[g] = new_t
+                stage_ref[k, 0, g] = new_s.astype(BF16)
+                stage_ref[k, 1, g] = new_t.astype(BF16)
+
+        for c in copies:
+            c.wait_send()
+    if gather:
+        each(pieces.total, gather.arrived, gather.sent)
+
+
+def compose(trans, state, shards, backward, top=None):
+    count, heads = state.shape[:2]
+    groups = count * heads
+    flat = (groups, HEAD_DIM, HEAD_DIM)
+    rounds = (shards - 1).bit_length()
+    out_shape = [jax.ShapeDtypeStruct(flat, F32)]
+    scratch = [
+        pltpu.VMEM((max(rounds - 1, 1), 2) + flat, BF16),
+        pltpu.VMEM((rounds, 2) + flat, BF16),
+        pltpu.VMEM(flat, BF16),
+        pltpu.VMEM(flat, F32),
+        pltpu.VMEM(flat, F32),
+        pltpu.SemaphoreType.DMA((rounds, 2)),
+        pltpu.SemaphoreType.DMA((rounds, 2)),
+    ]
+    operands = [trans.reshape(flat), state.reshape(flat)]
+    if not backward:
+        local = top.shape[1]
+        operands.append(top)
+        n = count * local // PIECE
+        out_shape.append(jax.ShapeDtypeStruct((n, PIECE * lax.axis_size("head"), top.shape[2]), BF16))
+        scratch += gather_scratch(count, local)
+    out = pl.pallas_call(
+        functools.partial(compose_body, shards, backward),
+        in_specs=vmem_specs(len(operands)),
+        out_specs=vmem_specs(len(out_shape)),
+        out_shape=out_shape,
+        scratch_shapes=scratch,
+        compiler_params=comm_params(5 if backward else 4),
+        cost_estimate=cost(30),
+        name="compose_back" if backward else "compose",
+    )(*operands)
+    return (out[0].reshape(state.shape), *out[1:])
+
+
+def regroup(blocks, count):
+    if blocks.shape[0] == count:
+        return blocks
+    _, members, hidden, _ = blocks.shape
+    whole = blocks.transpose(1, 2, 0, 3).reshape(members, hidden, count, -1)
+    return whole.transpose(2, 0, 1, 3)
 
 
 def per_device(
@@ -619,60 +1214,44 @@
     seq_offsets, seq_lengths, out_grad,
 ):
     count, local_rows, width = inputs.shape
-    rows = local_rows * lax.axis_size("head")
-    base = (lax.axis_index("seq") * rows).astype(jnp.int32).reshape(1)
-    taps = filter_weights.astype(F32)
+    heads, shards = lax.axis_size("head"), lax.axis_size("seq")
+    base = (lax.axis_index("seq") * local_rows * heads).astype(jnp.int32).reshape(1)
+    taps = filter_weights
+    beta_rows = beta_weight.T
     gain_row = out_gain.reshape(1, HEAD_DIM)
-    dense_full = lax.all_gather(dense_weights, "seq", axis=1, tiled=True)
-    grad_top = lax.all_gather(out_grad, "head", axis=1, tiled=True)
-
-    resid_in = inputs.astype(F32)
-    normed_local = rms(resid_in, attn_gain).astype(BF16)
-    gathered = lax.all_gather(normed_local, "head", axis=1, tiled=True)
-    halo = shifted(gathered[:, rows - HALO :, :], "seq", 1)
-    x_ext = jnp.concatenate([halo, gathered], axis=1)
-    pq, pk, pv, rates, ps, oloc, phi, psi, score, inv, wr, up, pair = mix_fwd(
-        seq_offsets, seq_lengths, base, x_ext, mixer_weights, beta_weight, taps
+    attn_row = attn_gain.reshape(1, width)
+    dense_row = dense_gain.reshape(1, width)
+    dense_full = regroup(lax.all_gather(jnp.swapaxes(dense_weights, 1, 2), "seq", axis=0), width // 128)
+
+    x_ext = norm_gather(inputs, attn_row, heads, shards)
+    pq, pk, pv, rates, ps, oloc, phi, psi, score, inv, wr, up, trans, state = mix_fwd(
+        seq_offsets, seq_lengths, base, x_ext, mixer_weights, beta_rows, taps
     )
-    state_in = compose(pair, "seq", False)
+    state_in, grad_top = compose(trans, state, shards, False, out_grad)
     start, mixed, head_out, attn_part = mix_out(state_in, ps, oloc, phi, psi, gain_row, mixer_weights)
-    attn = lax.psum_scatter(attn_part, "head", scatter_dimension=1, tiled=True).astype(F32)
-    resid_mid = resid_in + attn
-    dense_in = lax.all_gather(rms(resid_mid, dense_gain).astype(BF16), "head", axis=1, tiled=True)
-    down_part, gin_part, dense_part = dense(
-        dense_in.reshape(-1, width), grad_top.reshape(-1, width), dense_full
+    resid_mid, down_part, dense_part, grad_mid, grad_attn, dense_gain_part = dense_block(
+        attn_part, inputs, out_grad, grad_top, dense_row, dense_full
     )
-    gin = lax.psum_scatter(
-        gin_part.reshape(count, rows, width), "head", scatter_dimension=1, tiled=True
-    ).astype(F32)
-    down = lax.psum_scatter(
-        down_part.reshape(count, rows, width), "head", scatter_dimension=1, tiled=True
-    ).astype(F32)
-    dense_total = lax.psum_scatter(dense_part, "seq", scatter_dimension=1, tiled=True).astype(F32)
-    output = (resid_mid + down).astype(BF16)
-    grad_norm, dense_gain_part = rms_back(gin, resid_mid, dense_gain)
-    grad_mid = out_grad.astype(F32) + grad_norm
-    grad_attn = lax.all_gather(grad_mid.astype(BF16), "head", axis=1, tiled=True)
+    dense_mine = lax.psum_scatter(regroup(dense_part, shards), "seq", scatter_dimension=0, tiled=True)
+    dense_total = jnp.swapaxes(dense_mine[0], 1, 2).astype(F32)
     dout, out_gain_part, dstate = mix_back(grad_attn, mixer_weights, mixed, gain_row, ps, phi)
-    dpair = jnp.stack([jnp.swapaxes(pair[0], 2, 3), dstate])
-    dend = compose(dpair, "seq", True)
+    dend = compose(trans, dstate, shards, True)[0]
     gq, gk, gv, tail, rim, grate, filter_part = mix_grad(
         seq_offsets, seq_lengths, base, (pq, pk, pv), rates, taps, dend, dout, start, ps, phi, score, inv, wr, up
     )
     rim_next = shifted(rim, "seq", -1)
-    last_shard = lax.axis_index("seq") == lax.axis_size("seq") - 1
-    rim_next = jnp.where(last_shard, 0.0, rim_next)
     gx_part, mixer_part, beta_part = proj_back(
-        (gq, gk, gv), tail, rim_next, grate, x_ext, mixer_weights, beta_weight, grad_attn, head_out
+        (gq, gk, gv), tail, rim_next, grate, x_ext, mixer_weights, beta_rows, grad_attn, head_out
     )
-    gx = lax.psum_scatter(gx_part, "head", scatter_dimension=1, tiled=True).astype(F32)
-    grad_in_norm, attn_gain_part = rms_back(gx, resid_in, attn_gain)
-    input_grad = grad_mid + grad_in_norm
-    mixer_total = lax.psum(mixer_part.astype(F32), "seq")
-    beta_total, filter_total = lax.psum((beta_part, filter_part), "seq")
-    attn_gain_total, out_gain_total, dense_gain_total = lax.psum(
-        (attn_gain_part, out_gain_part.reshape(HEAD_DIM), dense_gain_part), ("seq", "head")
+    input_grad, output, mixer_total, rows_total, filter_total = finish(
+        gx_part, down_part, mixer_part, beta_part, filter_part,
+        jnp.zeros((1, width), F32), dense_gain_part, out_gain_part, inputs, grad_mid, resid_mid, attn_row, shards,
     )
+    local_heads = beta_rows.shape[0]
+    beta_total = rows_total[0, :local_heads].T
+    dense_gain_total = rows_total[1, local_heads]
+    out_gain_total = rows_total[1, local_heads + 1, :HEAD_DIM]
+    attn_gain_total = rows_total[1, local_heads + 2]
     return (
         output, input_grad, attn_gain_total, mixer_total, beta_total, filter_total, out_gain_total,
         dense_gain_total, dense_total,

time: 768 us -> 347 us (0.45)
  waiting for transfers between devices: 401 us -> 2.78 us
  blocking collectives: 228 us -> 0 us
  Pallas kernels: 85.3 us -> 311 us
  other arithmetic: 17.6 us -> 2.25 us
  matrix products: 8.04 us -> 0 us
    all_gather x7 -> x1, waiting for transfers between devices: 269 us -> 0.01 us  [per_device(): lax.all_gather(jnp.swapaxes(dense_weights, 1, 2), 'seq', axis=0)]
    psum x2 -> x0, blocking collectives: 228 us -> none  [the longest x1 190 us: per_device(): mixer_total = lax.psum(mixer_part.astype(F32), 'seq')]
    pallas_call x1 -> x5, Pallas kernels: 22 us -> 249 us  [the longest x2 103 us: compose(): pl.pallas_call(functools.partial(compose_body, shards, backward), in_spec...]
    reduce_scatter x5 -> x1, waiting for transfers between devices: 121 us -> 0.01 us  [per_device(): lax.psum_scatter(regroup(dense_part, shards), 'seq', scatter_dimension=0,...]
    dot_general x7 -> x0, matrix products: 8.04 us -> none  [one(): jnp.einsum('mhij,mhjk->mhik', block[0], state.astype(BF16), preferred_ele...]
  transfers between devices with their start and end apart: 14 -> 3, of which waited for: 12 -> 1; matrix products, arithmetic and copies ran while one was open for 3% -> 1% of each run, Pallas kernels for 4% -> 73%
where the time goes in v3:
time: 347 us; the launch traced here: 346 us
  Pallas kernels  311 us (90%)
  between operations  14.1 us (4%)
  local copies, waits for them, and re-layouts  12 us (3%)
  starting transfers between devices  3.71 us (1%)
    pallas_call x2, Pallas kernels, compose(): pl.pallas_call(functools.partial(compose_body, shards, backward), in_spec...  103 us
    pallas_call x1, Pallas kernels, finish(): pl.pallas_call(functools.partial(finish_body, shards), in_specs=vmem_spec...  67.5 us
    pallas_call x1, Pallas kernels, dense_block(): pl.pallas_call(dense_block_body, in_specs=vmem_specs(5) + [pl.BlockSpec(m...  58.7 us
    pallas_call x1, Pallas kernels, mix_fwd(): pl.pallas_call(mix_fwd_body, grid=(count, heads), in_specs=[smem_spec(),...  23.2 us
    pallas_call x1, Pallas kernels, norm_gather(): pl.pallas_call(functools.partial(norm_gather_body, heads, shards), in_spe...  19.7 us
    pallas_call x1, Pallas kernels, mix_grad(): pl.pallas_call(mix_grad_body, grid=(heads, count), in_specs=[smem_spec(),...  17.5 us
    pallas_call x1, Pallas kernels, proj_back(): pl.pallas_call(proj_back_body, grid=(count,), in_specs=[g_spec, g_spec, g...  11.1 us
    unnamed x10, local copies, waits for them, and re-layouts  7.41 us
  transfers between devices with their start and end apart: 3, of which 1 were waited for; matrix products, arithmetic and copies ran while one was open for 1% of the time, Pallas kernels for 73%

profile of v3, /device:TPU:0, one launch (start us, length us, event | category | flops | bytes accessed | tf_op | source)
XLA Modules:
  0.0 346.1 jit_solution(14665318581040162239)
XLA Ops:
  7.2 0.7 all-gather.3.cloned.1.call-update
  7.9 0.0 reduce-scatter.2.cloned.1.call-start
  8.0 19.7 %norm_gather.1.x_ref = bf16[2,528,1024]{2,1,0:T(8,128)(2,1)} custom-call(bf16[2,128,1024]{2,1,0:T(8,128)(2,1)} %x_ref.5, f32[1,1024]{1,0:T(1,128)} %bitcast.33), custom_call_target="tpu_custom_call" | custom-call | bytes 45000000 | tf_op jit(solution)/shard_map/norm_gather/pallas_call | solution.py:737
  27.7 23.2 %mix_fwd.1 = (bf16[2,528,256]{2,1,0:T(8,128)(2,1)}, bf16[2,528,256]{2,1,0:T(8,128)(2,1)}, bf16[2,528,256]{2,1,0:T(8,128)(2,1)}, f32[2,2,512,1]{3,2,1,0:T(8,128)}...) custom-call(s32[2,3]{1,0:T(2,128)} %off_ref.3, ...), custom_call_target="tpu_custom_call" | custom-call | bytes 69000000 | tf_op jit(solution)/shard_map/mix_fwd/pallas_call | solution.py:197
  50.9 53.9 %compose.1 = (f32[4,128,128]{2,1,0:T(8,128)}, bf16[4,256,1024]{2,1,0:T(8,128)(2,1)}) custom-call(bf16[4,128,128]{2,1,0:T(8,128)(2,1)} %bitcast.28, bf16[4,128,128]{2,1,0:T(8,128)(2,1)} %bitcast.31, bf16[2,128,1024]{2,1,0:T(8,128)(2,1)} %top_ref.1), custom_call_target="tpu_custom_call" | custom-call | bytes 90000000 | tf_op jit(solution)/shard_map/compose/pallas_call | solution.py:1191
  104.7 5.3 %mix_out.1 = (bf16[2,2,512,128]{3,2,1,0:T(8,128)(2,1)}, f32[2,2,512,128]{3,2,1,0:T(8,128)}, bf16[2,512,256]{2,1,0:T(8,128)(2,1)}, bf16[2,512,1024]{2,1,0:T(8,128)(2,1)}) custom-call(f32[2,2,128,128]{3,2,1,0:T(8,128)} %bitcast.30, bf16[2,2,512,128]{3,2,1,0:T(8,128)(2,1)} %get-tuple-element.60.ps_ref, f32[2,2,512,128]{3,2,1,0:T(8,128)} %get-tuple-element.61.oloc_ref, ...), custom_call_target="tpu_custom_call" | custom-call | bytes 15000000 | tf_op jit(solution)/shard_map/mix_out/pallas_call | solution.py:244
  110.0 58.7 %dense_block.1 = (f32[2,128,1024]{2,1,0:T(8,128)}, bf16[4,256,1024]{2,1,0:T(8,128)(2,1)}, bf16[8,3,704,128]{3,2,1,0:T(8,128)(2,1)}, f32[2,128,1024]{2,1,0:T(8,12...) custom-call(bf16[2,512,1024]{2,1,0:T(8,128)(2,1)} %get-tuple-element.64.part_ref, bf16[2,128,1024]{2,1,0:T(8,128)(2,1)} %x_ref.5, ...), custom_call_target="tpu_custom_call" | custom-call | bytes 165000000 | tf_op jit(solution)/shard_map/dense_block/pallas_call | solution.py:856
  168.7 5.7 %mix_back.1 = (bf16[2,2,512,128]{3,2,1,0:T(8,128)(2,1)}, f32[1,128]{1,0:T(1,128)}, bf16[2,2,128,128]{3,2,1,0:T(8,128)(2,1)}) custom-call(bf16[2,512,1024]{2,1,0:T(8,128)(2,1)} %get-tuple-element.66.grad_ref.gattn_ref, bf16[4,1024,256]{2,1,0:T(8,128)(2,1)} %w_ref.7, f32[2,2,512,128]{3,2,1,0:T(8,128)} %get-tuple-element.67.mixed_ref, f32[1,128]{1,0:T(1,128)} %bitcast.41, ...), custom_call_target="tpu_custom_call" | custom-call | bytes 18000000 | tf_op jit(solution)/shard_map/mix_back/pallas_call | solution.py:312
  174.4 48.8 %compose_back.1 = f32[4,128,128]{2,1,0:T(8,128)} custom-call(bf16[4,128,128]{2,1,0:T(8,128)(2,1)} %bitcast.29, bf16[4,128,128]{2,1,0:T(8,128)(2,1)} %bitcast.32), custom_call_target="tpu_custom_call" | custom-call | bytes 90000000 | tf_op jit(solution)/shard_map/compose_back/pallas_call | solution.py:1191
  223.3 17.5 %mix_grad.1 = (bf16[2,512,256]{2,1,0:T(8,128)(2,1)}, bf16[2,512,256]{2,1,0:T(8,128)(2,1)}, bf16[2,512,256]{2,1,0:T(8,128)(2,1)}, f32[2,3,8,256]{3,2,1,0:T(8,128)...) custom-call(s32[2,3]{1,0:T(2,128)} %off_ref.3, s32[2,3]{1,0:T(2,128)} %len_ref.3, ...), custom_call_target="tpu_custom_call" | custom-call | bytes 51000000 | tf_op jit(solution)/shard_map/mix_grad/pallas_call | solution.py:442
  240.7 3.6 %collective-permute-start = (f32[2,3,8,256]{3,2,1,0:T(8,128)}, f32[2,3,8,256]{3,2,1,0:T(8,128)S(1)}, u32[]{:S(2)}, u32[]{:S(2)}) collective-permute-start(f32[2,3,8,256]{3,2,1,0:T(8,128)} %get-tuple-element.79), channel_id=1, source_target_pairs={{0,28},{4,0},{8,4},{12,8},{16,12},{20,16},{24,20},{28,24},{1,29},{... | collective-permute-start | bytes 147464 | tf_op jit(solution)/shard_map/ppermute | solution.py:541
  244.4 2.1 collective-permute-done.rim_ref
  246.4 0.6 copy-done.1
  247.1 11.1 %proj_back.1 = (bf16[2,512,1024]{2,1,0:T(8,128)(2,1)}, bf16[4,1024,256]{2,1,0:T(8,128)(2,1)}, f32[2,1024]{1,0:T(2,128)}) custom-call(bf16[2,512,256]{2,1,0:T(8,128)(2,1)} %get-tuple-element.75.gq_ref, bf16[2,512,256]{2,1,0:T(8,128)(2,1)} %get-tuple-element.76.gk_ref, bf16[2,512,256]{2,1,0:T(8,128)(2,1)} %get-tuple-element.77.gv_ref, ...), custom_call_target="tpu_custom_call" | custom-call | bytes 33000000 | tf_op jit(solution)/shard_map/proj_back/pallas_call | solution.py:511
  258.1 0.6 broadcast_in_dim.3.attn_part_ref
  258.7 67.5 %finish.1 = (f32[2,128,1024]{2,1,0:T(8,128)}, bf16[2,128,1024]{2,1,0:T(8,128)(2,1)}, f32[4,1024,256]{2,1,0:T(8,128)}, f32[2,8,1024]{2,1,0:T(8,128)}, f32[3,4,256]{2,1,0:T(4,128)}) custom-call(bf16[2,512,1024]{2,1,0:T(8,128)(2,1)} %get-tuple-element.82.gx_ref, bf16[4,256,1024]{2,1,0:T(8,128)(2,1)} %get-tuple-element.83.down_ref, ...), custom_call_target="tpu_custom_call" | custom-call | bytes 210000000 | tf_op jit(solution)/shard_map/finish/pallas_call | solution.py:1061
  326.2 1.2 slice_bitcast_fusion.1
  327.4 1.4 fusion
  328.9 1.4 slice_bitcast_fusion
  330.2 2.2 convert_bitcast_fusion
  332.5 1.9 copy.24
  334.4 2.3 copy.25
  336.7 2.0 copy.26
  338.7 0.6 copy.27
  (9 shorter events, 0.1 us)
Async XLA Ops:
  7.2 102.8 %all-gather.3.cloned.1.call-start = ((), (), s32[]{:S(2)}) async-start(), calls=%async_computation.2 | async-start | bytes 4866048 | tf_op jit(solution)/shard_map/all_gather | solution.py:1224
  7.9 322.3 %reduce-scatter.2.cloned.1.call-start = ((), (), s32[]{:S(2)}) async-start(), calls=%async_computation.1 | async-start | bytes 4866048 | tf_op jit(solution)/shard_map/reduce_scatter | solution.py:1235
  240.7 5.7 %collective-permute-start = (f32[2,3,8,256]{3,2,1,0:T(8,128)}, f32[2,3,8,256]{3,2,1,0:T(8,128)S(1)}, u32[]{:S(2)}, u32[]{:S(2)}) collective-permute-start(f32[2,3,8,256]{3,2,1,0:T(8,128)} %get-tuple-element.79), channel_id=1, source_target_pairs={{0,28},{4,0},{8,4},{12,8},{16,12},{20,16},{24,20},{28,24},{1,29},{... | collective-permute-start | bytes 147464 | tf_op jit(solution)/shard_map/ppermute | solution.py:541
  246.4 0.6 copy-start.1
  330.2 6.4 %copy-start = (f32[4,1024,256]{2,1,0:T(8,128)S(1)}, f32[4,1024,256]{2,1,0:T(8,128)}, u32[]{:S(2)}) copy-start(f32[4,1024,256]{2,1,0:T(8,128)} %get-tuple-element.111) | copy-start | bytes 12582916
  336.7 2.0 copy-start.2
Sparse Core Ops, SparseCore 0:
  10.2 93.2 all-gather.2
  168.8 106.0 reduce-scatter.1

commit v4 on v1

v4 whole, which is shorter than its diff:
```python
import functools

import jax
import jax.numpy as jnp
from jax import lax
from jax.experimental import pallas as pl
from jax.experimental.pallas import tpu as pltpu
from jax.sharding import PartitionSpec as P

HEAD_DIM = 128
CONV = 4
CHUNK = 128
HALO = 16
RIM = 8
PIECE = 64
EPS = 1e-06
F32 = jnp.float32
BF16 = jnp.bfloat16
VMEM_LIMIT = 56 * 1024 * 1024


def mm(a, b, ca=1, cb=0):
    return lax.dot_general(
        a.astype(BF16), b.astype(BF16), (((ca,), (cb,)), ((), ())), preferred_element_type=F32
    )


def split(a):
    high = a.astype(BF16)
    return high, (a - high.astype(F32)).astype(BF16)


def mm3(a, b, ca=1, cb=0):
    ah, al = split(a)
    bh, bl = split(b)
    return mm(ah, bh, ca, cb) + (mm(ah, bl, ca, cb) + mm(al, bh, ca, cb))


def sigmoid(v):
    return 1.0 / (1.0 + jnp.exp(-v))


def row_info(off_ref, len_ref, m, base, rows):
    t = base + lax.broadcasted_iota(jnp.int32, (rows, 1), 0)
    start = jnp.zeros_like(t)
    length = jnp.zeros_like(t)
    for i in range(off_ref.shape[1]):
        inside = t >= off_ref[m, i]
        start = jnp.where(inside, off_ref[m, i], start)
        length = jnp.where(inside, len_ref[m, i], length)
    rel = t - start
    return rel, (rel < length).astype(F32)


def chunk_masks(rel):
    n = rel.shape[0]
    i = lax.broadcasted_iota(jnp.int32, (n, n), 0)
    j = lax.broadcasted_iota(jnp.int32, (n, n), 1)
    same = rel >= i - j
    strict = jnp.logical_and(same, i > j)
    incl = jnp.logical_and(same, i >= j)
    col = lax.broadcasted_iota(jnp.int32, (n, 1), 0)
    sees = (rel > col).astype(F32)
    last = rel[n - 1 : n, :]
    stays = ((n - 1 - col) <= last).astype(F32)
    keep = (last > n - 1).astype(F32)
    return strict, incl, sees, stays, keep


def unit_lower_inverse(a_list):
    n = a_list[0].shape[0]
    i = lax.broadcasted_iota(jnp.int32, (n, n), 0)
    j = lax.broadcasted_iota(jnp.int32, (n, n), 1)
    eye = (i == j).astype(F32)
    size = 1
    inv_list = [eye for _ in a_list]
    while size < n:
        pair = jnp.logical_and(i // size == j // size + 1, (i // size) % 2 == 1)
        below = [jnp.where(pair, a, 0.0) for a in a_list]
        if size == 1:
            inv_list = [eye - b for b in below]
        else:
            half = [mm3(b, inv) for b, inv in zip(below, inv_list)]
            inv_list = [inv - mm3(inv, h) for inv, h in zip(inv_list, half)]
        size *= 2
    return inv_list


def lagged(ext, lag, rows):
    moved = pltpu.roll(ext, lag, 0) if lag else ext
    return moved[HALO : HALO + rows]


def lag_masks(rel):
    return [None] + [(rel >= lag).astype(F32) for lag in range(1, CONV)]


def filtered(ext, taps, masks, rows):
    total = None
    for lag in range(CONV):
        term = taps[lag : lag + 1, :] * lagged(ext, lag, rows)
        if masks[lag] is not None:
            term = term * masks[lag]
        total = term if total is None else total + term
    return total


MESH = pl.DeviceIdType.MESH


def flip(index, bit):
    return index + bit * (1 - 2 * (index // bit % 2))


def remote(src, dst, send, recv, seq, head):
    return pltpu.make_async_remote_copy(
        src_ref=src, dst_ref=dst, send_sem=send, recv_sem=recv, device_id=(seq, head), device_id_type=MESH
    )


def greet(devices, expected):
    barrier = pltpu.get_barrier_semaphore()
    for seq, head in devices:
        pl.semaphore_signal(barrier, inc=1, device_id=(seq, head), device_id_type=MESH)
    pl.semaphore_wait(barrier, expected)


class Pieces:
    def __init__(self, count, local):
        self.local = local
        self.per = local // PIECE
        self.total = count * self.per
        self.seq, self.head = lax.axis_index("seq"), lax.axis_index("head")
        self.far, self.near = flip(self.head, 2), flip(self.head, 1)

    def mine(self, k):
        return k // self.per, pl.ds(pl.multiple_of(k % self.per * PIECE, PIECE), PIECE)

    def block(self, ref, k, owner, tiled, first=0):
        if tiled:
            return ref.at[k, pl.ds(pl.multiple_of(owner * PIECE, PIECE), PIECE), :]
        start = first + owner * self.local + k % self.per * PIECE
        return ref.at[k // self.per, pl.ds(pl.multiple_of(start, 16), PIECE), :]


class HeadGather:
    def __init__(self, pieces, out_ref, tiled, first, send, recv):
        self.pieces, self.out, self.tiled, self.first = pieces, out_ref, tiled, first
        self.send, self.recv = send, recv

    def place(self, k, owner):
        return self.pieces.block(self.out, k, owner, self.tiled, self.first)

    def copy(self, kind, k):
        p = self.pieces
        owner = p.far if kind == 2 else p.head
        target = p.near if kind else p.far
        ref = self.place(k, owner)
        return remote(ref, ref, self.send.at[kind, k], self.recv.at[kind, k], p.seq, target)

    def own(self, k):
        self.copy(0, k).start()
        self.copy(1, k).start()

    def forward(self, k):
        self.copy(0, k).wait_recv()
        self.copy(2, k).start()

    def arrived(self, k):
        self.copy(1, k).wait_recv()
        self.copy(2, k).wait_recv()

    def sent(self, k):
        for kind in range(3):
            self.copy(kind, k).wait_send()


class HeadScatter:
    def __init__(self, pieces, part_ref, tiled, near_ref, stage_ref, far_ref, send, recv):
        self.pieces, self.part, self.tiled = pieces, part_ref, tiled
        self.nearby, self.stage, self.faraway = near_ref, stage_ref, far_ref
        self.send, self.recv = send, recv

    def block(self, k, owner):
        return self.pieces.block(self.part, k, owner, self.tiled)

    def copy(self, kind, k):
        p = self.pieces
        if kind == 2:
            return remote(
                self.stage.at[k], self.faraway.at[k], self.send.at[2, k], self.recv.at[2, k], p.seq, p.far
            )
        owner = p.near if kind else flip(p.near, 2)
        return remote(
            self.block(k, owner), self.nearby.at[kind, k], self.send.at[kind, k], self.recv.at[kind, k], p.seq, p.near
        )

    def start(self, k):
        self.copy(0, k).start()
        self.copy(1, k).start()

    def forward(self, k):
        self.copy(0, k).wait_recv()
        total = self.block(k, self.pieces.far)[...].astype(F32) + self.nearby[0, k].astype(F32)
        self.stage[k] = total.astype(BF16)
        self.copy(2, k).start()

    def total(self, k):
        self.copy(1, k).wait_recv()
        self.copy(2, k).wait_recv()
        near = self.block(k, self.pieces.head)[...].astype(F32) + self.nearby[1, k].astype(F32)
        return near + self.faraway[k].astype(F32)

    def sent(self, k):
        for kind in range(3):
            self.copy(kind, k).wait_send()


def each(count, *steps):
    for step in steps:
        pl.loop(0, count)(step)


def scatter_scratch(count, local, width):
    n = count * local // PIECE
    return [
        pltpu.VMEM((2, n, PIECE, width), BF16),
        pltpu.VMEM((n, PIECE, width), BF16),
        pltpu.VMEM((n, PIECE, width), BF16),
        pltpu.SemaphoreType.DMA((3, n)),
        pltpu.SemaphoreType.DMA((3, n)),
    ]


def gather_scratch(count, local):
    n = count * local // PIECE
    return [pltpu.SemaphoreType.DMA((3, n)), pltpu.SemaphoreType.DMA((3, n))]


class Compose:
    def __init__(self, shards, heads, trans_ref, state_ref, out_ref, back_x_ref, back_y_ref, scratch):
        self.shards, self.heads = shards, heads
        self.trans, self.state, self.out, self.back_x, self.back_y = trans_ref, state_ref, out_ref, back_x_ref, back_y_ref
        self.stage, self.got, self.got_back, self.tx, self.s, self.send, self.recv = scratch
        self.seq, self.head = lax.axis_index("seq"), lax.axis_index("head")
        self.steps = [1 << k for k in range((shards - 1).bit_length())]

    def peer(self, distance):
        return lax.rem(self.seq + self.shards + distance, self.shards)

    def peers(self):
        return [(self.peer(-d), self.head) for d in self.steps] + [(self.peer(d), self.head) for d in self.steps[:-1]]

    def copies(self, m, k):
        d = self.steps[k]
        here = pl.ds(m * self.heads, self.heads)
        final = k == len(self.steps) - 1
        out = []
        for part in range(1 if final else 3):
            if part == 2:
                src = self.trans if k == 0 else self.back_y.at[k - 1]
                dst = self.got_back.at[k]
            else:
                src = (self.state, self.trans)[part] if k == 0 else self.stage.at[k - 1, part]
                dst = self.got.at[k, part]
            to = self.peer(-d if part == 2 else d)
            sems = self.send.at[part, k, m], self.recv.at[part, k, m]
            out.append(remote(src.at[here], dst.at[here], *sems, to, self.head))
        return out

    def begin(self, m, k):
        for c in self.copies(m, k):
            c.start()

    def turn(self, m, k):
        n = len(self.steps)
        if k == 0:
            self.begin(m, 0)
            return
        for c in self.copies(m, k - 1):
            c.wait_recv()
        k -= 1
        final = k == n - 1
        here = (self.seq >= self.steps[k]).astype(F32)
        here_back = (self.seq + self.steps[k] < self.shards).astype(F32)
        groups = range(m * self.heads, (m + 1) * self.heads)
        pairs = {}
        for g in groups:
            state = self.got[k, 0, g].astype(F32) * here
            if final:
                self.out[g] = state if k == 0 else self.out[g] + mm(self.tx[g], state)
                continue
            pairs[g] = jnp.concatenate([self.got[k, 1, g].astype(F32) * here, state], axis=1).astype(BF16)
            old_t = self.trans[g] if k == 0 else self.stage[k - 1, 1, g]
            old_s = self.state[g].astype(F32) if k == 0 else self.s[g]
            both = mm(old_t, pairs[g])
            new_s = old_s + both[:, HEAD_DIM:]
            self.s[g] = new_s
            self.stage[k, 0, g] = new_s.astype(BF16)
            self.stage[k, 1, g] = both[:, :HEAD_DIM].astype(BF16)
            later = (self.got_back[k, g].astype(F32) * here_back).astype(BF16)
            self.back_x[k, g] = later if k == 0 else mm(later, self.back_x[k - 1, g]).astype(BF16)
            self.back_y[k, g] = mm(later, self.trans[g] if k == 0 else self.back_y[k - 1, g]).astype(BF16)
        if final:
            return
        self.begin(m, k + 1)
        for g in groups:
            if k == 0:
                self.out[g] = pairs[g][:, HEAD_DIM:].astype(F32)
                self.tx[g] = pairs[g][:, :HEAD_DIM]
            else:
                both = mm(self.tx[g], pairs[g])
                self.out[g] += both[:, HEAD_DIM:]
                self.tx[g] = both[:, :HEAD_DIM].astype(BF16)

    def sent(self, count):
        for m in range(count):
            for k in range(len(self.steps)):
                for c in self.copies(m, k):
                    c.wait_send()

    def script(self, m):
        return [functools.partial(self.turn, m, k) for k in range(len(self.steps) + 1)]


def compose_scratch(shards, count, flat):
    rounds = (shards - 1).bit_length()
    more = max(rounds - 1, 1)
    return [
        pltpu.VMEM((more, 2) + flat, BF16),
        pltpu.VMEM((rounds, 2) + flat, BF16),
        pltpu.VMEM((more,) + flat, BF16),
        pltpu.VMEM(flat, BF16),
        pltpu.VMEM(flat, F32),
        pltpu.SemaphoreType.DMA((3, rounds, count)),
        pltpu.SemaphoreType.DMA((3, rounds, count)),
    ]


class ComposeBack:
    def __init__(self, shards, heads, trans_ref, state_ref, back_x_ref, back_y_ref, out_ref, scratch):
        self.shards, self.heads = shards, heads
        self.trans, self.state, self.back_x, self.back_y, self.out = trans_ref, state_ref, back_x_ref, back_y_ref, out_ref
        self.stage, self.got, self.s, self.send, self.recv = scratch
        self.seq, self.head = lax.axis_index("seq"), lax.axis_index("head")
        self.steps = [1 << k for k in range((shards - 1).bit_length())]

    def peer(self, distance):
        return lax.rem(self.seq + self.shards + distance, self.shards)

    def peers(self):
        return [(self.peer(d), self.head) for d in self.steps]

    def copy(self, m, k):
        here = pl.ds(m * self.heads, self.heads)
        src = self.state if k == 0 else self.stage.at[k - 1]
        dst = self.got.at[k]
        return remote(
            src.at[here], dst.at[here], self.send.at[k, m], self.recv.at[k, m], self.peer(-self.steps[k]), self.head
        )

    def begin(self, m, k):
        self.copy(m, k).start()

    def turn(self, m, k):
        n = len(self.steps)
        if k == 0:
            self.begin(m, 0)
            return
        k -= 1
        self.copy(m, k).wait_recv()
        here = (self.seq + self.steps[k] < self.shards).astype(F32)
        groups = range(m * self.heads, (m + 1) * self.heads)
        states = [(self.got[k, g].astype(F32) * here).astype(BF16) for g in groups]
        if k + 1 < n:
            for g, state in zip(groups, states):
                trans = self.trans[g] if k == 0 else self.back_y[k - 1, g]
                new_s = (self.state[g].astype(F32) if k == 0 else self.s[g]) + mm(trans, state, 0, 0)
                self.s[g] = new_s
                self.stage[k, g] = new_s.astype(BF16)
            self.begin(m, k + 1)
        for g, state in zip(groups, states):
            if k == 0:
                self.out[g] = state.astype(F32)
            else:
                self.out[g] += mm(self.back_x[k - 1, g], state, 0, 0)

    def sent(self, count):
        for m in range(count):
            for k in range(len(self.steps)):
                self.copy(m, k).wait_send()


def compose_back_scratch(shards, count, flat):
    rounds = (shards - 1).bit_length()
    return [
        pltpu.VMEM((max(rounds - 1, 1),) + flat, BF16),
        pltpu.VMEM((rounds,) + flat, BF16),
        pltpu.VMEM(flat, F32),
        pltpu.SemaphoreType.DMA((rounds, count)),
        pltpu.SemaphoreType.DMA((rounds, count)),
    ]


class LineGather:
    def __init__(self, shards, src_ref, place, send, recv, local):
        self.shards, self.src, self.place = shards, src_ref, place
        self.send, self.recv, self.local = send, recv, local
        self.seq, self.head = lax.axis_index("seq"), lax.axis_index("head")
        self.neighbour = flip(self.seq, 1)
        self.half = shards // 2

    def on_line(self, distance, base=None):
        base = self.seq if base is None else base
        return lax.rem(base + self.shards + 2 * distance, self.shards)

    def peers(self):
        return [(self.on_line(-d), self.head) for d in range(1, self.half)] + [(self.neighbour, self.head)]

    def along(self, member, d, block):
        sems = self.send.at[member, d], self.recv.at[member, d]
        return remote(self.src.at[member], self.place(member, block), *sems, self.on_line(d), self.head)

    def across(self, member, d, block):
        dst = self.place(member, block)
        sems = self.send.at[member, self.half + d], self.recv.at[member, self.half + d]
        return remote(dst if d else self.src.at[member], dst, *sems, self.neighbour, self.head)

    def mine(self, member):
        return pltpu.make_async_copy(self.src.at[member], self.place(member, self.seq), self.local.at[member])

    def start(self, member):
        self.mine(member).start()
        for d in range(1, self.half):
            self.along(member, d, self.seq).start()
        self.across(member, 0, self.seq).start()

    def forward(self, member):
        for d in range(1, self.half):
            block = self.on_line(-d)
            self.along(member, d, block).wait_recv()
            self.across(member, d, block).start()

    def arrived(self, member):
        self.mine(member).wait()
        for d in range(self.half):
            self.across(member, d, self.on_line(-d, self.neighbour)).wait_recv()

    def sent(self, member):
        for d in range(1, self.half):
            self.along(member, d, self.seq).wait_send()
        for d in range(self.half):
            self.across(member, d, self.on_line(-d)).wait_send()

    def finish(self, member):
        self.arrived(member)
        self.sent(member)


def mix_fwd_body(
    shards, count, heads, token_heads, extra, off_ref, len_ref, base_ref, w_ref, beta_ref, taps_ref, in_ref, gain_ref, top_ref, own_ref,
    pq_ref, pk_ref, pv_ref, rate_ref, ps_ref, oloc_ref, phi_ref, psi_ref, m_ref, inv_ref, wr_ref, up_ref,
    trans_ref, enter_ref, back_x_ref, back_y_ref, all_x_out, all_top_out, *refs,
):
    full_ref, refs = (refs[0], refs[1:]) if extra else (None, refs)
    all_x_ref, all_top_ref, out_sems, state_ref, x_send, x_recv, gather_send, gather_recv, halo_send, halo_recv, *refs = refs
    scratch, sems = refs[:7], refs[7:]
    mb = pl.program_id(0)
    head = pl.program_id(1)
    grid_step = mb * heads + head
    steps = count * heads
    local = in_ref.shape[1]
    pieces = Pieces(count, local)
    gather_x = HeadGather(pieces, all_x_ref, False, HALO, x_send, x_recv)
    gather = HeadGather(pieces, all_top_ref, True, 0, gather_send, gather_recv)
    rounds = Compose(shards, heads, trans_ref, state_ref, enter_ref, back_x_ref, back_y_ref, scratch)
    line = LineGather(shards, own_ref, lambda member, q: full_ref.at[q, member], *sems) if extra else None
    last = pieces.head == token_heads - 1

    def halo(target):
        src = all_x_ref.at[:, pl.ds(token_heads * local, HALO), :]
        dst = all_x_ref.at[:, pl.ds(0, HALO), :]
        return remote(src, dst, halo_send.at[target], halo_recv, lax.rem(pieces.seq + 1, shards), target)

    def some(act, first, stop):
        pl.loop(first, stop)(act)

    def write_out(i):
        src, dst = ((all_x_ref, all_x_out), (all_top_ref, all_top_out))[i]
        return pltpu.make_async_copy(src, dst, out_sems.at[i])

    @pl.when(grid_step == 0)
    def _():
        for k in range(pieces.total):
            m, here = pieces.mine(k)
            x = in_ref[m, here, :].astype(F32)
            gather_x.place(k, pieces.head)[...] = rms(x, gain_ref[...]).astype(BF16)
            gather.place(k, pieces.head)[...] = top_ref[m, here, :]
        before = lax.rem(pieces.seq + shards - 1, shards)
        peers = rounds.peers() + (line.peers() if extra else []) + [(pieces.seq, pieces.far), (pieces.seq, pieces.near)]
        greet(peers + [(before, token_heads - 1)], len(peers) + token_heads * last.astype(jnp.int32))
        some(gather_x.own, 0, pieces.per)

        @pl.when(last)
        def _():
            for target in range(token_heads):
                halo(target).start()

        some(gather_x.own, pieces.per, pieces.total)
        if extra:
            for member in range(2):
                line.start(member)
        some(gather_x.forward, 0, pieces.per)
        some(gather_x.arrived, 0, pieces.per)
        halo(0).wait_recv()

    @pl.when(grid_step == min(1, steps - 1))
    def _():
        some(gather_x.forward, pieces.per, pieces.total)
        each(pieces.total, gather.own)

    @pl.when(grid_step == min(heads, steps - 1))
    def _():
        some(gather_x.arrived, pieces.per, pieces.total)
        write_out(0).start()

    if extra:
        for at, member in ((1, 0), (steps - 1, 1)):

            @pl.when(grid_step == at)
            def _(member=member):
                line.forward(member)

    left = []
    plan = {}
    for m in range(count):
        turns = rounds.script(m)
        if m + 1 < count:
            places = [((m + 1) * heads - 1, 1), ((m + 1) * heads, 1)]
            for place in places:
                if turns:
                    plan.setdefault(place, []).append(turns.pop(0))
        left.append(turns)

    def advance(point):
        for (at, where), turns in plan.items():
            if where == point:

                @pl.when(grid_step == at)
                def _(turns=turns):
                    for turn in turns:
                        turn()

    rows = all_x_ref.shape[1] - HALO
    rel, valid = row_info(off_ref, len_ref, mb, base_ref[0], rows)
    x = all_x_ref[mb]
    masks = lag_masks(rel)
    acts = []
    for member, out in enumerate((pq_ref, pk_ref, pv_ref)):
        proj = mm(x, w_ref[member]).astype(BF16)
        out[0] = proj
        filt = filtered(proj.astype(F32), taps_ref[member].astype(F32), masks, rows)
        acts.append(filt * sigmoid(filt))
    query, key, value = acts
    query = query * lax.rsqrt(jnp.sum(query * query, axis=-1, keepdims=True) + EPS)
    key = key * lax.rsqrt(jnp.sum(key * key, axis=-1, keepdims=True) + EPS)
    raw_all = mm(x, beta_ref[...], 1, 1)[HALO:]
    lane = lax.broadcasted_iota(jnp.int32, raw_all.shape, 1)
    raw = jnp.sum(jnp.where(lane == head, raw_all, 0.0), axis=-1, keepdims=True)
    rate_ref[0, 0] = raw
    rate = sigmoid(raw) * valid
    spans = [slice(c * CHUNK, (c + 1) * CHUNK) for c in range(rows // CHUNK)]
    all_masks = [chunk_masks(rel[s]) for s in spans]
    systems, scores = [], []
    for s, (strict, incl, _, _, _) in zip(spans, all_masks):
        both = mm(jnp.concatenate([query[s], key[s]], axis=0), key[s], 1, 1)
        scores.append(jnp.where(incl, both[:CHUNK], 0.0))
        systems.append(jnp.where(strict, rate[s] * both[CHUNK:], 0.0))
    advance(0)
    inverses = unit_lower_inverse(systems)
    i = lax.broadcasted_iota(jnp.int32, (HEAD_DIM, HEAD_DIM), 0)
    j = lax.broadcasted_iota(jnp.int32, (HEAD_DIM, HEAD_DIM), 1)
    eye = (i == j).astype(F32)
    phis, psis, ps, olocs = [], [], [], []
    for s, masks_c, inv, score in zip(spans, all_masks, inverses, scores):
        _, _, sees, stays, keep = masks_c
        right = rate[s] * jnp.concatenate([sees * key[s], value[s]], axis=1)
        solved = mm(inv, right)
        write, update = solved[:, :HEAD_DIM], solved[:, HEAD_DIM:]
        moved = mm(stays * key[s], solved, 0, 0)
        phi = keep * eye - moved[:, :HEAD_DIM]
        psi = moved[:, HEAD_DIM:]
        scored = mm(score, solved)
        p = sees * query[s] - scored[:, :HEAD_DIM]
        m_ref[0, 0, s] = score.astype(BF16)
        inv_ref[0, 0, s] = inv.astype(BF16)
        wr_ref[0, 0, s] = write.astype(BF16)
        up_ref[0, 0, s] = update
        ps_ref[0, 0, s] = p.astype(BF16)
        oloc_ref[0, 0, s] = scored[:, HEAD_DIM:]
        phi_ref[0, 0, s] = phi
        psi_ref[0, 0, s] = psi
        phis.append(phi)
        psis.append(psi)
    trans, state = phis[0], psis[0]
    for phi, psi in zip(phis[1:], psis[1:]):
        both = mm3(phi, jnp.concatenate([trans, state], axis=1))
        trans = both[:, :HEAD_DIM]
        state = both[:, HEAD_DIM:] + psi
    trans_ref[grid_step] = trans.astype(BF16)
    state_ref[grid_step] = state.astype(BF16)
    advance(1)

    @pl.when(grid_step == count * heads - 1)
    def _():
        each(pieces.total, gather.forward)
        while any(left):
            for turns in left:
                if turns:
                    turns.pop(0)()
        rounds.sent(count)
        each(pieces.total, gather.arrived)
        write_out(1).start()
        each(pieces.total, gather.sent, gather_x.sent)
        write_out(0).wait()
        write_out(1).wait()

        @pl.when(last)
        def _():
            for target in range(token_heads):
                halo(target).wait_send()

        if extra:
            for member in range(2):
                line.finish(member)


def cost(us):
    return pl.CostEstimate(flops=0, bytes_accessed=int(us * 3.0e6), transcendentals=0)


def any_spec():
    return pl.BlockSpec(memory_space=pl.ANY)


def smem_spec():
    return pl.BlockSpec(memory_space=pltpu.SMEM)


def params(count, collective=None):
    return pltpu.CompilerParams(
        dimension_semantics=("arbitrary",) * count,
        vmem_limit_bytes=VMEM_LIMIT,
        collective_id=collective,
        has_side_effects=collective is not None,
    )


def line_scratch(shards):
    return [pltpu.SemaphoreType.DMA((3, shards))] * 2 + [pltpu.SemaphoreType.DMA((3,))]


def mix_fwd(offsets, lengths, base, mixer_weights, beta_weight, taps, inputs, gain, top, dense_weights, shards, extra):
    count, local, width = inputs.shape
    token_heads = lax.axis_size("head")
    rows = local * token_heads
    ext_rows = rows + HALO
    heads = beta_weight.shape[0]
    per_head = pl.BlockSpec((1, 1, rows, HEAD_DIM), lambda m, h: (m, h, 0, 0))
    proj_spec = pl.BlockSpec((1, ext_rows, HEAD_DIM), lambda m, h: (m, 0, h))
    proj_shape = jax.ShapeDtypeStruct((count, ext_rows, heads * HEAD_DIM), BF16)

    def big(kind):
        return jax.ShapeDtypeStruct((count, heads, rows, HEAD_DIM), kind)

    flat = (count * heads, HEAD_DIM, HEAD_DIM)
    more = max((shards - 1).bit_length() - 1, 1)
    all_x = (count, ext_rows, width)
    all_top = (count * local // PIECE, PIECE * token_heads, width)
    shapes = [
        jax.ShapeDtypeStruct(flat, BF16),
        jax.ShapeDtypeStruct(flat, F32),
        jax.ShapeDtypeStruct((more,) + flat, BF16),
        jax.ShapeDtypeStruct((more,) + flat, BF16),
        jax.ShapeDtypeStruct(all_x, BF16),
        jax.ShapeDtypeStruct(all_top, BF16),
    ]
    more_shapes = [jax.ShapeDtypeStruct((shards, 2) + dense_weights.shape[1:], BF16)] if extra else []
    shapes += more_shapes
    line_sems = line_scratch(shards) if extra else []
    return pl.pallas_call(
        functools.partial(mix_fwd_body, shards, count, heads, token_heads, extra),
        grid=(count, heads),
        in_specs=[
            smem_spec(), smem_spec(), smem_spec(),
            pl.BlockSpec((3, width, HEAD_DIM), lambda m, h: (0, 0, h)),
            pl.BlockSpec(beta_weight.shape, lambda m, h: (0, 0)),
            pl.BlockSpec((3, CONV, HEAD_DIM), lambda m, h: (0, 0, h)),
        ]
        + vmem_specs(3)
        + [any_spec()],
        out_specs=[proj_spec] * 3
        + [pl.BlockSpec((1, 1, rows, 1), lambda m, h: (m, h, 0, 0))]
        + [per_head] * 8
        + vmem_specs(4)
        + [any_spec()] * (len(shapes) - 4),
        out_shape=[proj_shape] * 3
        + [jax.ShapeDtypeStruct((count, heads, rows, 1), F32)]
        + [big(BF16), big(F32), big(F32), big(F32), big(BF16), big(BF16), big(BF16), big(F32)]
        + shapes,
        scratch_shapes=[
            pltpu.VMEM(all_x, BF16), pltpu.VMEM(all_top, BF16), pltpu.SemaphoreType.DMA((2,)), pltpu.VMEM(flat, BF16)
        ]
        + gather_scratch(count, local) * 2
        + [pltpu.SemaphoreType.DMA((token_heads,)), pltpu.SemaphoreType.DMA]
        + compose_scratch(shards, count, flat)
        + line_sems,
        compiler_params=params(2, 4),
        cost_estimate=cost(45),
        name="mix_fwd",
    )(offsets, lengths, base, mixer_weights, beta_weight, taps, inputs, gain, top, dense_weights)


def mix_out_body(state_ref, ps_ref, oloc_ref, phi_ref, psi_ref, gain_ref, w_ref, start_ref, mixed_ref, head_ref, part_ref):
    heads = ps_ref.shape[1]
    rows = ps_ref.shape[2]
    gain = gain_ref[...]
    states = [state_ref[0, h] for h in range(heads)]
    for c in range(rows // CHUNK):
        s = slice(c * CHUNK, (c + 1) * CHUNK)
        for h in range(heads):
            state = states[h]
            start_ref[0, h, s] = state.astype(BF16)
            mixed = oloc_ref[0, h, s] + mm(ps_ref[0, h, s], state)
            mixed_ref[0, h, s] = mixed
            normed = mixed * lax.rsqrt(jnp.mean(mixed * mixed, axis=-1, keepdims=True) + EPS) * gain
            head_ref[0, s, h * HEAD_DIM : (h + 1) * HEAD_DIM] = normed.astype(BF16)
            states[h] = mm3(phi_ref[0, h, s], state) + psi_ref[0, h, s]
    part_ref[0] = mm(head_ref[0], w_ref[0], 1, 1).astype(BF16)


def mix_out(state_in, ps, oloc, phi, psi, out_gain, mixer_weights):
    count, heads, rows, _ = ps.shape
    width = mixer_weights.shape[1]
    head_width = mixer_weights.shape[2]
    per_mb = pl.BlockSpec((1, heads, rows, HEAD_DIM), lambda m: (m, 0, 0, 0))
    return pl.pallas_call(
        mix_out_body,
        grid=(count,),
        in_specs=[
            pl.BlockSpec((1, heads, HEAD_DIM, HEAD_DIM), lambda m: (m, 0, 0, 0)),
            per_mb, per_mb, per_mb, per_mb,
            pl.BlockSpec((1, HEAD_DIM), lambda m: (0, 0)),
            pl.BlockSpec((1, width, head_width), lambda m: (3, 0, 0)),
        ],
        out_specs=[
            per_mb, per_mb,
            pl.BlockSpec((1, rows, head_width), lambda m: (m, 0, 0)),
            pl.BlockSpec((1, rows, width), lambda m: (m, 0, 0)),
        ],
        out_shape=[
            jax.ShapeDtypeStruct(ps.shape, BF16),
            jax.ShapeDtypeStruct(ps.shape, F32),
            jax.ShapeDtypeStruct((count, rows, head_width), BF16),
            jax.ShapeDtypeStruct((count, rows, width), BF16),
        ],
        compiler_params=params(1),
        cost_estimate=cost(5),
        name="mix_out",
    )(state_in, ps, oloc, phi, psi, out_gain, mixer_weights)


def mix_grad_body(
    shards, count, heads,
    off_ref, len_ref, base_ref, pq_ref, pk_ref, pv_ref, rate_ref, taps_ref, start_ref,
    m_ref, inv_ref, wr_ref, up_ref,
    grad_ref, wo_ref, mixed_ref, gain_ref, all_ps_ref, all_phi_ref, trans_ref, back_x_ref, back_y_ref,
    gq_ref, gk_ref, gv_ref, tail_ref, rim_ref, grate_ref, gtaps_ref, gain_grad_ref,
    dstate_ref, dend_ref, all_dout_ref, *scratch,
):
    mb = pl.program_id(0)
    head = pl.program_id(1)
    grid_step = mb * heads + head
    rounds = ComposeBack(shards, heads, trans_ref, dstate_ref, back_x_ref, back_y_ref, dend_ref, scratch)
    n = len(rounds.steps)
    late = [1] if count > 1 else []

    def mix_back(m):
        gain = gain_ref[...]
        grad_head = mm(grad_ref[m], wo_ref[0])
        states = [None] * heads
        for h in range(heads):
            e = grad_head[:, h * HEAD_DIM : (h + 1) * HEAD_DIM]
            v = mixed_ref[m, h]
            r = lax.rsqrt(jnp.mean(v * v, axis=-1, keepdims=True) + EPS)
            weighted = e * gain
            dout = r * weighted - v * (r * r * r * jnp.mean(weighted * v, axis=-1, keepdims=True))
            gain_grad_ref[...] += jnp.sum(e * v * r, axis=0, keepdims=True)
            all_dout_ref[m * heads + h] = dout.astype(BF16)
        for c in reversed(range(all_ps_ref.shape[2] // CHUNK)):
            s = slice(c * CHUNK, (c + 1) * CHUNK)
            for h in range(heads):
                new = mm(all_ps_ref[m, h, s], all_dout_ref[m * heads + h, s], 0, 0)
                if states[h] is not None:
                    new += mm3(all_phi_ref[m, h, s], states[h], 0, 0)
                states[h] = new
        for h in range(heads):
            dstate_ref[m * heads + h] = states[h].astype(BF16)

    @pl.when(grid_step == 0)
    def _():
        gain_grad_ref[...] = jnp.zeros_like(gain_grad_ref)
        gtaps_ref[...] = jnp.zeros_like(gtaps_ref)
        greet(rounds.peers(), n)
        for m in range(count):
            mix_back(m)
            rounds.turn(m, 0)
        for k in range(1, n + 1):
            for m in range(count):
                if m not in late:
                    rounds.turn(m, k)
            for m in late:
                if k > 1:
                    rounds.turn(m, k - 1)

    rows = rate_ref.shape[2]
    rel, valid = row_info(off_ref, len_ref, mb, base_ref[0], rows)
    masks = lag_masks(rel)
    projs, filts, sigs, acts = [], [], [], []
    for member, ref in enumerate((pq_ref, pk_ref, pv_ref)):
        proj = ref[0].astype(F32)
        filt = filtered(proj, taps_ref[member].astype(F32), masks, rows)
        sg = sigmoid(filt)
        projs.append(proj)
        filts.append(filt)
        sigs.append(sg)
        acts.append(filt * sg)
    rq = lax.rsqrt(jnp.sum(acts[0] * acts[0], axis=-1, keepdims=True) + EPS)
    rk = lax.rsqrt(jnp.sum(acts[1] * acts[1], axis=-1, keepdims=True) + EPS)
    query = acts[0] * rq
    key = acts[1] * rk
    value = acts[2]
    sig_rate = sigmoid(rate_ref[0, 0])
    rate = sig_rate * valid
    spans = [slice(c * CHUNK, (c + 1) * CHUNK) for c in range(rows // CHUNK)]
    dstates = [None] * len(spans)
    dstate = dend_ref[grid_step]
    for c in reversed(range(len(spans))):
        s = spans[c]
        dstates[c] = dstate
        if c:
            dstate = mm3(all_phi_ref[mb, head, s], dstate, 0, 0) + mm(all_ps_ref[mb, head, s], all_dout_ref[grid_step, s], 0, 0)
    dqs, dks, dvs, drates = [], [], [], []
    for c, s in enumerate(spans):
        strict, incl, sees, stays, _ = chunk_masks(rel[s])
        q, k, v, b = query[s], key[s], value[s], rate[s]
        dout = all_dout_ref[grid_step, s]
        start = start_ref[0, 0, s]
        fresh = up_ref[0, 0, s] - mm(wr_ref[0, 0, s], start)
        dfresh = mm(m_ref[0, 0, s], dout, 0, 0) + mm(stays * k, dstates[c])
        e = mm(inv_ref[0, 0, s], dfresh, 0, 0)
        left = jnp.concatenate([dout, e.astype(BF16)], axis=0)
        right = jnp.concatenate([fresh.astype(BF16), start], axis=0)
        outer = mm(left, right, 1, 1)
        dscore = jnp.where(incl, outer[:CHUNK, :CHUNK], 0.0)
        dsystem = jnp.where(strict, -outer[CHUNK:, :CHUNK], 0.0)
        grads = jnp.concatenate([dscore, dsystem], axis=0).astype(BF16)
        byk = mm(grads, k)
        z = byk[CHUNK:] - sees * outer[CHUNK:, CHUNK:]
        dqs.append(sees * outer[:CHUNK, CHUNK:] + byk[:CHUNK])
        dk = mm(grads, jnp.concatenate([q, b * k], axis=0), 0, 0)
        dks.append(dk + stays * mm(fresh, dstates[c], 1, 1) + b * z)
        dvs.append(b * e)
        drates.append(jnp.sum(e * v + k * z, axis=-1, keepdims=True))
    dq = jnp.concatenate(dqs, axis=0)
    dk = jnp.concatenate(dks, axis=0)
    dv = jnp.concatenate(dvs, axis=0)
    drate = jnp.concatenate(drates, axis=0)
    grate_ref[0, 0] = drate * valid * sig_rate * (1.0 - sig_rate)
    dacts = [
        rq * dq - acts[0] * (rq * rq * rq * jnp.sum(dq * acts[0], axis=-1, keepdims=True)),
        rk * dk - acts[1] * (rk * rk * rk * jnp.sum(dk * acts[1], axis=-1, keepdims=True)),
        dv,
    ]
    for member, out in enumerate((gq_ref, gk_ref, gv_ref)):
        sg = sigs[member]
        dfilt = dacts[member] * (sg * (1.0 + filts[member] * (1.0 - sg)))
        taps = taps_ref[member].astype(F32)
        total = None
        pieces = []
        for lag in range(CONV):
            masked = dfilt if lag == 0 else dfilt * masks[lag]
            pieces.append(jnp.sum(masked * lagged(projs[member], lag, rows), axis=0, keepdims=True))
            scaled = masked * taps[lag : lag + 1, :]
            ext = jnp.concatenate([jnp.zeros((RIM, HEAD_DIM), F32), scaled], axis=0)
            if lag:
                ext = pltpu.roll(ext, rows + RIM - lag, 0)
            total = ext if total is None else total + ext
        here = total[RIM:]
        out[0] = here.astype(BF16)
        tail_ref[0, member] = here[rows - RIM :]
        rim_ref[0, member] = total[:RIM]
        lanes = pl.ds(pl.multiple_of(head * HEAD_DIM, HEAD_DIM), HEAD_DIM)
        gtaps_ref[member, :, lanes] += jnp.concatenate(pieces, axis=0)

    @pl.when(grid_step == 0)
    def _():
        for m in late:
            rounds.turn(m, n)

    @pl.when(grid_step == count * heads - 1)
    def _():
        rounds.sent(count)


def mix_grad(
    offsets, lengths, base, proj3, rates, taps, start, m, inv, wr, up,
    grad_attn, mixer_weights, mixed, out_gain, ps, phi, trans, back_x, back_y, shards,
):
    count, heads, rows, _ = ps.shape
    ext_rows = rows + HALO
    width = mixer_weights.shape[1]
    head_width = mixer_weights.shape[2]
    flat = (count * heads, HEAD_DIM, HEAD_DIM)
    per_head = pl.BlockSpec((1, 1, rows, HEAD_DIM), lambda m, h: (m, h, 0, 0))
    proj_spec = pl.BlockSpec((1, ext_rows, HEAD_DIM), lambda m, h: (m, 0, h))
    out_spec = pl.BlockSpec((1, rows, HEAD_DIM), lambda m, h: (m, 0, h))
    rate_spec = pl.BlockSpec((1, 1, rows, 1), lambda m, h: (m, h, 0, 0))
    small = pl.BlockSpec((1, 3, RIM, HEAD_DIM), lambda m, h: (m, 0, 0, h))
    small_shape = jax.ShapeDtypeStruct((count, 3, RIM, head_width), F32)
    return pl.pallas_call(
        functools.partial(mix_grad_body, shards, count, heads),
        grid=(count, heads),
        in_specs=[
            smem_spec(), smem_spec(), smem_spec(),
            proj_spec, proj_spec, proj_spec, rate_spec,
            pl.BlockSpec((3, CONV, HEAD_DIM), lambda m, h: (0, 0, h)),
        ]
        + [per_head] * 5
        + vmem_specs(1)
        + [pl.BlockSpec((1, width, head_width), lambda m, h: (3, 0, 0))]
        + vmem_specs(7),
        out_specs=[out_spec] * 3 + [small, small, rate_spec] + vmem_specs(2),
        out_shape=[jax.ShapeDtypeStruct((count, rows, head_width), BF16)] * 3
        + [
            small_shape, small_shape,
            jax.ShapeDtypeStruct(rates.shape, F32),
            jax.ShapeDtypeStruct(taps.shape, F32),
            jax.ShapeDtypeStruct((1, HEAD_DIM), F32),
        ],
        scratch_shapes=[
            pltpu.VMEM(flat, BF16),
            pltpu.VMEM(flat, F32),
            pltpu.VMEM((count * heads, rows, HEAD_DIM), BF16),
        ]
        + compose_back_scratch(shards, count, flat),
        compiler_params=params(2, 5),
        cost_estimate=cost(45),
        name="mix_grad",
    )(
        offsets, lengths, base, *proj3, rates, taps, start, m, inv, wr, up,
        grad_attn, mixer_weights, mixed, out_gain, ps, phi, trans, back_x, back_y,
    )


def rms(values, gain):
    return values * lax.rsqrt(jnp.mean(values * values, axis=-1, keepdims=True) + EPS) * gain


def rms_back(grad, values, gain):
    inv = lax.rsqrt(jnp.mean(values * values, axis=-1, keepdims=True) + EPS)
    weighted = grad * gain
    grad_in = inv * weighted - values * inv**3 * jnp.mean(weighted * values, axis=-1, keepdims=True)
    return grad_in, jnp.sum(grad * values * inv, axis=0, keepdims=True)

def vmem_specs(count):
    return [pl.BlockSpec(memory_space=pltpu.VMEM)] * count


def comm_params(collective):
    return pltpu.CompilerParams(
        collective_id=collective, has_side_effects=True, vmem_limit_bytes=VMEM_LIMIT
    )


def dense_block_body(
    shards, extra, part_ref, x_ref, top_ref, all_top_ref, gain_ref, w_ref, own_ref,
    resid_ref, down_ref, grad_ref, mid_ref, out_ref, gain_grad_ref,
    wt_ref, wsem, acc_ref, in_ref, gin_ref, gate_ref, up_ref, *scratch,
):
    count, local, width = x_ref.shape
    groups = w_ref.shape[0]
    cut = width // groups
    ready = 2 if extra else 3
    pieces = Pieces(count, local)
    line = None
    if extra:
        line = LineGather(
            shards, own_ref, lambda i, q: wt_ref.at[i, :, pl.ds(pl.multiple_of(q * cut, cut), cut)], *scratch[14:]
        )
    first = HeadScatter(pieces, part_ref, False, *scratch[:5])
    spread = HeadGather(pieces, in_ref, True, 0, *scratch[5:7])
    second = HeadScatter(pieces, gin_ref, True, *scratch[7:12])
    back = HeadGather(pieces, out_ref, False, 0, *scratch[12:14])

    def weights(p):
        return pltpu.make_async_copy(w_ref.at[p, 0:ready], wt_ref.at[0:ready, :, pl.ds(p * cut, cut)], wsem.at[p])

    peers = line.peers() if extra else []
    for p in range(groups):
        weights(p).start()
    greet([(pieces.seq, pieces.far), (pieces.seq, pieces.near)] + peers, 2 + len(peers))
    n = pieces.total
    each(n, first.start)
    if extra:
        line.start(2)
    each(n, first.forward)
    gain_grad_ref[...] = jnp.zeros_like(gain_grad_ref)

    @pl.loop(0, n)
    def _(k):
        m, here = pieces.mine(k)
        resid = x_ref[m, here, :].astype(F32) + first.total(k)
        resid_ref[m, here, :] = resid
        spread.place(k, pieces.head)[...] = rms(resid, gain_ref[...]).astype(BF16)
        spread.own(k)

    for p in range(groups):
        weights(p).wait()

    def turn_back(k):
        m, here = pieces.mine(k)
        grad, gain_part = rms_back(second.total(k), resid_ref[m, here, :], gain_ref[...])
        mid = top_ref[m, here, :].astype(F32) + grad
        gain_grad_ref[...] += gain_part
        mid_ref[m, here, :] = mid
        back.place(k, pieces.head)[...] = mid.astype(BF16)
        back.own(k)

    spread.forward(0)
    if extra:
        line.forward(2)

    @pl.loop(0, n)
    def _(k):
        spread.arrived(k)
        x = in_ref[k]
        gate_ref[k] = mm(x, wt_ref[0], 1, 1)
        up_ref[k] = mm(x, wt_ref[1], 1, 1)

        @pl.when(k + 1 < n)
        def _():
            spread.forward(k + 1)

    if extra:
        line.arrived(2)

    @pl.loop(0, n)
    def _(k):
        x = in_ref[k]
        gate = gate_ref[k]
        up = up_ref[k]
        grad_hidden = mm(all_top_ref[k], wt_ref[2], 1, 1)
        sg = sigmoid(gate)
        silu = gate * sg
        hidden = (silu * up).astype(BF16)
        grad_gate = (grad_hidden * up * (sg * (1.0 + gate * (1.0 - sg)))).astype(BF16)
        grad_up = (grad_hidden * silu).astype(BF16)
        gin_ref[k] = (mm(grad_gate, wt_ref[0]) + mm(grad_up, wt_ref[1])).astype(BF16)
        second.start(k)
        down_ref[k] = mm(hidden, wt_ref[2]).astype(BF16)
        second.forward(k)
        adds = (mm(grad_gate, x, 0, 0), mm(grad_up, x, 0, 0), mm(hidden, all_top_ref[k], 0, 0))

        @pl.when(k == 0)
        def _():
            for i, add in enumerate(adds):
                acc_ref[i] = add

        @pl.when(jnp.logical_and(k > 0, k + 1 < n))
        def _():
            for i, add in enumerate(adds):
                acc_ref[i] += add

        @pl.when(k + 1 == n)
        def _():
            for i, add in enumerate(adds):
                total = (acc_ref[i] + add).astype(BF16)
                for p in range(groups):
                    grad_ref[p, i] = total[:, p * cut : (p + 1) * cut]

        @pl.when(k > 0)
        def _():
            turn_back(k - 1)

        @pl.when(k > 1)
        def _():
            back.forward(k - 2)

    turn_back(n - 1)
    back.forward(n - 2)
    back.forward(n - 1)
    each(n, back.arrived, back.sent, second.sent, spread.sent, first.sent)
    if extra:
        line.sent(2)


def dense_block(part, inputs, top, all_top, gain, weights, own, shards, extra):
    count, local, width = inputs.shape
    groups, _, hidden, cut = weights.shape
    n = count * local // PIECE
    tile = all_top.shape[1]
    rows = part.shape[1]
    return pl.pallas_call(
        functools.partial(dense_block_body, shards, extra),
        in_specs=vmem_specs(5) + [any_spec()] * 2,
        out_specs=vmem_specs(6),
        out_shape=[
            jax.ShapeDtypeStruct(inputs.shape, F32),
            jax.ShapeDtypeStruct((n, tile, width), BF16),
            jax.ShapeDtypeStruct((groups, 3, hidden, cut), BF16),
            jax.ShapeDtypeStruct(inputs.shape, F32),
            jax.ShapeDtypeStruct((count, rows, width), BF16),
            jax.ShapeDtypeStruct((1, width), F32),
        ],
        scratch_shapes=[
            pltpu.VMEM((3, hidden, width), BF16),
            pltpu.SemaphoreType.DMA((groups,)),
            pltpu.VMEM((3, hidden, width), F32),
            pltpu.VMEM((n, tile, width), BF16),
            pltpu.VMEM((n, tile, width), BF16),
            pltpu.VMEM((n, tile, hidden), F32),
            pltpu.VMEM((n, tile, hidden), F32),
        ]
        + (scatter_scratch(count, local, width) + gather_scratch(count, local)) * 2
        + (line_scratch(shards) if extra else []),
        compiler_params=comm_params(1),
        cost_estimate=cost(55),
        name="dense_block",
    )(part, inputs, top, all_top, gain, weights, own)


class SeqSum:
    def __init__(self, shards, part_ref, work_ref, got_ref, full_ref, send, recv):
        self.part, self.work, self.got, self.full = part_ref, work_ref, got_ref, full_ref
        self.send, self.recv = send, recv
        self.seq, self.head = lax.axis_index("seq"), lax.axis_index("head")
        self.bits = [1 << k for k in range((shards - 1).bit_length())]
        self.members, self.rows = part_ref.shape[0], part_ref.shape[1] // 2
        self.half = 128
        self.chunks = 2 * self.members * (part_ref.shape[2] // self.half)
        self.steps = 2 * len(self.bits)
        self.order = [self.members - 1, *range(self.members - 1)]
        self.copies = {}
        self.kept, self.gone = [0], []
        size = self.rows
        for bit in self.bits:
            size //= 2
            mine = self.seq // bit % 2
            self.gone.append(self.kept[-1] + size * (1 - mine))
            self.kept.append(self.kept[-1] + size * mine)

    def view(self, ref, chunk, first, size):
        per = self.chunks // self.members
        first = pl.multiple_of(chunk % 2 * self.rows + first, 8)
        return ref.at[self.order[chunk // per], pl.ds(first, size), pl.ds(chunk % per // 2 * self.half, self.half)]

    def begin(self, chunk, step):
        size = self.rows >> (step + 1)
        src = self.view(self.part if step == 0 else self.work, chunk, self.gone[step], size)
        offset = self.rows - 2 * size
        dst = self.view(self.got, chunk, offset, size)
        c = remote(src, dst, self.send.at[step, chunk], self.recv.at[step, chunk], flip(self.seq, self.bits[step]), self.head)
        c.start()
        self.copies[step, chunk] = c

    def fold(self, chunk, step):
        size = self.rows >> (step + 1)
        self.copies[step, chunk].wait_recv()
        got = self.view(self.got, chunk, self.rows - 2 * size, size)
        kept = self.view(self.part if step == 0 else self.work, chunk, self.kept[step + 1], size)
        total = (kept[...].astype(F32) + got[...].astype(F32)).astype(BF16)
        last = step == len(self.bits) - 1
        self.view(self.full if last else self.work, chunk, self.kept[step + 1], size)[...] = total

    def spread(self, chunk, step):
        back = len(self.bits) - 1 - step
        size = self.rows >> (back + 1)
        ref = self.view(self.full, chunk, self.kept[back + 1], size)
        at = len(self.bits) + step
        c = remote(ref, ref, self.send.at[at, chunk], self.recv.at[at, chunk], flip(self.seq, self.bits[back]), self.head)
        c.start()
        self.copies[at, chunk] = c

    def stage(self, chunk, step):
        n = len(self.bits)
        if step > n:
            self.copies[step - 1, chunk].wait_recv()
        elif step > 0:
            self.fold(chunk, step - 1)
        if step < n:
            self.begin(chunk, step)
        elif step < 2 * n:
            self.spread(chunk, step - n)

    def tick(self, t):
        done = []
        for chunk in range(self.chunks):
            step, odd = divmod(t - chunk, 2)
            if not odd and 0 <= step <= self.steps:
                self.stage(chunk, step)
                if step == self.steps:
                    done.append(chunk)
        return done

    def ticks(self):
        return self.chunks + 2 * self.steps

    def finish(self):
        for c in self.copies.values():
            c.wait_send()


def finish_body(
    shards, gq_ref, gk_ref, gv_ref, tail_ref, rim_ref, grate_ref, all_x_ref, w_ref, beta_ref, gattn_ref, head_ref,
    down_ref, taps_ref, dense_part_ref, out_part_ref, x_ref, mid_ref, resid_ref, gain_ref,
    in_grad_ref, output_ref, total_ref, rows_ref, filter_ref,
    gx_ref, mixer_ref, g_ref, rim_got, rim_send, rim_recv, *scratch,
):
    gx_scratch, down_scratch = scratch[:5], scratch[5:10]
    work_ref, got_ref, full_ref, ms, mr, row_got, row_now, tap_got, tap_now, rs, rr, gain_grad_ref = scratch[10:]
    count, local, width = x_ref.shape
    heads = beta_ref.shape[0]
    members = taps_ref.shape[0]
    rows = gq_ref.shape[1]
    pieces = Pieces(count, local)
    gx = HeadScatter(pieces, gx_ref, False, *gx_scratch)
    down = HeadScatter(pieces, down_ref, True, *down_scratch)
    total = SeqSum(shards, mixer_ref, work_ref, got_ref, full_ref, ms, mr)
    seq, head = pieces.seq, pieces.head

    row_now[0] = jnp.zeros(row_now.shape[1:], F32)
    tap_now[0] = jnp.zeros(tap_now.shape[1:], F32)
    row_now[0, heads : heads + 1, :] = dense_part_ref[...]
    row_now[0, heads + 1 : heads + 2, 0:HEAD_DIM] = out_part_ref[...]
    for k in range(members):
        tap_now[0, 8 * k : 8 * k + CONV, :] = taps_ref[k]
    rounds = [(flip(seq, bit), head) for bit in total.bits] + [(seq, flip(head, 2)), (seq, flip(head, 1))]
    before = lax.rem(seq + shards - 1, shards)
    after = lax.rem(seq + 1, shards)
    greet(rounds + [(after, head)], len(rounds) + 1)
    rim = remote(rim_ref, rim_got, rim_send, rim_recv, before, head)
    rim.start()
    small = {}

    def grates(m):
        lane = lax.broadcasted_iota(jnp.int32, (rows, heads), 1)
        out = jnp.zeros((rows, heads), F32)
        for h in range(heads):
            out = jnp.where(lane == h, grate_ref[m, h], out)
        return out

    def weight_grad(member):
        total = None
        for m in range(count):
            left, right = (gattn_ref[m], head_ref[m]) if member == members else (all_x_ref[m, HALO:, :], g_ref[member, m])
            add = mm(left, right, 0, 0)
            total = add if total is None else total + add
        mixer_ref[member] = total.astype(BF16)

    def join_rims():
        rim.wait_recv()
        for member, ref in enumerate((gq_ref, gk_ref, gv_ref)):
            for m in range(count):
                g_ref[member, m, 0 : rows - 2 * RIM, :] = ref[m, 0 : rows - 2 * RIM, :]
                last = (tail_ref[m, member] + rim_got[m, member]).astype(BF16)
                g_ref[member, m, rows - 2 * RIM :, :] = jnp.concatenate([ref[m, rows - 2 * RIM : rows - RIM, :], last], axis=0)

    def row_grad(m):
        total = mm(grates(m), beta_ref[...])
        for member in range(members):
            total += mm(g_ref[member, m], w_ref[member], 1, 1)
        gx_ref[m] = total.astype(BF16)
        for k in range(m * pieces.per, (m + 1) * pieces.per):
            gx.start(k)

    def beta_grad():
        total = None
        for m in range(count):
            add = mm(grates(m), all_x_ref[m, HALO:, :], 0, 0)
            total = add if total is None else total + add
        row_now[0, 0:heads, :] = total

    def small_start(k):
        small[k] = [
            remote(row_now.at[k], row_got.at[k], rs.at[0, k], rr.at[0, k], *rounds[k]),
            remote(tap_now.at[k], tap_got.at[k], rs.at[1, k], rr.at[1, k], *rounds[k]),
        ]
        for c in small[k]:
            c.start()

    def small_end(k):
        for c in small[k]:
            c.wait_recv()
        row_now[k + 1] = row_now[k] + row_got[k]
        tap_now[k + 1] = tap_now[k] + tap_got[k]

    n = pieces.total
    gain_grad_ref[...] = jnp.zeros_like(gain_grad_ref)

    def gx_end(k):
        m, here = pieces.mine(k)
        grad, gain_part = rms_back(gx.total(k), x_ref[m, here, :].astype(F32), gain_ref[...])
        gain_grad_ref[...] += gain_part
        in_grad_ref[m, here, :] = mid_ref[m, here, :] + grad
        down.forward(k)

    def down_end(k):
        m, here = pieces.mine(k)
        output_ref[m, here, :] = (resid_ref[m, here, :] + down.total(k)).astype(BF16)

    def small_turn(k):
        if k == 0:
            row_now[0, heads + 2 : heads + 3, :] = gain_grad_ref[...]
        else:
            small_end(k - 1)
        if k < len(rounds):
            small_start(k)

    def weight_ready(chunk):
        per = total.chunks // total.members
        if chunk < total.chunks and chunk % per == 0:
            weight_grad(total.order[chunk // per])

    aside = [(1, join_rims), (1, functools.partial(row_grad, 0))]
    aside += [(2, functools.partial(row_grad, m)) for m in range(1, count)]
    aside += [(3, lambda: each(n, gx.forward, down.start)), (4, beta_grad)]
    aside += [(n + 2 + 2 * k, functools.partial(gx_end, k)) for k in range(n)]
    first = 3 * n + 2
    for k in range(max(len(rounds) + 1, n)):
        if k <= len(rounds):
            aside.append((first + 2 * k, functools.partial(small_turn, k)))
        if k < n:
            aside.append((first + 2 * k + 1, functools.partial(down_end, k)))
    weight_ready(0)
    for t in range(total.ticks()):
        for chunk in total.tick(t):
            whole = total.view(full_ref, chunk, 0, total.rows)
            total.view(total_ref, chunk, 0, total.rows)[...] = whole[...].astype(F32)
        while aside and aside[0][0] <= t:
            aside.pop(0)[1]()
        weight_ready(t + 1)
    for _, act in aside:
        act()
    k = len(total.bits)
    rows_ref[0] = row_now[k]
    rows_ref[1] = row_now[len(rounds)]
    for member in range(members):
        filter_ref[member] = tap_now[k, 8 * member : 8 * member + CONV, :]
    for group in small.values():
        for c in group:
            c.wait_send()
    each(pieces.total, gx.sent, down.sent)
    total.finish()
    rim.wait_send()


def finish(
    g3, tail, rim, grate, all_x, mixer_weights, beta_rows, grad_attn, head_out,
    down_part, taps_part, dense_part, out_part, inputs, mid, resid, gain, shards,
):
    count, local, width = inputs.shape
    members, _, head_width = mixer_weights.shape
    rows = g3[0].shape[1]
    bits = (shards - 1).bit_length()
    rounds = bits + 2
    chunks = 2 * members * head_width // 128
    whole = pltpu.VMEM(mixer_weights.shape, BF16)
    return pl.pallas_call(
        functools.partial(finish_body, shards),
        in_specs=vmem_specs(19),
        out_specs=vmem_specs(5),
        out_shape=[
            jax.ShapeDtypeStruct(inputs.shape, F32),
            jax.ShapeDtypeStruct(inputs.shape, BF16),
            jax.ShapeDtypeStruct(mixer_weights.shape, F32),
            jax.ShapeDtypeStruct((2, 8, width), F32),
            jax.ShapeDtypeStruct(taps_part.shape, F32),
        ],
        scratch_shapes=[
            pltpu.VMEM((count, rows, width), BF16),
            whole,
            pltpu.VMEM((3, count, rows, head_width), BF16),
            pltpu.VMEM(rim.shape, F32),
            pltpu.SemaphoreType.DMA,
            pltpu.SemaphoreType.DMA,
        ]
        + scatter_scratch(count, local, width) * 2
        + [
            whole, whole, whole,
            pltpu.SemaphoreType.DMA((2 * bits, chunks)),
            pltpu.SemaphoreType.DMA((2 * bits, chunks)),
            pltpu.VMEM((rounds, 8, width), F32),
            pltpu.VMEM((rounds + 1, 8, width), F32),
            pltpu.VMEM((rounds, 24, head_width), F32),
            pltpu.VMEM((rounds + 1, 24, head_width), F32),
            pltpu.SemaphoreType.DMA((2, rounds)),
            pltpu.SemaphoreType.DMA((2, rounds)),
            pltpu.VMEM((1, width), F32),
        ],
        compiler_params=comm_params(3),
        cost_estimate=cost(75),
        name="finish",
    )(
        *g3, tail, rim, grate, all_x, mixer_weights, beta_rows, grad_attn, head_out,
        down_part, taps_part, dense_part, out_part, inputs, mid, resid, gain,
    )


def regroup(blocks, count):
    if blocks.shape[0] == count:
        return blocks
    _, members, hidden, _ = blocks.shape
    whole = blocks.transpose(1, 2, 0, 3).reshape(members, hidden, count, -1)
    return whole.transpose(2, 0, 1, 3)


def per_device(
    inputs, attn_gain, mixer_weights, beta_weight, filter_weights, out_gain, dense_gain, dense_weights,
    seq_offsets, seq_lengths, out_grad,
):
    count, local_rows, width = inputs.shape
    heads, shards = lax.axis_size("head"), lax.axis_size("seq")
    base = (lax.axis_index("seq") * local_rows * heads).astype(jnp.int32).reshape(1)
    taps = filter_weights
    beta_rows = beta_weight.T
    gain_row = out_gain.reshape(1, HEAD_DIM)
    attn_row = attn_gain.reshape(1, width)
    dense_row = dense_gain.reshape(1, width)
    weights_t = jnp.swapaxes(dense_weights, 1, 2)
    extra = width == 128 * shards
    pq, pk, pv, rates, ps, oloc, phi, psi, score, inv, wr, up, trans, enter, back_x, back_y, x_ext, grad_top, *full = mix_fwd(
        seq_offsets, seq_lengths, base, mixer_weights, beta_rows, taps, inputs, attn_row, out_grad, weights_t, shards, extra
    )
    dense_full = full[0] if extra else regroup(lax.all_gather(weights_t, "seq", axis=0), width // 128)
    state_in = enter.reshape((count, -1) + enter.shape[1:])
    start, mixed, head_out, attn_part = mix_out(state_in, ps, oloc, phi, psi, gain_row, mixer_weights)
    resid_mid, down_part, dense_part, grad_mid, grad_attn, dense_gain_part = dense_block(
        attn_part, inputs, out_grad, grad_top, dense_row, dense_full, weights_t, shards, extra
    )
    dense_mine = lax.psum_scatter(regroup(dense_part, shards), "seq", scatter_dimension=0, tiled=True)
    dense_total = jnp.swapaxes(dense_mine[0], 1, 2).astype(F32)
    gq, gk, gv, tail, rim, grate, filter_part, out_gain_part = mix_grad(
        seq_offsets, seq_lengths, base, (pq, pk, pv), rates, taps, start, score, inv, wr, up,
        grad_attn, mixer_weights, mixed, gain_row, ps, phi, trans, back_x, back_y, shards,
    )
    input_grad, output, mixer_total, rows_total, filter_total = finish(
        (gq, gk, gv), tail, rim, grate, x_ext, mixer_weights, beta_rows, grad_attn, head_out,
        down_part, filter_part, dense_gain_part, out_gain_part, inputs, grad_mid, resid_mid, attn_row, shards,
    )
    local_heads = beta_rows.shape[0]
    beta_total = rows_total[0, :local_heads].T
    dense_gain_total = rows_total[1, local_heads]
    out_gain_total = rows_total[1, local_heads + 1, :HEAD_DIM]
    attn_gain_total = rows_total[1, local_heads + 2]
    return (
        output, input_grad, attn_gain_total, mixer_total, beta_total, filter_total, out_gain_total,
        dense_gain_total, dense_total,
    )


def solution(mesh):
    rows = P(None, ("seq", "head"), None)
    return jax.shard_map(
        per_device,
        mesh=mesh,
        in_specs=(
            rows, P(), P(None, None, "head"), P(None, "head"), P(None, None, "head"), P(), P(),
            P(None, "seq", "head"), P(), P(), rows,
        ),
        out_specs=(
            rows, rows, P(), P(None, None, "head"), P(None, "head"), P(None, None, "head"), P(), P(),
            P(None, "seq", "head"),
        ),
        check_vma=False,
    )
```

time: 768 us -> 323 us (0.42)
  waiting for transfers between devices: 401 us -> 0.02 us
  blocking collectives: 228 us -> 0 us
  Pallas kernels: 85.3 us -> 295 us
  other arithmetic: 17.6 us -> 2.25 us
  matrix products: 8.04 us -> 0 us
    all_gather x7 -> x0, waiting for transfers between devices: 269 us -> none  [the longest x2 95.5 us: compose(): gathered = lax.all_gather(pair, axis)]
    psum x2 -> x0, blocking collectives: 228 us -> none  [the longest x1 190 us: per_device(): mixer_total = lax.psum(mixer_part.astype(F32), 'seq')]
    pallas_call x5 -> x4, Pallas kernels: 80.2 us -> 290 us  [the longest x1 90.4 us: finish(): pl.pallas_call(functools.partial(finish_body, shards), in_specs=vmem_spec...]
    reduce_scatter x5 -> x1, waiting for transfers between devices: 121 us -> 0.01 us  [per_device(): lax.psum_scatter(regroup(dense_part, shards), 'seq', scatter_dimension=0,...]
    ppermute x2 -> x0, waiting for transfers between devices: 9.16 us -> none  [shifted(): lax.ppermute(block, axis, [(i, (i + distance) % count) for i in range(cou...]
    dot_general x7 -> x0, matrix products: 8.04 us -> none  [one(): jnp.einsum('mhij,mhjk->mhik', block[0], state.astype(BF16), preferred_ele...]
  transfers between devices with their start and end apart: 14 -> 1, of which waited for: 12 -> 0; matrix products, arithmetic and copies ran while one was open for 3% -> 1% of each run, Pallas kernels for 4% -> 44%
where the time goes in v4:
time: 323 us; the launch traced here: 322 us
  Pallas kernels  295 us (91%)
  between operations  14.1 us (4%)
  local copies, waits for them, and re-layouts  10.8 us (3%)
    pallas_call x1, Pallas kernels, finish(): pl.pallas_call(functools.partial(finish_body, shards), in_specs=vmem_spec...  90.4 us
    pallas_call x1, Pallas kernels, dense_block(): pl.pallas_call(functools.partial(dense_block_body, shards, extra), in_spe...  76.6 us
    pallas_call x1, Pallas kernels, mix_fwd(): pl.pallas_call(functools.partial(mix_fwd_body, shards, count, heads, toke...  72.4 us
    pallas_call x1, Pallas kernels, mix_grad(): pl.pallas_call(functools.partial(mix_grad_body, shards, count, heads), gr...  50.5 us
    unnamed x8, local copies, waits for them, and re-layouts  6.79 us
  transfers between devices with their start and end apart: 1, of which 0 were waited for; matrix products, arithmetic and copies ran while one was open for 1% of the time, Pallas kernels for 44%

profile of v4, /device:TPU:0, one launch (start us, length us, event | category | flops | bytes accessed | tf_op | source)
XLA Modules:
  0.0 322.4 jit_solution(13819581454025588014)
XLA Ops:
  7.2 0.0 reduce-scatter.2.cloned.1.call-start
  7.2 72.4 %mix_fwd.1 = (bf16[2,528,256]{2,1,0:T(8,128)(2,1)}, bf16[2,528,256]{2,1,0:T(8,128)(2,1)}, bf16[2,528,256]{2,1,0:T(8,128)(2,1)}, f32[2,2,512,1]{3,2,1,0:T(8,128)}...) custom-call(s32[2,3]{1,0:T(2,128)} %off_ref.3, ...), custom_call_target="tpu_custom_call" | custom-call | bytes 135000000 | tf_op jit(solution)/shard_map/mix_fwd/pallas_call | solution.py:691
  79.7 5.3 %mix_out.1 = (bf16[2,2,512,128]{3,2,1,0:T(8,128)(2,1)}, f32[2,2,512,128]{3,2,1,0:T(8,128)}, bf16[2,512,256]{2,1,0:T(8,128)(2,1)}, bf16[2,512,1024]{2,1,0:T(8,128)(2,1)}) custom-call(f32[2,2,128,128]{3,2,1,0:T(8,128)} %bitcast.22, bf16[2,2,512,128]{3,2,1,0:T(8,128)(2,1)} %get-tuple-element.56.ps_ref.all_ps_ref, ...), custom_call_target="tpu_custom_call" | custom-call | bytes 15000000 | tf_op jit(solution)/shard_map/mix_out/pallas_call | solution.py:747
  84.9 76.6 %dense_block.1 = (f32[2,128,1024]{2,1,0:T(8,128)}, bf16[4,256,1024]{2,1,0:T(8,128)(2,1)}, bf16[8,3,704,128]{3,2,1,0:T(8,128)(2,1)}, f32[2,128,1024]{2,1,0:T(8,12...) custom-call(bf16[2,512,1024]{2,1,0:T(8,128)(2,1)} %get-tuple-element.65.part_ref, bf16[2,128,1024]{2,1,0:T(8,128)(2,1)} %x_ref.3, ...), custom_call_target="tpu_custom_call" | custom-call | bytes 165000000 | tf_op jit(solution)/shard_map/dense_block/pallas_call | solution.py:1114
  161.5 0.0 reduce-scatter.2.cloned.1.call-update
  161.5 50.5 %mix_grad.1 = (bf16[2,512,256]{2,1,0:T(8,128)(2,1)}, bf16[2,512,256]{2,1,0:T(8,128)(2,1)}, bf16[2,512,256]{2,1,0:T(8,128)(2,1)}, f32[2,3,8,256]{3,2,1,0:T(8,128)...) custom-call(s32[2,3]{1,0:T(2,128)} %off_ref.3, ...), custom_call_target="tpu_custom_call" | custom-call | bytes 135000000 | tf_op jit(solution)/shard_map/mix_grad/pallas_call | solution.py:931
  212.1 90.4 %finish.1 = (f32[2,128,1024]{2,1,0:T(8,128)}, bf16[2,128,1024]{2,1,0:T(8,128)(2,1)}, f32[4,1024,256]{2,1,0:T(8,128)}, f32[2,8,1024]{2,1,0:T(8,128)}, f32[3,4,256]{2,1,0:T(4,128)}) custom-call(bf16[2,512,256]{2,1,0:T(8,128)(2,1)} %get-tuple-element.73.gq_ref, bf16[2,512,256]{2,1,0:T(8,128)(2,1)} %get-tuple-element.74.gk_ref, ...), custom_call_target="tpu_custom_call" | custom-call | bytes 225000000 | tf_op jit(solution)/shard_map/finish/pallas_call | solution.py:1379
  302.5 1.2 slice_bitcast_fusion.1
  303.7 1.4 slice_bitcast_fusion
  305.0 1.4 fusion
  306.5 0.0 reduce-scatter.2.cloned.1.call-done
  306.5 0.0 copy-start
  306.5 2.2 convert_bitcast_fusion
  308.7 1.9 copy.24
  310.6 2.3 copy.25
  312.9 0.0 copy-done
  312.9 0.0 copy-start.1
  312.9 2.0 copy.26
  314.9 0.0 copy-done.1
  314.9 0.6 copy.27
Async XLA Ops:
  7.2 299.3 %reduce-scatter.2.cloned.1.call-start = ((), (), s32[]{:S(2)}) async-start(), calls=%async_computation.1 | async-start | bytes 4866048 | tf_op jit(solution)/shard_map/reduce_scatter | solution.py:1451
  306.5 6.4 %copy-start = (f32[4,1024,256]{2,1,0:T(8,128)S(1)}, f32[4,1024,256]{2,1,0:T(8,128)}, u32[]{:S(2)}) copy-start(f32[4,1024,256]{2,1,0:T(8,128)} %get-tuple-element.107) | copy-start | bytes 12582916
  312.9 2.0 copy-start.1
Sparse Core Ops, SparseCore 0:
  161.6 118.8 reduce-scatter.1

commit v5 on v4

--- a/solution.py
+++ b/solution.py
@@ -1439,10 +1439,11 @@
     dense_row = dense_gain.reshape(1, width)
     weights_t = jnp.swapaxes(dense_weights, 1, 2)
     extra = width == 128 * shards
-    pq, pk, pv, rates, ps, oloc, phi, psi, score, inv, wr, up, trans, enter, back_x, back_y, x_ext, grad_top, *full = mix_fwd(
-        seq_offsets, seq_lengths, base, mixer_weights, beta_rows, taps, inputs, attn_row, out_grad, weights_t, shards, extra
+    pq, pk, pv, rates, ps, oloc, phi, psi, score, inv, wr, up, trans, enter, back_x, back_y, x_ext, grad_top = mix_fwd(
+        seq_offsets, seq_lengths, base, mixer_weights, beta_rows, taps, inputs, attn_row, out_grad, weights_t, shards, False
     )
-    dense_full = full[0] if extra else regroup(lax.all_gather(weights_t, "seq", axis=0), width // 128)
+    ready = 2 if extra else 3
+    dense_full = regroup(lax.all_gather(weights_t[:ready], "seq", axis=0), width // 128)
     state_in = enter.reshape((count, -1) + enter.shape[1:])
     start, mixed, head_out, attn_part = mix_out(state_in, ps, oloc, phi, psi, gain_row, mixer_weights)
     resid_mid, down_part, dense_part, grad_mid, grad_attn, dense_gain_part = dense_block(

time: 323 us -> 327 us (1.012)
    pallas_call x1, Pallas kernels: 72.4 us -> 77.7 us  [mix_fwd(): pl.pallas_call(functools.partial(mix_fwd_body, shards, count, heads, toke...]
  transfers between devices with their start and end apart: 1 -> 2, of which waited for: 0 -> 0; matrix products, arithmetic and copies ran while one was open for 1% -> 1% of each run, Pallas kernels for 44% -> 68%
where the time goes in v5:
time: 327 us
  Pallas kernels  298 us (91%)
  between operations  14.1 us (4%)
  local copies, waits for them, and re-layouts  12.5 us (4%)
    pallas_call x1, Pallas kernels, finish(): pl.pallas_call(functools.partial(finish_body, shards), in_specs=vmem_spec...  89.5 us
    pallas_call x1, Pallas kernels, mix_fwd(): pl.pallas_call(functools.partial(mix_fwd_body, shards, count, heads, toke...  77.7 us
    pallas_call x1, Pallas kernels, dense_block(): pl.pallas_call(functools.partial(dense_block_body, shards, extra), in_spe...  74.4 us
    pallas_call x1, Pallas kernels, mix_grad(): pl.pallas_call(functools.partial(mix_grad_body, shards, count, heads), gr...  51.1 us
    unnamed x8, local copies, waits for them, and re-layouts  6.79 us
  transfers between devices with their start and end apart: 2, of which 0 were waited for; matrix products, arithmetic and copies ran while one was open for 1% of the time, Pallas kernels for 68%

profile of v5, /device:TPU:0, one launch (start us, length us, event | category | flops | bytes accessed | tf_op | source)
XLA Modules:
  0.0 327.0 jit_solution(15049199980926523815)
XLA Ops:
  7.2 0.0 all-gather.3.cloned.1.call-start
  7.2 1.7 slice.20
  9.0 0.0 all-gather.3.cloned.1.call-update
  9.0 0.0 reduce-scatter.2.cloned.1.call-start
  9.0 77.7 %mix_fwd.1 = (bf16[2,528,256]{2,1,0:T(8,128)(2,1)}, bf16[2,528,256]{2,1,0:T(8,128)(2,1)}, bf16[2,528,256]{2,1,0:T(8,128)(2,1)}, f32[2,2,512,1]{3,2,1,0:T(8,128)}...) custom-call(s32[2,3]{1,0:T(2,128)} %off_ref.3, ...), custom_call_target="tpu_custom_call" | custom-call | bytes 135000000 | tf_op jit(solution)/shard_map/mix_fwd/pallas_call | solution.py:691
  86.8 5.3 %mix_out.1 = (bf16[2,2,512,128]{3,2,1,0:T(8,128)(2,1)}, f32[2,2,512,128]{3,2,1,0:T(8,128)}, bf16[2,512,256]{2,1,0:T(8,128)(2,1)}, bf16[2,512,1024]{2,1,0:T(8,128)(2,1)}) custom-call(f32[2,2,128,128]{3,2,1,0:T(8,128)} %bitcast.25, bf16[2,2,512,128]{3,2,1,0:T(8,128)(2,1)} %get-tuple-element.55.ps_ref.all_ps_ref, ...), custom_call_target="tpu_custom_call" | custom-call | bytes 15000000 | tf_op jit(solution)/shard_map/mix_out/pallas_call | solution.py:747
  92.1 0.0 all-gather.3.cloned.1.call-done
  92.1 74.4 %dense_block.1 = (f32[2,128,1024]{2,1,0:T(8,128)}, bf16[4,256,1024]{2,1,0:T(8,128)(2,1)}, bf16[8,3,704,128]{3,2,1,0:T(8,128)(2,1)}, f32[2,128,1024]{2,1,0:T(8,12...) custom-call(bf16[2,512,1024]{2,1,0:T(8,128)(2,1)} %get-tuple-element.64.part_ref, bf16[2,128,1024]{2,1,0:T(8,128)(2,1)} %x_ref.3, ...), custom_call_target="tpu_custom_call" | custom-call | bytes 165000000 | tf_op jit(solution)/shard_map/dense_block/pallas_call | solution.py:1114
  166.5 0.0 reduce-scatter.2.cloned.1.call-update
  166.5 51.1 %mix_grad.1 = (bf16[2,512,256]{2,1,0:T(8,128)(2,1)}, bf16[2,512,256]{2,1,0:T(8,128)(2,1)}, bf16[2,512,256]{2,1,0:T(8,128)(2,1)}, f32[2,3,8,256]{3,2,1,0:T(8,128)...) custom-call(s32[2,3]{1,0:T(2,128)} %off_ref.3, ...), custom_call_target="tpu_custom_call" | custom-call | bytes 135000000 | tf_op jit(solution)/shard_map/mix_grad/pallas_call | solution.py:931
  217.6 89.5 %finish.1 = (f32[2,128,1024]{2,1,0:T(8,128)}, bf16[2,128,1024]{2,1,0:T(8,128)(2,1)}, f32[4,1024,256]{2,1,0:T(8,128)}, f32[2,8,1024]{2,1,0:T(8,128)}, f32[3,4,256]{2,1,0:T(4,128)}) custom-call(bf16[2,512,256]{2,1,0:T(8,128)(2,1)} %get-tuple-element.71.gq_ref, bf16[2,512,256]{2,1,0:T(8,128)(2,1)} %get-tuple-element.72.gk_ref, ...), custom_call_target="tpu_custom_call" | custom-call | bytes 225000000 | tf_op jit(solution)/shard_map/finish/pallas_call | solution.py:1379
  307.1 1.2 slice_bitcast_fusion.1
  308.3 1.4 slice_bitcast_fusion
  309.7 1.4 fusion
  311.1 0.0 reduce-scatter.2.cloned.1.call-done
  311.1 0.0 copy-start
  311.1 2.2 convert_bitcast_fusion
  313.3 1.9 copy.24
  315.2 2.3 copy.25
  317.5 0.0 copy-done
  317.5 0.0 copy-start.1
  317.5 2.0 copy.26
  319.5 0.0 copy-done.1
  319.5 0.6 copy.27
Async XLA Ops:
  7.2 84.9 %all-gather.3.cloned.1.call-start = ((), (), s32[]{:S(2)}) async-start(), calls=%async_computation.2 | async-start | bytes 3244032 | tf_op jit(solution)/shard_map/all_gather | solution.py:1446
  9.0 302.1 %reduce-scatter.2.cloned.1.call-start = ((), (), s32[]{:S(2)}) async-start(), calls=%async_computation.1 | async-start | bytes 4866048 | tf_op jit(solution)/shard_map/reduce_scatter | solution.py:1452
  311.1 6.4 %copy-start = (f32[4,1024,256]{2,1,0:T(8,128)S(1)}, f32[4,1024,256]{2,1,0:T(8,128)}, u32[]{:S(2)}) copy-start(f32[4,1024,256]{2,1,0:T(8,128)} %get-tuple-element.105) | copy-start | bytes 12582916
  317.5 2.0 copy-start.1
Sparse Core Ops, SparseCore 0:
  10.2 70.6 all-gather.2
  166.6 118.7 reduce-scatter.1

commit v6 on v4

--- a/solution.py
+++ b/solution.py
@@ -986,7 +986,7 @@
 def dense_block_body(
     shards, extra, part_ref, x_ref, top_ref, all_top_ref, gain_ref, w_ref, own_ref,
     resid_ref, down_ref, grad_ref, mid_ref, out_ref, gain_grad_ref,
-    wt_ref, wsem, acc_ref, in_ref, gin_ref, gate_ref, up_ref, *scratch,
+    wt_ref, wsem, acc_ref, in_ref, gin_ref, *scratch,
 ):
     count, local, width = x_ref.shape
     groups = w_ref.shape[0]
@@ -1043,24 +1043,20 @@
 
     @pl.loop(0, n)
     def _(k):
+        if not extra:
+            grad_hidden = mm(all_top_ref[k], wt_ref[2], 1, 1)
         spread.arrived(k)
         x = in_ref[k]
-        gate_ref[k] = mm(x, wt_ref[0], 1, 1)
-        up_ref[k] = mm(x, wt_ref[1], 1, 1)
-
-        @pl.when(k + 1 < n)
-        def _():
-            spread.forward(k + 1)
-
-    if extra:
-        line.arrived(2)
-
-    @pl.loop(0, n)
-    def _(k):
-        x = in_ref[k]
-        gate = gate_ref[k]
-        up = up_ref[k]
-        grad_hidden = mm(all_top_ref[k], wt_ref[2], 1, 1)
+        gate = mm(x, wt_ref[0], 1, 1)
+        up = mm(x, wt_ref[1], 1, 1)
+        if extra:
+
+            @pl.when(k == 0)
+            def _():
+                line.arrived(2)
+
+        if extra:
+            grad_hidden = mm(all_top_ref[k], wt_ref[2], 1, 1)
         sg = sigmoid(gate)
         silu = gate * sg
         hidden = (silu * up).astype(BF16)
@@ -1068,6 +1064,11 @@
         grad_up = (grad_hidden * silu).astype(BF16)
         gin_ref[k] = (mm(grad_gate, wt_ref[0]) + mm(grad_up, wt_ref[1])).astype(BF16)
         second.start(k)
+
+        @pl.when(k + 1 < n)
+        def _():
+            spread.forward(k + 1)
+
         down_ref[k] = mm(hidden, wt_ref[2]).astype(BF16)
         second.forward(k)
         adds = (mm(grad_gate, x, 0, 0), mm(grad_up, x, 0, 0), mm(hidden, all_top_ref[k], 0, 0))
@@ -1129,8 +1130,6 @@
             pltpu.VMEM((3, hidden, width), F32),
             pltpu.VMEM((n, tile, width), BF16),
             pltpu.VMEM((n, tile, width), BF16),
-            pltpu.VMEM((n, tile, hidden), F32),
-            pltpu.VMEM((n, tile, hidden), F32),
         ]
         + (scatter_scratch(count, local, width) + gather_scratch(count, local)) * 2
         + (line_scratch(shards) if extra else []),
@@ -1438,7 +1437,7 @@
     attn_row = attn_gain.reshape(1, width)
     dense_row = dense_gain.reshape(1, width)
     weights_t = jnp.swapaxes(dense_weights, 1, 2)
-    extra = width == 128 * shards
+    extra = False
     pq, pk, pv, rates, ps, oloc, phi, psi, score, inv, wr, up, trans, enter, back_x, back_y, x_ext, grad_top, *full = mix_fwd(
         seq_offsets, seq_lengths, base, mixer_weights, beta_rows, taps, inputs, attn_row, out_grad, weights_t, shards, extra
     )

time: 323 us -> 323 us (level)
  waiting for transfers between devices: 0.02 us -> 12.5 us
  Pallas kernels: 295 us -> 283 us
    pallas_call x1, Pallas kernels: 76.6 us -> 61.9 us  [dense_block(): pl.pallas_call(functools.partial(dense_block_body, shards, extra), in_spe...]
    all_gather x0 -> x1, waiting for transfers between devices: none -> 11.8 us  [per_device(): lax.all_gather(weights_t, 'seq', axis=0)]
    pallas_call x1, Pallas kernels: 72.4 us -> 75.8 us  [mix_fwd(): pl.pallas_call(functools.partial(mix_fwd_body, shards, count, heads, toke...]
  transfers between devices with their start and end apart: 1 -> 2, of which waited for: 0 -> 1; matrix products, arithmetic and copies ran while one was open for 1% -> 1% of each run, Pallas kernels for 44% -> 69%
where the time goes in v6:
time: 323 us
  Pallas kernels  283 us (88%)
  between operations  14.1 us (4%)
  waiting for transfers between devices  12.5 us (4%)
  local copies, waits for them, and re-layouts  10.8 us (3%)
    pallas_call x1, Pallas kernels, finish(): pl.pallas_call(functools.partial(finish_body, shards), in_specs=vmem_spec...  87.9 us
    pallas_call x1, Pallas kernels, mix_fwd(): pl.pallas_call(functools.partial(mix_fwd_body, shards, count, heads, toke...  75.8 us
    pallas_call x1, Pallas kernels, dense_block(): pl.pallas_call(functools.partial(dense_block_body, shards, extra), in_spe...  61.9 us
    pallas_call x1, Pallas kernels, mix_grad(): pl.pallas_call(functools.partial(mix_grad_body, shards, count, heads), gr...  52.4 us
    all_gather x1, waiting for transfers between devices, per_device(): lax.all_gather(weights_t, 'seq', axis=0)  11.8 us
    unnamed x8, local copies, waits for them, and re-layouts  6.79 us
  transfers between devices with their start and end apart: 2, of which 1 were waited for; matrix products, arithmetic and copies ran while one was open for 1% of the time, Pallas kernels for 69%

profile of v6, /device:TPU:0, one launch (start us, length us, event | category | flops | bytes accessed | tf_op | source)
XLA Modules:
  0.0 323.0 jit_solution(9902144399873228632)
XLA Ops:
  7.2 0.0 all-gather.3.cloned.1.call-start
  7.2 0.7 all-gather.3.cloned.1.call-update
  7.9 0.0 reduce-scatter.2.cloned.1.call-start
  8.0 75.8 %mix_fwd.1 = (bf16[2,528,256]{2,1,0:T(8,128)(2,1)}, bf16[2,528,256]{2,1,0:T(8,128)(2,1)}, bf16[2,528,256]{2,1,0:T(8,128)(2,1)}, f32[2,2,512,1]{3,2,1,0:T(8,128)}...) custom-call(s32[2,3]{1,0:T(2,128)} %off_ref.3, ...), custom_call_target="tpu_custom_call" | custom-call | bytes 135000000 | tf_op jit(solution)/shard_map/mix_fwd/pallas_call | solution.py:691
  83.7 5.3 %mix_out.1 = (bf16[2,2,512,128]{3,2,1,0:T(8,128)(2,1)}, f32[2,2,512,128]{3,2,1,0:T(8,128)}, bf16[2,512,256]{2,1,0:T(8,128)(2,1)}, bf16[2,512,1024]{2,1,0:T(8,128)(2,1)}) custom-call(f32[2,2,128,128]{3,2,1,0:T(8,128)} %bitcast.25, bf16[2,2,512,128]{3,2,1,0:T(8,128)(2,1)} %get-tuple-element.55.ps_ref.all_ps_ref, ...), custom_call_target="tpu_custom_call" | custom-call | bytes 15000000 | tf_op jit(solution)/shard_map/mix_out/pallas_call | solution.py:747
  89.0 11.8 %all-gather.3.cloned.1.call-done = bf16[24,704,128]{2,1,0:T(8,128)(2,1)} async-done(((bf16[3,704,128]{2,1,0:T(8,128)(2,1)}), bf16[24,704,128]{2,1,0:T(8,128)(2,1)}) %all-gather.3.cloned.1.call-update) | async-done | bytes 4325392 | tf_op jit(solution)/shard_map/all_gather | solution.py:1444
  100.8 61.9 %dense_block.1 = (f32[2,128,1024]{2,1,0:T(8,128)}, bf16[4,256,1024]{2,1,0:T(8,128)(2,1)}, bf16[8,3,704,128]{3,2,1,0:T(8,128)(2,1)}, f32[2,128,1024]{2,1,0:T(8,12...) custom-call(bf16[2,512,1024]{2,1,0:T(8,128)(2,1)} %get-tuple-element.64.part_ref, bf16[2,128,1024]{2,1,0:T(8,128)(2,1)} %x_ref.3, ...), custom_call_target="tpu_custom_call" | custom-call | bytes 165000000 | tf_op jit(solution)/shard_map/dense_block/pallas_call | solution.py:1115
  162.7 0.0 reduce-scatter.2.cloned.1.call-update
  162.7 52.4 %mix_grad.1 = (bf16[2,512,256]{2,1,0:T(8,128)(2,1)}, bf16[2,512,256]{2,1,0:T(8,128)(2,1)}, bf16[2,512,256]{2,1,0:T(8,128)(2,1)}, f32[2,3,8,256]{3,2,1,0:T(8,128)...) custom-call(s32[2,3]{1,0:T(2,128)} %off_ref.3, ...), custom_call_target="tpu_custom_call" | custom-call | bytes 135000000 | tf_op jit(solution)/shard_map/mix_grad/pallas_call | solution.py:931
  215.2 87.9 %finish.1 = (f32[2,128,1024]{2,1,0:T(8,128)}, bf16[2,128,1024]{2,1,0:T(8,128)(2,1)}, f32[4,1024,256]{2,1,0:T(8,128)}, f32[2,8,1024]{2,1,0:T(8,128)}, f32[3,4,256]{2,1,0:T(4,128)}) custom-call(bf16[2,512,256]{2,1,0:T(8,128)(2,1)} %get-tuple-element.71.gq_ref, bf16[2,512,256]{2,1,0:T(8,128)(2,1)} %get-tuple-element.72.gk_ref, ...), custom_call_target="tpu_custom_call" | custom-call | bytes 225000000 | tf_op jit(solution)/shard_map/finish/pallas_call | solution.py:1378
  303.1 1.2 slice_bitcast_fusion.1
  304.3 1.4 slice_bitcast_fusion
  305.7 1.4 fusion
  307.1 0.0 reduce-scatter.2.cloned.1.call-done
  307.1 0.0 copy-start
  307.1 2.2 convert_bitcast_fusion
  309.3 1.9 copy.24
  311.2 2.3 copy.25
  313.5 0.0 copy-done
  313.5 0.0 copy-start.1
  313.5 2.0 copy.26
  315.5 0.0 copy-done.1
  315.5 0.6 copy.27
Async XLA Ops:
  7.2 93.7 %all-gather.3.cloned.1.call-start = ((), (), s32[]{:S(2)}) async-start(), calls=%async_computation.2 | async-start | bytes 4866048 | tf_op jit(solution)/shard_map/all_gather | solution.py:1444
  7.9 299.2 %reduce-scatter.2.cloned.1.call-start = ((), (), s32[]{:S(2)}) async-start(), calls=%async_computation.1 | async-start | bytes 4866048 | tf_op jit(solution)/shard_map/reduce_scatter | solution.py:1450
  307.1 6.4 %copy-start = (f32[4,1024,256]{2,1,0:T(8,128)S(1)}, f32[4,1024,256]{2,1,0:T(8,128)}, u32[]{:S(2)}) copy-start(f32[4,1024,256]{2,1,0:T(8,128)} %get-tuple-element.105) | copy-start | bytes 12582916
  313.5 2.0 copy-start.1
Sparse Core Ops, SparseCore 0:
  10.2 90.5 all-gather.2
  162.9 118.3 reduce-scatter.1
